TPU v7x, 32 devices: a whole 2x2x4 slice. The times are simulated.
32 devices in a mesh: dp: 16 (over z, y, core), tensor: 2 (over x).
Axes of the slice: x: 2, y: 2, z: 4, core: 2. Of those that a mesh axis runs over, the one named last changes fastest.
Arguments:
- tokens: bfloat16 [32768, 768], P(('dp', 'tensor')), may hold values from -6 to 6
- memory: bfloat16 [16, 1500, 768], P('dp'), may hold values from -6 to 6
- seg_ids: int32 [32768], P(('dp', 'tensor')), may hold values from 0 to 4, as said below
- positions: int32 [32768], P(('dp', 'tensor')), may hold values from 0 to 1535, as said below
- grad_output: bfloat16 [32768, 768], P(('dp', 'tensor')), may hold values from -6 to 6
- attn_in: bfloat16 [768, 3, 768], P('dp', None, 'tensor'), may hold values from -0.21875 to 0.21875
- attn_out: bfloat16 [768, 768], P('tensor', 'dp'), may hold values from -2.5 to 2.5
- cross_q: bfloat16 [768, 768], P('dp', 'tensor'), may hold values from -0.21875 to 0.21875
- cross_kv: bfloat16 [768, 2, 768], P('dp', None, 'tensor'), may hold values from -0.21875 to 0.21875
- cross_out: bfloat16 [768, 768], P('tensor', 'dp'), may hold values from -2.5 to 2.5
- mlp_in: bfloat16 [768, 3072], P('dp', 'tensor'), may hold values from -0.21875 to 0.21875
- mlp_out: bfloat16 [3072, 768], P('tensor', 'dp'), may hold values from -0.109375 to 0.109375
- norm_gain: float32 [3, 768], replicated, may hold values from 0.5 to 1.5
- norm_bias: float32 [3, 768], replicated, may hold values from -1 to 1
- proj_bias: float32 [6, 768], replicated, may hold values from -0.5 to 0.5
- mlp_bias: float32 [3072], replicated, may hold values from -1 to 1
- out_bias: float32 [768], replicated, may hold values from -2.5 to 2.5
Outputs:
- output: bfloat16 [32768, 768], P(('dp', 'tensor'))
- grad_tokens: float32 [32768, 768], P(('dp', 'tensor'))
- grad_attn_in: float32 [768, 3, 768], P('dp', None, 'tensor')
- grad_attn_out: float32 [768, 768], P('tensor', 'dp')
- grad_cross_q: float32 [768, 768], P('dp', 'tensor')
- grad_cross_kv: float32 [768, 2, 768], P('dp', None, 'tensor')
- grad_cross_out: float32 [768, 768], P('tensor', 'dp')
- grad_mlp_in: float32 [768, 3072], P('dp', 'tensor')
- grad_mlp_out: float32 [3072, 768], P('tensor', 'dp')
- grad_norm_gain: float32 [3, 768], replicated
- grad_norm_bias: float32 [3, 768], replicated
- grad_proj_bias: float32 [6, 768], replicated
- grad_mlp_bias: float32 [3072], replicated
- grad_out_bias: float32 [768], replicated
Inputs may be any that keep to these rules, and one draw needn't show every extreme that they name: `seg_ids`: within each group of 2048 consecutive tokens, the first 1024 are 0 (the prompt); the rest are 4 runs numbered 1 to 4 in order, each of 1 to 512 tokens, one of exactly 512 tokens. Prompt tokens have positions 0, 1, ... in order; each continuation's tokens have positions 1024, 1025, ... in order.
All inputs are finite; a program needn't handle non-finite values.
Results may differ from a plain program's by a relative error of at most 0.029.
Values may be sent and summed in bfloat16 or wider, within the bound.
A program may use at most 256 MiB of HBM per device.

v0:
```python
import math

import jax
import jax.numpy as jnp
from jax import lax
from jax.sharding import PartitionSpec as P

HEAD = 64


EPSILON = 1e-05
NEG_LARGE = -1e30


def layer_norm(values, gain_row, offset_row):
    centre = values - jnp.mean(values, -1, keepdims=True)
    spread = jnp.mean(centre * centre, -1, keepdims=True)
    return centre * lax.rsqrt(spread + EPSILON) * gain_row + offset_row


def exact_gelu(values):
    return jax.nn.gelu(values, approximate=False)


def contract_rows(left, right):
    return lax.dot_general(
        left, right, (((0,), (0,)), ((), ())), preferred_element_type=jnp.float32
    )


def score_block(q_rows, key_rows, q_seg, q_pos, k_seg, k_pos, masked):
    scores = jnp.einsum("qhd,khd->hqk", q_rows, key_rows, preferred_element_type=jnp.float32)
    if masked:
        allowed = (k_pos[None, :] <= q_pos[:, None]) & (
            (k_seg[None, :] == 0) | (k_seg[None, :] == q_seg[:, None])
        )
        scores = jnp.where(allowed[None], scores, NEG_LARGE)
    return scores


def attend_forward(queries, key_rows, values, q_seg, q_pos, k_seg, k_pos, masked):
    row_count, heads_here, head_dim = queries.shape
    blk_width = math.gcd(row_count, 512)
    blk_count = row_count // blk_width

    def one_block(pieces):
        q_rows, seg_rows, pos_rows = pieces
        scores = score_block(q_rows, key_rows, seg_rows, pos_rows, k_seg, k_pos, masked)
        row_peak = jnp.max(scores, -1, keepdims=True)
        exp_scores = jnp.exp(scores - row_peak)
        row_total = jnp.sum(exp_scores, -1, keepdims=True)
        attn_probs = (exp_scores / row_total).astype(jnp.bfloat16)
        mixed_out = jnp.einsum(
            "hqk,khd->qhd", attn_probs, values, preferred_element_type=jnp.float32
        )
        return (mixed_out, (row_peak + jnp.log(row_total))[..., 0])

    mixed_out, log_sum = lax.map(
        one_block,
        (
            queries.reshape(blk_count, blk_width, heads_here, head_dim),
            q_seg.reshape(blk_count, blk_width),
            q_pos.reshape(blk_count, blk_width),
        ),
    )
    return (mixed_out.reshape(row_count, heads_here * head_dim), log_sum)


def attend_backward(
    queries, key_rows, values, log_sum, grad_mixed, q_seg, q_pos, k_seg, k_pos, masked
):
    row_count, heads_here, head_dim = queries.shape
    blk_width = math.gcd(row_count, 512)
    blk_count = row_count // blk_width

    def one_block(carry, pieces):
        grad_keys, grad_values = carry
        q_rows, seg_rows, pos_rows, lse_rows, grad_rows = pieces
        scores = score_block(q_rows, key_rows, seg_rows, pos_rows, k_seg, k_pos, masked)
        probs_full = jnp.exp(scores - lse_rows[..., None])
        grad_values = grad_values + jnp.einsum(
            "hqk,qhd->khd",
            probs_full.astype(jnp.bfloat16),
            grad_rows,
            preferred_element_type=jnp.float32,
        )
        grad_probs = jnp.einsum(
            "qhd,khd->hqk", grad_rows, values, preferred_element_type=jnp.float32
        )
        inner = jnp.sum(probs_full * grad_probs, -1, keepdims=True)
        grad_scores = (probs_full * (grad_probs - inner)).astype(jnp.bfloat16)
        grad_query = jnp.einsum(
            "hqk,khd->qhd", grad_scores, key_rows, preferred_element_type=jnp.float32
        )
        grad_keys = grad_keys + jnp.einsum(
            "hqk,qhd->khd", grad_scores, q_rows, preferred_element_type=jnp.float32
        )
        return ((grad_keys, grad_values), grad_query)

    zero_rows = jnp.zeros(key_rows.shape, jnp.float32)
    (grad_keys, grad_values), grad_query = lax.scan(
        one_block,
        (zero_rows, zero_rows),
        (
            queries.reshape(blk_count, blk_width, heads_here, head_dim),
            q_seg.reshape(blk_count, blk_width),
            q_pos.reshape(blk_count, blk_width),
            log_sum,
            grad_mixed.reshape(blk_count, blk_width, heads_here, head_dim),
        ),
    )
    return (grad_query.reshape(row_count, heads_here, head_dim), grad_keys, grad_values)


def fetch_weights(attn_in, attn_out, cross_q, cross_kv, cross_out, mlp_in, mlp_out):
    return (
        lax.all_gather(attn_in, "dp", axis=0, tiled=True),
        lax.all_gather(attn_out, "dp", axis=1, tiled=True),
        lax.all_gather(cross_q, "dp", axis=0, tiled=True),
        lax.all_gather(cross_kv, "dp", axis=0, tiled=True),
        lax.all_gather(cross_out, "dp", axis=1, tiled=True),
        lax.all_gather(mlp_in, "dp", axis=0, tiled=True),
        lax.all_gather(mlp_out, "dp", axis=1, tiled=True),
    )


def gather_norm(normed):
    return lax.all_gather(normed, "tensor", axis=0, tiled=True)


def gather_grad(grad_low):
    return lax.all_gather(grad_low, "tensor", axis=0, tiled=True)


def branch_rows(left, right):
    return lax.psum_scatter(
        jnp.dot(left, right, preferred_element_type=jnp.float32).astype(jnp.bfloat16),
        "tensor",
        scatter_dimension=0,
        tiled=True,
    ).astype(jnp.float32)


def input_grad_rows(left, right):
    return lax.psum_scatter(
        lax.dot_general(
            left, right, (((1,), (1,)), ((), ())), preferred_element_type=jnp.float32
        ).astype(jnp.bfloat16),
        "tensor",
        scatter_dimension=0,
        tiled=True,
    ).astype(jnp.float32)


def on_device(
    tokens,
    memory,
    seg_ids,
    positions,
    grad_output,
    attn_in,
    attn_out,
    cross_q,
    cross_kv,
    cross_out,
    mlp_in,
    mlp_out,
    norm_gain,
    norm_bias,
    proj_bias,
    mlp_bias,
    out_bias,
):
    model_width = tokens.shape[1]
    local_width = attn_in.shape[2]
    local_units = mlp_in.shape[1]
    heads_here = local_width // HEAD
    q_scale = HEAD ** (-0.5)
    tensor_rank = lax.axis_index("tensor")
    tensor_count = lax.axis_size("tensor")

    def local_part(row_values, size_here):
        return lax.dynamic_slice_in_dim(row_values, tensor_rank * size_here, size_here)

    def widen(part_values, full_size):
        return lax.dynamic_update_slice_in_dim(
            jnp.zeros((full_size,), jnp.float32), part_values, tensor_rank * part_values.shape[0], 0
        )

    def norm_back(resid_in, index_row, grad_norm):
        _, pull = jax.vjp(layer_norm, resid_in, norm_gain[index_row], norm_bias[index_row])
        return pull(grad_norm)

    w_qkv, w_attn_out, w_cross_q, w_cross_kv, w_cross_out, w_mlp_in, w_mlp_out = fetch_weights(
        attn_in, attn_out, cross_q, cross_kv, cross_out, mlp_in, mlp_out
    )
    resid_zero = tokens.astype(jnp.float32)
    norm_one = layer_norm(resid_zero, norm_gain[0], norm_bias[0]).astype(jnp.bfloat16)
    full_one, seg_full, pos_full = (
        lax.all_gather(norm_one, "tensor", axis=0, tiled=True),
        lax.all_gather(seg_ids, "tensor", axis=0, tiled=True),
        lax.all_gather(positions, "tensor", axis=0, tiled=True),
    )
    group_rows = full_one.shape[0]
    qkv_cols = jnp.dot(
        full_one, w_qkv.reshape(model_width, 3 * local_width), preferred_element_type=jnp.float32
    )
    q_self = (
        ((qkv_cols[:, :local_width] + local_part(proj_bias[0], local_width)) * q_scale)
        .astype(jnp.bfloat16)
        .reshape(group_rows, heads_here, HEAD)
    )
    k_self = (
        qkv_cols[:, local_width : 2 * local_width]
        .astype(jnp.bfloat16)
        .reshape(group_rows, heads_here, HEAD)
    )
    v_self = (
        (qkv_cols[:, 2 * local_width :] + local_part(proj_bias[1], local_width))
        .astype(jnp.bfloat16)
        .reshape(group_rows, heads_here, HEAD)
    )
    attn_self, lse_self = attend_forward(
        q_self, k_self, v_self, seg_full, pos_full, seg_full, pos_full, True
    )
    attn_self = attn_self.astype(jnp.bfloat16)
    resid_one = resid_zero + branch_rows(attn_self, w_attn_out) + proj_bias[2]
    norm_two = layer_norm(resid_one, norm_gain[1], norm_bias[1]).astype(jnp.bfloat16)
    full_two = gather_norm(norm_two)
    q_cross = (
        (
            (
                jnp.dot(full_two, w_cross_q, preferred_element_type=jnp.float32)
                + local_part(proj_bias[3], local_width)
            )
            * q_scale
        )
        .astype(jnp.bfloat16)
        .reshape(group_rows, heads_here, HEAD)
    )
    mem_rows = memory[0]
    frame_rows = mem_rows.shape[0]
    kv_cols = jnp.dot(
        mem_rows,
        w_cross_kv.reshape(model_width, 2 * local_width),
        preferred_element_type=jnp.float32,
    )
    k_cross = kv_cols[:, :local_width].astype(jnp.bfloat16).reshape(frame_rows, heads_here, HEAD)
    v_cross = (
        (kv_cols[:, local_width:] + local_part(proj_bias[4], local_width))
        .astype(jnp.bfloat16)
        .reshape(frame_rows, heads_here, HEAD)
    )
    attn_cross, lse_cross = attend_forward(
        q_cross, k_cross, v_cross, seg_full, pos_full, seg_full, pos_full, False
    )
    attn_cross = attn_cross.astype(jnp.bfloat16)
    resid_two = resid_one + branch_rows(attn_cross, w_cross_out) + proj_bias[5]
    norm_three = layer_norm(resid_two, norm_gain[2], norm_bias[2]).astype(jnp.bfloat16)
    full_three = gather_norm(norm_three)
    pre_act = jnp.dot(full_three, w_mlp_in, preferred_element_type=jnp.float32) + local_part(
        mlp_bias, local_units
    )
    hidden = exact_gelu(pre_act).astype(jnp.bfloat16)
    resid_out = resid_two + branch_rows(hidden, w_mlp_out) + out_bias
    output = resid_out.astype(jnp.bfloat16)
    grad_resid = grad_output.astype(jnp.float32)
    grad_low = grad_resid.astype(jnp.bfloat16)
    grad_branch = gather_grad(grad_low)
    gb_mlp_out = jnp.sum(grad_low, 0, dtype=jnp.float32)
    gw_mlp_out = contract_rows(hidden, grad_branch)
    grad_hidden = lax.dot_general(
        grad_branch, w_mlp_out, (((1,), (1,)), ((), ())), preferred_element_type=jnp.float32
    )
    _, gelu_pull = jax.vjp(exact_gelu, pre_act)
    grad_pre = gelu_pull(grad_hidden)[0].astype(jnp.bfloat16)
    gw_mlp_in = contract_rows(full_three, grad_pre)
    gb_mlp_in = jnp.sum(grad_pre, 0, dtype=jnp.float32)
    grad_norm = input_grad_rows(grad_pre, w_mlp_in)
    grad_input, gain_three, shift_three = norm_back(resid_two, 2, grad_norm)
    grad_resid = grad_resid + grad_input
    grad_low = grad_resid.astype(jnp.bfloat16)
    grad_branch = gather_grad(grad_low)
    gb_cross_out = jnp.sum(grad_low, 0, dtype=jnp.float32)
    gw_cross_out = contract_rows(attn_cross, grad_branch)
    grad_attn = lax.dot_general(
        grad_branch, w_cross_out, (((1,), (1,)), ((), ())), preferred_element_type=jnp.float32
    )
    grad_attn = grad_attn.astype(jnp.bfloat16).reshape(group_rows, heads_here, HEAD)
    grad_q, grad_k, grad_v = attend_backward(
        q_cross,
        k_cross,
        v_cross,
        lse_cross,
        grad_attn,
        seg_full,
        pos_full,
        seg_full,
        pos_full,
        False,
    )
    grad_q_low = grad_q.astype(jnp.bfloat16).reshape(group_rows, local_width) * q_scale
    grad_v_low = grad_v.astype(jnp.bfloat16).reshape(frame_rows, local_width)
    grad_kv_low = jnp.concatenate(
        [grad_k.astype(jnp.bfloat16).reshape(frame_rows, local_width), grad_v_low], 1
    )
    gw_cross_q = contract_rows(full_two, grad_q_low)
    gb_cross_q = jnp.sum(grad_q_low, 0, dtype=jnp.float32)
    gw_cross_kv = contract_rows(mem_rows, grad_kv_low).reshape(model_width, 2, local_width)
    gb_cross_v = jnp.sum(grad_v_low, 0, dtype=jnp.float32)
    grad_norm = input_grad_rows(grad_q_low, w_cross_q)
    grad_input, gain_two, shift_two = norm_back(resid_one, 1, grad_norm)
    grad_resid = grad_resid + grad_input
    grad_low = grad_resid.astype(jnp.bfloat16)
    grad_branch = gather_grad(grad_low)
    gb_attn_out = jnp.sum(grad_low, 0, dtype=jnp.float32)
    gw_attn_out = contract_rows(attn_self, grad_branch)
    grad_attn = lax.dot_general(
        grad_branch, w_attn_out, (((1,), (1,)), ((), ())), preferred_element_type=jnp.float32
    )
    grad_attn = grad_attn.astype(jnp.bfloat16).reshape(group_rows, heads_here, HEAD)
    grad_q, grad_k, grad_v = attend_backward(
        q_self, k_self, v_self, lse_self, grad_attn, seg_full, pos_full, seg_full, pos_full, True
    )
    grad_q_low = grad_q.astype(jnp.bfloat16).reshape(group_rows, local_width) * q_scale
    grad_v_low = grad_v.astype(jnp.bfloat16).reshape(group_rows, local_width)
    grad_qkv_low = jnp.concatenate(
        [grad_q_low, grad_k.astype(jnp.bfloat16).reshape(group_rows, local_width), grad_v_low], 1
    )
    gw_qkv = contract_rows(full_one, grad_qkv_low).reshape(model_width, 3, local_width)
    gb_q_self = jnp.sum(grad_q_low, 0, dtype=jnp.float32)
    gb_v_self = jnp.sum(grad_v_low, 0, dtype=jnp.float32)
    grad_norm = input_grad_rows(grad_qkv_low, w_qkv.reshape(model_width, 3 * local_width))
    grad_input, gain_one, shift_one = norm_back(resid_zero, 0, grad_norm)
    grad_tokens = grad_resid + grad_input
    g_attn_in, g_attn_out, g_cross_q, g_cross_kv, g_cross_out, g_mlp_in, g_mlp_out = (
        lax.psum_scatter(gw_qkv, "dp", scatter_dimension=0, tiled=True),
        lax.psum_scatter(gw_attn_out, "dp", scatter_dimension=1, tiled=True),
        lax.psum_scatter(gw_cross_q, "dp", scatter_dimension=0, tiled=True),
        lax.psum_scatter(gw_cross_kv, "dp", scatter_dimension=0, tiled=True),
        lax.psum_scatter(gw_cross_out, "dp", scatter_dimension=1, tiled=True),
        lax.psum_scatter(gw_mlp_in, "dp", scatter_dimension=0, tiled=True),
        lax.psum_scatter(gw_mlp_out, "dp", scatter_dimension=1, tiled=True),
    )
    gain_grads = jnp.stack([gain_one, gain_two, gain_three])
    shift_grads = jnp.stack([shift_one, shift_two, shift_three])
    proj_grads = jnp.stack(
        [
            widen(gb_q_self, model_width),
            widen(gb_v_self, model_width),
            gb_attn_out,
            widen(gb_cross_q, model_width),
            widen(gb_cross_v, model_width),
            gb_cross_out,
        ]
    )
    unit_grads = widen(gb_mlp_in, local_units * tensor_count)
    g_gain, g_shift, g_proj, g_units, g_out_bias = lax.psum(
        (gain_grads, shift_grads, proj_grads, unit_grads, gb_mlp_out), ("dp", "tensor")
    )
    return (
        output,
        grad_tokens,
        g_attn_in,
        g_attn_out,
        g_cross_q,
        g_cross_kv,
        g_cross_out,
        g_mlp_in,
        g_mlp_out,
        g_gain,
        g_shift,
        g_proj,
        g_units,
        g_out_bias,
    )


def solution(mesh):
    in_specs = (
        P(("dp", "tensor"), None),
        P("dp", None, None),
        P(("dp", "tensor")),
        P(("dp", "tensor")),
        P(("dp", "tensor"), None),
        P("dp", None, "tensor"),
        P("tensor", "dp"),
        P("dp", "tensor"),
        P("dp", None, "tensor"),
        P("tensor", "dp"),
        P("dp", "tensor"),
        P("tensor", "dp"),
        P(),
        P(),
        P(),
        P(),
        P(),
    )
    out_specs = (
        P(("dp", "tensor"), None),
        P(("dp", "tensor"), None),
        P("dp", None, "tensor"),
        P("tensor", "dp"),
        P("dp", "tensor"),
        P("dp", None, "tensor"),
        P("tensor", "dp"),
        P("dp", "tensor"),
        P("tensor", "dp"),
        P(),
        P(),
        P(),
        P(),
        P(),
    )
    return jax.shard_map(
        on_device, mesh=mesh, in_specs=in_specs, out_specs=out_specs, check_vma=False
    )
```

profile of v0, /device:TPU:0, one launch (start us, length us, event | category | flops | bytes accessed | tf_op | source)
XLA Modules:
  0.0 2210.5 jit_solution(12112022454052298511)
XLA Ops:
  28.6 26.1 %all_gather.49 = bf16[384,768]{0,1:T(8,128)(2,1)} all-gather(bf16[384,48]{0,1:T(8,128)(2,1)S(1)} %copy-done.71), channel_id=1, replica_groups=mesh['dp'=16,'tensor'=2] {'dp'}, dimensions={1}, use_global_device_ids=true | all-gather | bytes 626688 | tf_op jit(solution)/shard_map/all_gather | solution.py:118
  59.3 41.9 %all-gather.11.cloned.1.call-done = bf16[2048,768]{1,0:T(8,128)(2,1)} async-done(((bf16[1024,768]{1,0:T(8,128)(2,1)}), bf16[2048,768]{1,0:T(8,128)(2,1)}) %all-gather.11.cloned.1.call-update) | async-done | bytes 3145744 | tf_op jit(solution)/shard_map/all_gather | solution.py:200
  119.1 157.1 %while.54 = (s32[]{:T(128)}, bf16[4,512,6,64]{1,3,2,0:T(8,128)(2,1)}, f32[4,6,512]{2,1,0:T(8,128)S(1)}, s32[2048]{0:T(1024)S(1)}, s32[4,512]{1,0:T(4,128)S(1)}, ...) while((s32[]{:T(128)}, ...), condition=%wide.region_5.6_spmd, body=%wide.region_2.5_spmd.sunk | while | flops 1671429120 | bytes 103051472 | solution.py:58
  284.8 42.9 %reduce-scatter.12.cloned.1.call-done = bf16[1024,768]{1,0:T(8,128)(2,1)} async-done(((bf16[2048,768]{1,0:T(8,128)(2,1)}), bf16[1024,768]{1,0:T(8,128)(2,1)}) %reduce-scatter.12.cloned.1.call-update) | async-done | bytes 1572880 | tf_op jit(solution)/shard_map/reduce_scatter | solution.py:136
  334.8 24.5 %all_gather.51 = bf16[768,384]{1,0:T(8,128)(2,1)} all-gather(bf16[48,384]{1,0:T(8,128)(2,1)S(1)} %copy-done.72), channel_id=1, replica_groups=mesh['dp'=16,'tensor'=2] {'dp'}, dimensions={0}, use_global_device_ids=true | all-gather | bytes 626688 | tf_op jit(solution)/shard_map/all_gather | solution.py:119
  359.3 20.9 all_gather.53
  394.2 21.8 all-gather.15.cloned.1.call-done
  429.2 113.2 %while.55 = (s32[]{:T(128)}, bf16[4,512,6,64]{1,3,2,0:T(8,128)(2,1)}, f32[4,6,512]{2,1,0:T(8,128)}, bf16[4,512,6,64]{1,3,2,0:T(8,128)(2,1)}, bf16[1500,6,64]{0,2...) while((s32[]{:T(128)}, bf16[4,512,6,64]{1,3,2,0:T(8,128)(2,1)}, f32[4,6,512]{2,1,0:T(8,128)}, ...), condition=%wide.region_12.13_spmd, body=%wide.region_9.12_spmd.sunk | while | flops 1207292928 | bytes 58958944 | solution.py:58
  551.5 42.7 %reduce-scatter.14.cloned.1.call-done = bf16[1024,768]{1,0:T(8,128)(2,1)} async-done(((bf16[2048,768]{1,0:T(8,128)(2,1)}), bf16[1024,768]{1,0:T(8,128)(2,1)}) %reduce-scatter.14.cloned.1.call-update) | async-done | bytes 1572880 | tf_op jit(solution)/shard_map/reduce_scatter | solution.py:136
  602.4 36.4 %all-gather.21.cloned.1.call-done = bf16[768,1536]{1,0:T(8,128)(2,1)} async-done(((bf16[48,1536]{1,0:T(8,128)(2,1)}), bf16[768,1536]{1,0:T(8,128)(2,1)}) %all-gather.21.cloned.1.call-update) | async-done | bytes 2359312 | tf_op jit(solution)/shard_map/all_gather | solution.py:122
  638.8 45.9 %all-gather.19.cloned.1.call-done = bf16[2048,768]{1,0:T(8,128)(2,1)} async-done(((bf16[1024,768]{1,0:T(8,128)(2,1)}), bf16[2048,768]{1,0:T(8,128)(2,1)}) %all-gather.19.cloned.1.call-update) | async-done | bytes 3145744 | tf_op jit(solution)/shard_map/all_gather | solution.py:128
  684.6 35.1 %multiply_convert_fusion.2 = (bf16[2048,1536]{1,0:T(8,128)(2,1)}, f32[2048,1536]{1,0:T(8,128)}, f32[2048,1536]{1,0:T(8,128)}) fusion(f32[1536]{0:T(1024)S(1)} %dynamic_slice.58, bf16[2048,768]{1,0:T(8,128)(2,1)} %all-gather.19.cloned.1.call-done, bf16[768,1536]{1,0:T(8,128)(2,1)} %all-gather.21.cloned.1.call-done), kind=kOutput, calls=%fused_computation.91 | convolution fusion | flops 5039456256 | bytes 36968448 | tf_op jit(solution)/shard_map/dot_general | solution.py:261
  731.1 44.4 %all-gather.23.cloned.1.call-done = bf16[1536,768]{0,1:T(8,128)(2,1)} async-done(((bf16[1536,48]{0,1:T(8,128)(2,1)}), bf16[1536,768]{0,1:T(8,128)(2,1)}) %all-gather.23.cloned.1.call-update) | async-done | bytes 2359312 | tf_op jit(solution)/shard_map/all_gather | solution.py:123
  811.5 33.1 %reduce-scatter.18.cloned.1.call-done = bf16[1024,768]{1,0:T(8,128)(2,1)} async-done(((bf16[2048,768]{1,0:T(8,128)(2,1)}), bf16[1024,768]{1,0:T(8,128)(2,1)}) %reduce-scatter.18.cloned.1.call-update) | async-done | bytes 1572880 | tf_op jit(solution)/shard_map/reduce_scatter | solution.py:145
  848.7 41.4 %reduce-scatter.16.cloned.1.call-done = bf16[1024,768]{1,0:T(8,128)(2,1)} async-done(((bf16[2048,768]{1,0:T(8,128)(2,1)}), bf16[1024,768]{1,0:T(8,128)(2,1)}) %reduce-scatter.16.cloned.1.call-update) | async-done | bytes 1572880 | tf_op jit(solution)/shard_map/reduce_scatter | solution.py:136
  897.1 45.0 %all-gather.27.cloned.1.call-done = bf16[2048,768]{1,0:T(8,128)(2,1)} async-done(((bf16[1024,768]{1,0:T(8,128)(2,1)}), bf16[2048,768]{1,0:T(8,128)(2,1)}) %all-gather.27.cloned.1.call-update) | async-done | bytes 3145744 | tf_op jit(solution)/shard_map/all_gather | solution.py:132
  958.2 212.2 %while.56 = (s32[]{:T(128)}, f32[1500,6,64]{0,2,1:T(8,128)}, f32[1500,6,64]{0,2,1:T(8,128)}, bf16[4,512,6,64]{1,3,2,0:T(8,128)(2,1)}, bf16[4,512,6,64]{1,3,2,0:T...) while((s32[]{:T(128)}, f32[1500,6,64]{0,2,1:T(8,128)}, ...), condition=%wide.region_22.23_spmd.clone, body=%wide.region_20.22_spmd.clone.sunk | while | flops 2992892928 | bytes 182835472 | solution.py:101
  1179.2 43.4 %reduce-scatter.20.cloned.1.call-done = bf16[1024,768]{1,0:T(8,128)(2,1)} async-done(((bf16[2048,768]{1,0:T(8,128)(2,1)}), bf16[1024,768]{1,0:T(8,128)(2,1)}) %reduce-scatter.20.cloned.1.call-update) | async-done | bytes 1572880 | tf_op jit(solution)/shard_map/reduce_scatter | solution.py:145
  1246.8 32.9 %all-gather.29.cloned.1.call-done = bf16[2048,768]{1,0:T(8,128)(2,1)} async-done(((bf16[1024,768]{1,0:T(8,128)(2,1)}), bf16[2048,768]{1,0:T(8,128)(2,1)}) %all-gather.29.cloned.1.call-update) | async-done | bytes 3145744 | tf_op jit(solution)/shard_map/all_gather | solution.py:132
  1295.2 348.4 %while.57 = (s32[]{:T(128)}, f32[2048,6,64]{0,2,1:T(8,128)}, f32[2048,6,64]{0,2,1:T(8,128)}, bf16[4,512,6,64]{1,3,2,0:T(8,128)(2,1)}, bf16[4,512,6,64]{1,3,2,0:T...) while((s32[]{:T(128)}, f32[2048,6,64]{0,2,1:T(8,128)}, ...), condition=%wide.region_28.29_spmd.clone, body=%wide.region_26.28_spmd.clone.sunk | while | flops 4109368320 | bytes 212725936 | solution.py:101
  1341.6 21.1 multiply_convert_fusion.7
  1428.1 21.1 multiply_convert_fusion.7
  1515.5 21.1 multiply_convert_fusion.7
  1602.9 21.1 multiply_convert_fusion.7
  1711.1 102.9 %all-reduce.6.cloned.1.call-done = (f32[768,3,384]{2,1,0:T(4,128)}, f32[768,2,384]{2,1,0:T(2,128)}) async-done(((f32[768,3,384]{2,1,0:T(4,128)}, f32[768,2,384]{2,1,0:T(2,128)}), (f32[768,3,384]{2,1,0:T(4,128)}, f32[768,2,384]{2,1,0:T(2,128)})) %all-reduce.6.cloned.1.call-update) | async-done | bytes 5898256
  1817.3 42.3 %reduce-scatter.22.cloned.1.call-done = bf16[1024,768]{1,0:T(8,128)(2,1)} async-done(((bf16[2048,768]{1,0:T(8,128)(2,1)}), bf16[1024,768]{1,0:T(8,128)(2,1)}) %reduce-scatter.22.cloned.1.call-update) | async-done | bytes 1572880 | tf_op jit(solution)/shard_map/reduce_scatter | solution.py:145
  1864.9 41.1 %all-reduce.2 = (f32[3,768]{1,0:T(4,128)}, f32[3,768]{1,0:T(4,128)}, f32[6,768]{1,0:T(8,128)}, f32[3072]{0:T(1024)}, f32[768]{0:T(1024)}) all-reduce(f32[3,768]{1,0:T(4,128)S(1)} %pad_maximum_fusion.3, f32[3,768]{1,0:T(4,128)S(1)} %pad_maximum_fusion.4, ...), channel_id=1, replica_groups=mesh['dp'=16,'tensor'=2] {'dp','tensor'}, use_global_device_ids=true, to_apply=%region_42.43 | all-reduce | flops 13056 | bytes 104448 | tf_op jit(solution)/shard_map/psum | solution.py:358
  1910.6 29.5 %reduce-scatter.30.cloned.1.call-done = f32[48,1536]{1,0:T(8,128)} async-done(((f32[768,1536]{1,0:T(8,128)}), f32[48,1536]{1,0:T(8,128)}) %reduce-scatter.30.cloned.1.call-update) | async-done | bytes 294928 | tf_op jit(solution)/shard_map/reduce_scatter | solution.py:342
  1940.1 79.5 %reduce-scatter.32.cloned.1.call-done = f32[1536,48]{0,1:T(8,128)} async-done(((f32[1536,768]{0,1:T(8,128)}), f32[1536,48]{0,1:T(8,128)}) %reduce-scatter.32.cloned.1.call-update) | async-done | bytes 294928 | tf_op jit(solution)/shard_map/reduce_scatter | solution.py:343
  2019.6 61.1 %reduce-scatter.28.cloned.1.call-done = f32[384,48]{0,1:T(8,128)} async-done(((f32[384,768]{0,1:T(8,128)}), f32[384,48]{0,1:T(8,128)}) %reduce-scatter.28.cloned.1.call-update) | async-done | bytes 73744 | tf_op jit(solution)/shard_map/reduce_scatter | solution.py:341
  2080.7 61.3 %reduce-scatter.26.cloned.1.call-done = f32[48,384]{1,0:T(8,128)} async-done(((f32[768,384]{1,0:T(8,128)}), f32[48,384]{1,0:T(8,128)}) %reduce-scatter.26.cloned.1.call-update) | async-done | bytes 73744 | tf_op jit(solution)/shard_map/reduce_scatter | solution.py:339
  2142.0 61.3 %reduce-scatter.24.cloned.1.call-done = f32[384,48]{0,1:T(8,128)} async-done(((f32[384,768]{0,1:T(8,128)}), f32[384,48]{0,1:T(8,128)}) %reduce-scatter.24.cloned.1.call-update) | async-done | bytes 73744 | tf_op jit(solution)/shard_map/reduce_scatter | solution.py:338
  (530 shorter events, 1050.2 us)
Async XLA Ops:
  7.2 374.6 %copy-start = (bf16[1,1500,768]{2,1,0:T(8,128)(2,1)S(1)}, bf16[1,1500,768]{2,1,0:T(8,128)(2,1)}, u32[]{:S(2)}) copy-start(bf16[1,1500,768]{2,1,0:T(8,128)(2,1)} %param.26) | copy-start | bytes 6912004
  7.2 48.3 %all-gather.13.cloned.1.call-start = ((), (), s32[]{:S(2)}) async-start(), calls=%async_computation.12 | async-start | bytes 1880064 | tf_op jit(solution)/shard_map/all_gather | solution.py:117
  7.9 93.3 %all-gather.11.cloned.1.call-start = ((), (), s32[]{:S(2)}) async-start(), calls=%async_computation.11 | async-start | bytes 4718592 | tf_op jit(solution)/shard_map/all_gather | solution.py:200
  17.7 310.0 %reduce-scatter.12.cloned.1.call-start = ((), (), s32[]{:S(2)}) async-start(), calls=%async_computation.13 | async-start | bytes 4718592 | tf_op jit(solution)/shard_map/reduce_scatter | solution.py:136
  284.2 96.0 %all-gather.17.cloned.1.call-start = ((), (), s32[]{:S(2)}) async-start(), calls=%async_computation.15 | async-start | bytes 1253376 | tf_op jit(solution)/shard_map/all_gather | solution.py:120
  284.8 131.2 %all-gather.15.cloned.1.call-start = ((), (), s32[]{:S(2)}) async-start(), calls=%async_computation.14 | async-start | bytes 4718592 | tf_op jit(solution)/shard_map/all_gather | solution.py:128
  334.7 259.5 %reduce-scatter.14.cloned.1.call-start = ((), (), s32[]{:S(2)}) async-start(), calls=%async_computation.16 | async-start | bytes 4718592 | tf_op jit(solution)/shard_map/reduce_scatter | solution.py:136
  550.7 88.1 %all-gather.21.cloned.1.call-start = ((), (), s32[]{:S(2)}) async-start(), calls=%async_computation.18 | async-start | bytes 2506752 | tf_op jit(solution)/shard_map/all_gather | solution.py:122
  551.4 133.2 %all-gather.19.cloned.1.call-start = ((), (), s32[]{:S(2)}) async-start(), calls=%async_computation.17 | async-start | bytes 4718592 | tf_op jit(solution)/shard_map/all_gather | solution.py:128
  600.9 130.2 %all-gather.25.cloned.1.call-start = ((), (), s32[]{:S(2)}) async-start(), calls=%async_computation.21 | async-start | bytes 4718592 | tf_op jit(solution)/shard_map/all_gather | solution.py:132
  601.6 173.9 %all-gather.23.cloned.1.call-start = ((), (), s32[]{:S(2)}) async-start(), calls=%async_computation.19 | async-start | bytes 2506752 | tf_op jit(solution)/shard_map/all_gather | solution.py:123
  602.2 242.4 %reduce-scatter.18.cloned.1.call-start = ((), (), s32[]{:S(2)}) async-start(), calls=%async_computation.22 | async-start | bytes 4718592 | tf_op jit(solution)/shard_map/reduce_scatter | solution.py:145
  802.3 87.9 %reduce-scatter.16.cloned.1.call-start = ((), (), s32[]{:S(2)}) async-start(), calls=%async_computation.20 | async-start | bytes 4718592 | tf_op jit(solution)/shard_map/reduce_scatter | solution.py:136
  811.5 78.7 %copy-start.93 = (f32[768]{0:T(1024)S(1)}, f32[768]{0:T(1024)}, u32[]{:S(2)}) copy-start(f32[768]{0:T(1024)} %param.41) | copy-start | bytes 9220
  811.5 130.7 %all-gather.27.cloned.1.call-start = ((), (), s32[]{:S(2)}) async-start(), calls=%async_computation.23 | async-start | bytes 4718592 | tf_op jit(solution)/shard_map/all_gather | solution.py:132
  894.7 47.4 %copy-start.40 = (bf16[384,768]{0,1:T(8,128)(2,1)S(1)}, bf16[384,768]{0,1:T(8,128)(2,1)}, u32[]{:S(2)}) copy-start(bf16[384,768]{0,1:T(8,128)(2,1)} %all_gather.53) | copy-start | bytes 1769476
  897.1 325.6 %reduce-scatter.20.cloned.1.call-start = ((), (), s32[]{:S(2)}) async-start(), calls=%async_computation.24 | async-start | bytes 4718592 | tf_op jit(solution)/shard_map/reduce_scatter | solution.py:145
  1179.2 47.9 %copy-start.68 = (f32[1024]{0:T(1024)S(1)}, f32[1024]{0:T(1024)}, u32[]{:S(2)}) copy-start(f32[1024]{0:T(1024)} %copy-done.67) | copy-start | bytes 12292
  1179.2 48.0 %copy-start.64 = (f32[1024]{0:T(1024)S(1)}, f32[1024]{0:T(1024)}, u32[]{:S(2)}) copy-start(f32[1024]{0:T(1024)} %copy-done.63) | copy-start | bytes 12292
  1179.2 100.5 %all-gather.29.cloned.1.call-start = ((), (), s32[]{:S(2)}) async-start(), calls=%async_computation.25 | async-start | bytes 4718592 | tf_op jit(solution)/shard_map/all_gather | solution.py:132
  1234.6 579.4 %all-reduce.6.cloned.1.call-start = ((), (), s32[]{:S(2)}) async-start(), calls=%async_computation.32 | async-start | bytes 14155776
  1663.1 196.6 %reduce-scatter.22.cloned.1.call-start = ((), (), s32[]{:S(2)}) async-start(), calls=%async_computation.26 | async-start | bytes 4718592 | tf_op jit(solution)/shard_map/reduce_scatter | solution.py:145
  1672.2 268.0 %reduce-scatter.30.cloned.1.call-start = ((), (), s32[]{:S(2)}) async-start(), calls=%async_computation.30 | async-start | bytes 5013504 | tf_op jit(solution)/shard_map/reduce_scatter | solution.py:342
  1682.3 337.4 %reduce-scatter.32.cloned.1.call-start = ((), (), s32[]{:S(2)}) async-start(), calls=%async_computation.31 | async-start | bytes 5013504 | tf_op jit(solution)/shard_map/reduce_scatter | solution.py:343
  1692.5 388.2 %reduce-scatter.28.cloned.1.call-start = ((), (), s32[]{:S(2)}) async-start(), calls=%async_computation.29 | async-start | bytes 1253376 | tf_op jit(solution)/shard_map/reduce_scatter | solution.py:341
  1698.0 444.1 %reduce-scatter.26.cloned.1.call-start = ((), (), s32[]{:S(2)}) async-start(), calls=%async_computation.28 | async-start | bytes 1253376 | tf_op jit(solution)/shard_map/reduce_scatter | solution.py:339
  1703.3 500.1 %reduce-scatter.24.cloned.1.call-start = ((), (), s32[]{:S(2)}) async-start(), calls=%async_computation.27 | async-start | bytes 1253376 | tf_op jit(solution)/shard_map/reduce_scatter | solution.py:338
  1705.7 153.9 %copy-start.46 = (f32[1024]{0:T(1024)S(1)}, f32[1024]{0:T(1024)}, u32[]{:S(2)}) copy-start(f32[1024]{0:T(1024)} %copy-done.45) | copy-start | bytes 12292
  1705.7 153.9 %copy-start.52 = (f32[768]{0:T(1024)S(1)}, f32[768]{0:T(1024)}, u32[]{:S(2)}) copy-start(f32[768]{0:T(1024)} %copy-done.51) | copy-start | bytes 9220
  1711.0 151.8 %copy-start.66 = (f32[1024]{0:T(1024)S(1)}, f32[1024]{0:T(1024)}, u32[]{:S(2)}) copy-start(f32[1024]{0:T(1024)} %copy-done.65) | copy-start | bytes 12292
  1711.0 151.8 %copy-start.58 = (f32[1024]{0:T(1024)S(1)}, f32[1024]{0:T(1024)}, u32[]{:S(2)}) copy-start(f32[1024]{0:T(1024)} %copy-done.57) | copy-start | bytes 12292
  1817.3 47.5 %copy-start.86 = (f32[768]{0:T(1024)S(1)}, f32[768]{0:T(1024)}, u32[]{:S(2)}) copy-start(f32[768]{0:T(1024)} %get-tuple-element.578) | copy-start | bytes 9220
  (111 other events, 1034.3 us)
Sparse Core Ops, SparseCore 0:
  10.3 45.0 all-gather.12
  57.6 43.5 all-gather.10
  284.3 43.3 reduce-scatter.11
  330.1 39.8 all-gather.16
  372.0 43.8 all-gather.14
  550.8 43.3 reduce-scatter.13
  596.5 42.2 all-gather.20
  640.9 43.6 all-gather.18
  686.2 44.9 all-gather.24
  733.3 42.2 all-gather.22
  802.4 42.1 reduce-scatter.17
  846.8 43.3 reduce-scatter.15
  897.2 44.9 all-gather.26
  1179.3 43.3 reduce-scatter.19
  1234.7 44.9 all-gather.28
  1663.2 150.7 all-reduce.5
  1816.2 43.3 reduce-scatter.21
  1863.9 76.1 reduce-scatter.29
  1945.0 74.5 reduce-scatter.31
  2023.7 56.9 reduce-scatter.27
  2084.9 57.0 reduce-scatter.25
  2146.2 57.0 reduce-scatter.23
where the time goes:
time: 2220 us; the launch traced here: 2210 us
  waiting for transfers between devices  925 us (42%)
  matrix products  740 us (33%)
  other arithmetic  295 us (13%)
  blocking collectives  122 us (5%)
  local copies, waits for them, and re-layouts  109 us (5%)
    dot_general x16, matrix products, score_block(): jnp.einsum('qhd,khd->hqk', q_rows, key_rows, preferred_element_type=jnp.f...  188 us
    convert_element_type x8, other arithmetic, one_block(): grad_scores = (probs_full * (grad_probs - inner)).astype(jnp.bfloat16)  137 us
    reduce_scatter x3, waiting for transfers between devices, branch_rows(): lax.psum_scatter(jnp.dot(left, right, preferred_element_type=jnp.float32)...  127 us
    dot_general x8, matrix products, one_block(): jnp.einsum('qhd,khd->hqk', grad_rows, values, preferred_element_type=jnp....  121 us
    reduce_scatter x3, waiting for transfers between devices, input_grad_rows(): lax.psum_scatter(lax.dot_general(left, right, (((1,), (1,)), ((), ())), p...  119 us
    unnamed x23, waiting for transfers between devices  106 us
    all_gather x3, waiting for transfers between devices, gather_grad(): return lax.all_gather(grad_low, 'tensor', axis=0, tiled=True)  89.3 us
    dot_general x8, matrix products, one_block(): jnp.einsum('hqk,qhd->khd', probs_full.astype(jnp.bfloat16), grad_rows, pr...  84.9 us
  transfers between devices with their start and end apart: 22, of which 21 were waited for; matrix products, arithmetic and copies ran while one was open for 7% of the time, Pallas kernels for 0%

commit v1 on v0

v1 whole, which is shorter than its diff:
```python
import functools, jax, jax.numpy as jnp
from jax import lax
from jax.experimental import pallas as pl
from jax.experimental.pallas import tpu as pltpu
from jax.sharding import Mesh
from jax.sharding import PartitionSpec as P
HEAD=64
BLK=256
LANES=128
NEG=-1e30
LOG2E=1.4426950408889634
F32=jnp.float32; BF=jnp.bfloat16

def lane_ids(rows): return lax.broadcasted_iota(jnp.int32,(rows,LANES),1)

def nt(a,b): return lax.dot_general(a,b,(((1,),(1,)),((),())),preferred_element_type=F32)
def nn(a,b): return lax.dot_general(a,b,(((1,),(0,)),((),())),preferred_element_type=F32)
def tn(a,b): return lax.dot_general(a,b,(((0,),(0,)),((),())),preferred_element_type=F32)

def pick(head, lanes): return (lanes<64) if head==0 else (lanes>=64)

def self_fwd_kernel(q_ref,k_ref,v_ref,segq_ref,segk_ref,o_ref,lse_ref,vx_ref):
    rows=q_ref.shape[0]; half=rows//2; n=rows//BLK
    vx_ref[:,:LANES]=v_ref[...]
    vx_ref[:,LANES:]=jnp.ones((rows,LANES),BF)
    lanes=lane_ids(BLK)
    for i in range(n):
        r0=i*BLK; kn=r0+BLK
        q=q_ref[r0:kn,:]
        outs=[];lses=[]
        for h in range(2):
            qm=jnp.where(pick(h,lanes),q,jnp.zeros_like(q))
            s=nt(qm,k_ref[:kn,:])
            cut = half if i>=n//2 else r0
            a=s[:,:cut] if cut>0 else None
            b=s[:,cut:]
            w=kn-cut
            qi=lax.broadcasted_iota(jnp.int32,(BLK,w),0)+(r0-cut)
            kj=lax.broadcasted_iota(jnp.int32,(BLK,w),1)
            ok=kj<=qi
            if i>=n//2:
                ok=ok&(segk_ref[:,r0-half-(r0-cut):kn-half]==segq_ref[r0-half:kn-half,:])
            b=jnp.where(ok,b,NEG)
            m=jnp.max(b,-1,keepdims=True)
            if a is not None: m=jnp.maximum(m,jnp.max(a,-1,keepdims=True))
            pb=jnp.exp2(b-m).astype(BF)
            ox=nn(pb,vx_ref[cut:kn,:])
            if a is not None:
                pa=jnp.exp2(a-m).astype(BF)
                ox=ox+nn(pa,vx_ref[:cut,:])
            l=ox[:,LANES:]
            outs.append(ox[:,:LANES]/l); lses.append(m+jnp.log2(l))
        sel=lanes<64
        o_ref[r0:kn,:]=jnp.where(sel,outs[0],outs[1]).astype(BF)
        lse_ref[r0:kn,:]=jnp.where(sel,lses[0],lses[1])

def self_fwd(qkv,segq,segk,heads):
    rows=qkv.shape[0]; npair=heads//2
    return pl.pallas_call(self_fwd_kernel,
        grid=(npair,),
        in_specs=[pl.BlockSpec((rows,LANES),lambda p:(0,p)),
                  pl.BlockSpec((rows,LANES),lambda p:(0,npair+p)),
                  pl.BlockSpec((rows,LANES),lambda p:(0,2*npair+p)),
                  pl.BlockSpec(segq.shape,lambda p:(0,0)),pl.BlockSpec(segk.shape,lambda p:(0,0))],
        out_specs=[pl.BlockSpec((rows,LANES),lambda p:(0,p)),pl.BlockSpec((rows,LANES),lambda p:(0,p))],
        out_shape=[jax.ShapeDtypeStruct((rows,heads*64),BF),jax.ShapeDtypeStruct((rows,heads*64),F32)],
        scratch_shapes=[pltpu.VMEM((rows,2*LANES),BF)],
        compiler_params=pltpu.CompilerParams(vmem_limit_bytes=60*2**20),
        name="self_fwd",
    )(qkv,qkv,qkv,segq,segk)

def cross_fwd_kernel(frames,q_ref,k_ref,v_ref,o_ref,lse_ref,kx_ref,vx_ref):
    rows=q_ref.shape[0]; n=rows//BLK; kp=k_ref.shape[0]
    tail=frames//BLK*BLK
    kx_ref[...]=k_ref[...]
    vx_ref[:,:LANES]=v_ref[...]
    vx_ref[:,LANES:]=jnp.ones((kp,LANES),BF)
    if frames<kp:
        keep=lax.broadcasted_iota(jnp.int32,(kp-tail,LANES),0)+tail<frames
        kx_ref[tail:,:]=jnp.where(keep,k_ref[tail:,:],jnp.zeros((),BF))
        vx_ref[tail:,:LANES]=jnp.where(keep,v_ref[tail:,:],jnp.zeros((),BF))
    lanes=lane_ids(BLK)
    for i in range(n):
        r0=i*BLK
        q=q_ref[r0:r0+BLK,:]
        outs=[];lses=[]
        for h in range(2):
            qm=jnp.where(pick(h,lanes),q,jnp.zeros_like(q))
            s=nt(qm,kx_ref[...])
            if frames<kp:
                kj=lax.broadcasted_iota(jnp.int32,(BLK,kp-tail),1)+tail
                s=jnp.concatenate([s[:,:tail],jnp.where(kj<frames,s[:,tail:],NEG)],axis=1)
            m=jnp.max(s,-1,keepdims=True)
            p=jnp.exp2(s-m).astype(BF)
            ox=nn(p,vx_ref[...])
            l=ox[:,LANES:]
            outs.append(ox[:,:LANES]/l); lses.append(m+jnp.log2(l))
        sel=lanes<64
        o_ref[r0:r0+BLK,:]=jnp.where(sel,outs[0],outs[1]).astype(BF)
        lse_ref[r0:r0+BLK,:]=jnp.where(sel,lses[0],lses[1])

def cross_fwd(q,kv,heads):
    rows=q.shape[0]; npair=heads//2; frames=kv.shape[0]
    kp=(frames+BLK-1)//BLK*BLK
    return pl.pallas_call(functools.partial(cross_fwd_kernel,frames),
        grid=(npair,),
        in_specs=[pl.BlockSpec((rows,LANES),lambda p:(0,p)),
                  pl.BlockSpec((kp,LANES),lambda p:(0,p)),
                  pl.BlockSpec((kp,LANES),lambda p:(0,npair+p))],
        out_specs=[pl.BlockSpec((rows,LANES),lambda p:(0,p)),pl.BlockSpec((rows,LANES),lambda p:(0,p))],
        out_shape=[jax.ShapeDtypeStruct((rows,heads*64),BF),jax.ShapeDtypeStruct((rows,heads*64),F32)],
        scratch_shapes=[pltpu.VMEM((kp,LANES),BF),pltpu.VMEM((kp,2*LANES),BF)],
        compiler_params=pltpu.CompilerParams(vmem_limit_bytes=60*2**20),
        name="cross_fwd",
    )(q,kv,kv)

def split3(x):
    hi=x.astype(BF); r=x-hi.astype(F32); mid=r.astype(BF); lo=(r-mid.astype(F32)).astype(BF)
    return hi,mid,lo

def aug(value,head,lanes,one_lane):
    hi,mid,lo=split3(-value)
    z=jnp.zeros(lanes.shape,F32)
    b=64*head
    x=jnp.where(lanes==b,hi.astype(F32),jnp.where(lanes==b+1,mid.astype(F32),jnp.where(lanes==b+2,lo.astype(F32),z)))
    if one_lane: x=jnp.where(lanes==b+3,1.0,x)
    return x.astype(BF)

def build_q(q_ref,do_ref,o_ref,lse_ref,qx_ref,dox_ref,masked):
    rows=q_ref.shape[0]
    lanes=lane_ids(BLK)
    for r0 in range(0,rows,BLK):
        r1=r0+BLK
        q=q_ref[r0:r1,:]; do=do_ref[r0:r1,:]; lse=lse_ref[r0:r1,:]
        prod=do.astype(F32)*o_ref[r0:r1,:].astype(F32)
        for h in range(2):
            sel=pick(h,lanes)
            delta=jnp.sum(jnp.where(sel,prod,0.0),-1,keepdims=True)
            qx_ref[h,r0:r1,:LANES]=jnp.where(sel,q,jnp.zeros((),BF))
            qx_ref[h,r0:r1,LANES:]=aug(lse,h,lanes,masked)
            dox_ref[h,r0:r1,:LANES]=jnp.where(sel,do,jnp.zeros((),BF))
            dox_ref[h,r0:r1,LANES:]=aug(delta,h,lanes,False)

def build_k(k_ref,v_ref,kx_ref,km_ref,vx_ref,frames):
    rows=k_ref.shape[0]
    lanes=lane_ids(BLK)
    low=lanes%64
    for r0 in range(0,rows,BLK):
        r1=r0+BLK
        k=k_ref[r0:r1,:]; v=v_ref[r0:r1,:]
        ones=jnp.where(low<3,1.0,0.0)
        if frames is not None:
            kones=jnp.where(low==3,0.0,ones)
            if r1>frames:
                bad=lax.broadcasted_iota(jnp.int32,(BLK,LANES),0)+r0>=frames
                k=jnp.where(bad,jnp.zeros((),BF),k); v=jnp.where(bad,jnp.zeros((),BF),v)
                kones=jnp.where(bad&(low==3),NEG,ones)
        else: kones=ones
        kx_ref[r0:r1,:LANES]=k; kx_ref[r0:r1,LANES:]=kones.astype(BF)
        vx_ref[r0:r1,:LANES]=v; vx_ref[r0:r1,LANES:]=ones.astype(BF)
        for h in range(2): km_ref[h,r0:r1,:]=jnp.where(pick(h,lanes),k,jnp.zeros((),BF))

def block_back(kx,vx,km,qx,dox,mask):
    s=nt(kx,qx)
    if mask is not None: s=jnp.where(mask,s,NEG)
    p=jnp.exp2(s)
    dp=nt(vx,dox)
    ds=(p*dp).astype(BF)
    pb=p.astype(BF)
    dv=nn(pb,dox[:,:LANES])
    dk=nn(ds,qx[:,:LANES])
    dq=tn(ds,km)
    return dv,dk,dq

def self_bwd_kernel(q_ref,k_ref,v_ref,do_ref,o_ref,lse_ref,segq_ref,segk_ref,dq_ref,dk_ref,dv_ref,
                    qx_ref,dox_ref,kx_ref,km_ref,vx_ref,dqa_ref,dka_ref,dva_ref):
    rows=q_ref.shape[0]; n=rows//BLK; half=rows//2
    build_q(q_ref,do_ref,o_ref,lse_ref,qx_ref,dox_ref,False)
    build_k(k_ref,v_ref,kx_ref,km_ref,vx_ref,None)
    dqa_ref[...]=jnp.zeros_like(dqa_ref)
    tri=lax.broadcasted_iota(jnp.int32,(BLK,BLK),0)<=lax.broadcasted_iota(jnp.int32,(BLK,BLK),1)
    def pair(j,i,mask,first):
        kr=pl.ds(pl.multiple_of(j*BLK,BLK),BLK); qr=pl.ds(pl.multiple_of(i*BLK,BLK),BLK)
        r=[block_back(kx_ref[kr,:],vx_ref[kr,:],km_ref[h,kr,:],qx_ref[h,qr,:],dox_ref[h,qr,:],mask) for h in range(2)]
        dv=r[0][0]+r[1][0]; dk=r[0][1]+r[1][1]; dq=r[0][2]+r[1][2]
        if first: dva_ref[...]=dv; dka_ref[...]=dk
        else: dva_ref[...]+=dv; dka_ref[...]+=dk
        dqa_ref[qr,:]+=dq
    def flush(j):
        kr=pl.ds(pl.multiple_of(j*BLK,BLK),BLK)
        dk_ref[kr,:]=(dka_ref[...]*(1/LOG2E)).astype(BF)
        dv_ref[kr,:]=dva_ref[...].astype(BF)
    def outer_prompt(j,_):
        pair(j,j,tri,True)
        def inner(i,_): pair(j,i,None,False); return 0
        lax.fori_loop(j+1,n,inner,0)
        flush(j); return 0
    lax.fori_loop(0,n//2,outer_prompt,0)
    def segmask(j,i):
        sk=segk_ref[pl.ds(pl.multiple_of(j*BLK-half,BLK),BLK),:]
        sq=segq_ref[i-n//2]
        return sk==sq
    def outer_cont(j,_):
        pair(j,j,tri&segmask(j,j),True)
        def inner(i,_): pair(j,i,segmask(j,i),False); return 0
        lax.fori_loop(j+1,n,inner,0)
        flush(j); return 0
    lax.fori_loop(n//2,n,outer_cont,0)
    dq_ref[...]=(dqa_ref[...]*0.125).astype(BF)

def self_bwd(qkv,do,o,lse,segq,segk,heads):
    rows=qkv.shape[0]; npair=heads//2
    big=lambda f:pl.BlockSpec((rows,LANES),f)
    out=jax.ShapeDtypeStruct((rows,heads*64),BF)
    return pl.pallas_call(self_bwd_kernel,
        grid=(npair,),
        in_specs=[big(lambda p:(0,p)),big(lambda p:(0,npair+p)),big(lambda p:(0,2*npair+p)),big(lambda p:(0,p)),big(lambda p:(0,p)),big(lambda p:(0,p)),
                  pl.BlockSpec(segq.shape,lambda p:(0,0,0)),pl.BlockSpec(segk.shape,lambda p:(0,0))],
        out_specs=[big(lambda p:(0,p))]*3,
        out_shape=[out]*3,
        scratch_shapes=[pltpu.VMEM((2,rows,2*LANES),BF),pltpu.VMEM((2,rows,2*LANES),BF),pltpu.VMEM((rows,2*LANES),BF),
                        pltpu.VMEM((2,rows,LANES),BF),pltpu.VMEM((rows,2*LANES),BF),pltpu.VMEM((rows,LANES),F32),
                        pltpu.VMEM((BLK,LANES),F32),pltpu.VMEM((BLK,LANES),F32)],
        compiler_params=pltpu.CompilerParams(vmem_limit_bytes=60*2**20),
        name="self_bwd",
    )(qkv,qkv,qkv,do,o,lse,segq,segk)

def cross_bwd_kernel(frames,q_ref,k_ref,v_ref,do_ref,o_ref,lse_ref,dq_ref,dk_ref,dv_ref,
                     qx_ref,dox_ref,kx_ref,km_ref,vx_ref,dqa_ref,dka_ref,dva_ref):
    rows=q_ref.shape[0]; n=rows//BLK; kp=k_ref.shape[0]; nk=kp//BLK
    build_q(q_ref,do_ref,o_ref,lse_ref,qx_ref,dox_ref,True)
    build_k(k_ref,v_ref,kx_ref,km_ref,vx_ref,frames)
    dqa_ref[...]=jnp.zeros_like(dqa_ref)
    def outer(j,_):
        kr=pl.ds(pl.multiple_of(j*BLK,BLK),BLK)
        dva=None
        for i in range(n):
            qr=slice(i*BLK,(i+1)*BLK)
            r=[block_back(kx_ref[kr,:],vx_ref[kr,:],km_ref[h,kr,:],qx_ref[h,qr,:],dox_ref[h,qr,:],None) for h in range(2)]
            dv=r[0][0]+r[1][0]; dk=r[0][1]+r[1][1]; dq=r[0][2]+r[1][2]
            if i==0: dva_ref[...]=dv; dka_ref[...]=dk
            else: dva_ref[...]+=dv; dka_ref[...]+=dk
            dqa_ref[qr,:]+=dq
        dk_ref[kr,:]=(dka_ref[...]*(1/LOG2E)).astype(BF)
        dv_ref[kr,:]=dva_ref[...].astype(BF)
        return 0
    lax.fori_loop(0,nk,outer,0)
    dq_ref[...]=(dqa_ref[...]*0.125).astype(BF)

def cross_bwd(q,kv,do,o,lse,heads):
    rows=q.shape[0]; npair=heads//2; frames=kv.shape[0]
    kp=(frames+BLK-1)//BLK*BLK
    big=lambda f:pl.BlockSpec((rows,LANES),f)
    kb=lambda f:pl.BlockSpec((kp,LANES),f)
    return pl.pallas_call(functools.partial(cross_bwd_kernel,frames),
        grid=(npair,),
        in_specs=[big(lambda p:(0,p)),kb(lambda p:(0,p)),kb(lambda p:(0,npair+p)),big(lambda p:(0,p)),big(lambda p:(0,p)),big(lambda p:(0,p))],
        out_specs=[big(lambda p:(0,p)),kb(lambda p:(0,p)),kb(lambda p:(0,p))],
        out_shape=[jax.ShapeDtypeStruct((rows,heads*64),BF),jax.ShapeDtypeStruct((frames,heads*64),BF),jax.ShapeDtypeStruct((frames,heads*64),BF)],
        scratch_shapes=[pltpu.VMEM((2,rows,2*LANES),BF),pltpu.VMEM((2,rows,2*LANES),BF),pltpu.VMEM((kp,2*LANES),BF),
                        pltpu.VMEM((2,kp,LANES),BF),pltpu.VMEM((kp,2*LANES),BF),pltpu.VMEM((rows,LANES),F32),
                        pltpu.VMEM((BLK,LANES),F32),pltpu.VMEM((BLK,LANES),F32)],
        compiler_params=pltpu.CompilerParams(vmem_limit_bytes=60*2**20),
        name="cross_bwd",
    )(q,kv,kv,do,o,lse)


EPSILON = 1e-05


def layer_norm(values, gain_row, offset_row):
    centre = values - jnp.mean(values, -1, keepdims=True)
    spread = jnp.mean(centre * centre, -1, keepdims=True)
    return centre * lax.rsqrt(spread + EPSILON) * gain_row + offset_row


def exact_gelu(values):
    return jax.nn.gelu(values, approximate=False)


ALL = ("chip", "core", "tensor")


def fetch(shard):
    rows, cols = shard.shape
    full = lax.all_gather(shard, ALL, axis=0, tiled=False)
    return full.reshape(-1, 2, rows, cols).transpose(0, 2, 1, 3).reshape(-1, 2, cols)


def spread_sum(grad):
    rows, _, cols = grad.shape
    here = rows // (lax.axis_size("chip") * 2)
    blocks = grad.astype(BF).reshape(-1, here, 2, cols).transpose(0, 2, 1, 3).reshape(-1, cols)
    return lax.psum_scatter(blocks, ALL, scatter_dimension=0, tiled=True).astype(F32)


def on_device(tokens, memory, seg_ids, positions, grad_output, attn_in, attn_out, cross_q, cross_kv,
              cross_out, mlp_in, mlp_out, norm_gain, norm_bias, proj_bias, mlp_bias, out_bias):
    width = tokens.shape[1]
    part = attn_in.shape[2]
    units = mlp_in.shape[1]
    heads = width // HEAD
    core = lax.axis_index("core")
    tensor = lax.axis_index("tensor")
    swap = [(0, 0), (1, 2), (2, 1), (3, 3)]
    fix = lambda x: lax.ppermute(x, ("core", "tensor"), swap)
    other = lambda x: lax.ppermute(x, "core", [(0, 1), (1, 0)])

    def norm_back(resid_in, index_row, grad_norm):
        _, pull = jax.vjp(layer_norm, resid_in, norm_gain[index_row], norm_bias[index_row])
        return pull(grad_norm)

    rows_here = attn_in.shape[0]
    w_a = fetch(attn_in.reshape(rows_here, 3 * part))
    w_b = fetch(jnp.concatenate([attn_out.T, cross_q, cross_kv.reshape(rows_here, 2 * part), cross_out.T], 1))
    w_c = fetch(jnp.concatenate([mlp_in, mlp_out.T], 1))
    w_qkv = w_a.reshape(width, 2 * 3 * part)
    wt_attn_out = w_b[:, :, :part].reshape(width, width)
    w_cross_q = w_b[:, :, part:2 * part].reshape(width, width)
    w_cross_kv = w_b[:, :, 2 * part:4 * part].reshape(width, 2, 2, part).transpose(0, 2, 1, 3).reshape(width, 2 * width)
    wt_cross_out = w_b[:, :, 4 * part:].reshape(width, width)
    w_mlp_in = w_c[:, :, :units].reshape(width, 2 * units)
    wt_mlp_out = w_c[:, :, units:].reshape(width, 2 * units)

    rows = tokens.shape[0]
    moved = fix(tokens)
    grad_in = fix(grad_output)
    seg_mine = fix(seg_ids)
    seg_cont = jnp.where(core == 1, seg_mine, other(seg_mine))
    mem = memory[0]
    mem = jnp.where(core == tensor, mem, other(mem))

    resid_zero = moved.astype(F32)
    norm_one = layer_norm(resid_zero, norm_gain[0], norm_bias[0]).astype(BF)
    qkv = jnp.dot(norm_one, w_qkv, preferred_element_type=F32).reshape(rows, 2, 3, part)
    add = jnp.stack([proj_bias[0].reshape(2, part), jnp.zeros((2, part), F32), proj_bias[1].reshape(2, part)], 1)
    scale = jnp.array([HEAD ** -0.5 * LOG2E, 1.0, 1.0], F32)[None, :, None]
    qkv = ((qkv + add) * scale).astype(BF).reshape(rows, 2, 3 * part)

    def to_heads(x):
        kept = jnp.where(core == 0, x[:, 0], x[:, 1])
        come = other(jnp.where(core == 0, x[:, 1], x[:, 0]))
        return jnp.concatenate([jnp.where(core == 0, kept, come), jnp.where(core == 0, come, kept)], 0)

    def to_tokens(x):
        kept = jnp.where(core == 0, x[:rows], x[rows:])
        come = other(jnp.where(core == 0, x[rows:], x[:rows]))
        return jnp.stack([jnp.where(core == 0, kept, come), jnp.where(core == 0, come, kept)], 1)

    qkv_heads = to_heads(qkv)
    attn_heads, lse_self = self_fwd(qkv_heads, seg_cont[:, None], seg_cont[None, :], heads // 2)
    attn_self = to_tokens(attn_heads).reshape(rows, width)
    resid_one = resid_zero + nt(attn_self, wt_attn_out) + proj_bias[2]
    norm_two = layer_norm(resid_one, norm_gain[1], norm_bias[1]).astype(BF)
    q_cross = ((nn(norm_two, w_cross_q) + proj_bias[3]) * (HEAD ** -0.5 * LOG2E)).astype(BF)
    kv = (nn(mem, w_cross_kv) + jnp.concatenate([jnp.zeros((width,), F32), proj_bias[4]])).astype(BF)
    attn_cross, lse_cross = cross_fwd(q_cross, kv, heads)
    resid_two = resid_one + nt(attn_cross, wt_cross_out) + proj_bias[5]
    norm_three = layer_norm(resid_two, norm_gain[2], norm_bias[2]).astype(BF)
    pre_act = nn(norm_three, w_mlp_in) + mlp_bias
    hidden = exact_gelu(pre_act).astype(BF)
    resid_out = resid_two + nt(hidden, wt_mlp_out) + out_bias
    output = fix(resid_out.astype(BF))

    g_low = grad_in
    grad_resid = grad_in.astype(F32)
    gb_mlp_out = jnp.sum(grad_resid, 0)
    gw_mlp_out = tn(g_low, hidden)
    grad_hidden = nn(g_low, wt_mlp_out)
    _, gelu_pull = jax.vjp(exact_gelu, pre_act)
    grad_pre = gelu_pull(grad_hidden)[0].astype(BF)
    gw_mlp_in = tn(norm_three, grad_pre)
    gb_mlp_in = jnp.sum(grad_pre, 0, dtype=F32)
    g_c = spread_sum(jnp.concatenate([gw_mlp_in.reshape(width, 2, units), gw_mlp_out.reshape(width, 2, units)], 2))
    grad_input, gain_three, shift_three = norm_back(resid_two, 2, nt(grad_pre, w_mlp_in))
    grad_resid = grad_resid + grad_input
    g_low = grad_resid.astype(BF)
    gb_cross_out = jnp.sum(grad_resid, 0)
    gw_cross_out = tn(g_low, attn_cross)
    grad_attn = nn(g_low, wt_cross_out).astype(BF)
    dq, dk, dv = cross_bwd(q_cross, kv, grad_attn, attn_cross, lse_cross, heads)
    gw_cross_q = tn(norm_two, dq)
    gb_cross_q = jnp.sum(dq, 0, dtype=F32)
    gw_cross_k = tn(mem, dk)
    gw_cross_v = tn(mem, dv)
    gb_cross_v = jnp.sum(dv, 0, dtype=F32)
    grad_input, gain_two, shift_two = norm_back(resid_one, 1, nt(dq, w_cross_q))
    grad_resid = grad_resid + grad_input
    g_low = grad_resid.astype(BF)
    gb_attn_out = jnp.sum(grad_resid, 0)
    gw_attn_out = tn(g_low, attn_self)
    split = lambda x: x.reshape(width, 2, part)
    g_b = spread_sum(jnp.concatenate([split(gw_attn_out), split(gw_cross_q), split(gw_cross_k), split(gw_cross_v), split(gw_cross_out)], 2))
    grad_attn = nn(g_low, wt_attn_out).astype(BF)
    dq, dk, dv = self_bwd(qkv_heads, to_heads(grad_attn.reshape(rows, 2, part)), attn_heads, lse_self,
                          seg_cont.reshape(-1, 1, BLK), seg_cont[:, None], heads // 2)
    dqkv = to_tokens(jnp.concatenate([dq, dk, dv], 1))
    flat = dqkv.reshape(rows, 2 * 3 * part)
    g_a = spread_sum(tn(norm_one, flat).reshape(width, 2, 3 * part))
    gb_qkv = jnp.sum(flat, 0, dtype=F32).reshape(2, 3, part)
    grad_input, gain_one, shift_one = norm_back(resid_zero, 0, nt(flat, w_qkv))
    grad_tokens = fix((grad_resid + grad_input).astype(BF)).astype(F32)
    gain_grads = jnp.stack([gain_one, gain_two, gain_three])
    shift_grads = jnp.stack([shift_one, shift_two, shift_three])
    proj_grads = jnp.stack([gb_qkv[:, 0].reshape(-1), gb_qkv[:, 2].reshape(-1), gb_attn_out, gb_cross_q, gb_cross_v, gb_cross_out])
    g_gain, g_shift, g_proj, g_units, g_out_bias = lax.psum((gain_grads, shift_grads, proj_grads, gb_mlp_in, gb_mlp_out), ALL)
    cut = lambda i: g_b[:, i * part:(i + 1) * part]
    return (output, grad_tokens, g_a.reshape(rows_here, 3, part), cut(0).T, cut(1),
            g_b[:, 2 * part:4 * part].reshape(rows_here, 2, part), cut(4).T,
            g_c[:, :units], g_c[:, units:].T, g_gain, g_shift, g_proj, g_units, g_out_bias)


def solution(mesh):
    devices = mesh.devices.reshape(-1, 2, mesh.shape["tensor"])
    grid = Mesh(devices, ALL)
    dp = ("chip", "core")
    in_specs = (P(ALL, None), P(dp, None, None), P(ALL), P(ALL), P(ALL, None), P(dp, None, "tensor"), P("tensor", dp),
                P(dp, "tensor"), P(dp, None, "tensor"), P("tensor", dp), P(dp, "tensor"), P("tensor", dp),
                P(), P(), P(), P(), P())
    out_specs = (P(ALL, None), P(ALL, None), P(dp, None, "tensor"), P("tensor", dp), P(dp, "tensor"), P(dp, None, "tensor"),
                 P("tensor", dp), P(dp, "tensor"), P("tensor", dp), P(), P(), P(), P(), P())
    return jax.shard_map(on_device, mesh=grid, in_specs=in_specs, out_specs=out_specs, check_vma=False)
```

time: 2220 us -> 956 us (0.43)
  waiting for transfers between devices: 925 us -> 191 us
  matrix products: 740 us -> 165 us
  other arithmetic: 295 us -> 72.5 us
  Pallas kernels: 0 us -> 221 us
  blocking collectives: 122 us -> 39 us
  local copies, waits for them, and re-layouts: 109 us -> 189 us
  starting transfers between devices: 0.9 us -> 48.4 us
    dot_general x76 -> x21, matrix products: 740 us -> 165 us  [the longest x6 70.6 us: nn(): lax.dot_general(a, b, (((1,), (0,)), ((), ())), preferred_element_type=F32)]
    reduce_scatter x11 -> x3, waiting for transfers between devices: 539 us -> 125 us  [spread_sum(): lax.psum_scatter(blocks, ALL, scatter_dimension=0, tiled=True).astype(F32)]
    all_gather x10 -> x3, waiting for transfers between devices: 280 us -> 57.3 us  [fetch(): full = lax.all_gather(shard, ALL, axis=0, tiled=False)]
    pallas_call x0 -> x4, Pallas kernels: none -> 221 us  [the longest x1 84.5 us: cross_bwd(): pl.pallas_call(functools.partial(cross_bwd_kernel, frames), grid=(npair,)...]
    convert_element_type x15 -> x5, other arithmetic: 150 us -> 7.6 us  [the longest x2 3.44 us: on_device(): g_low = grad_resid.astype(BF)]
    unnamed x23 -> x6, waiting for transfers between devices: 106 us -> 0.1 us
    reduce_sum x14 -> x4, other arithmetic: 96.7 us -> 6.81 us  [the longest x1 3.41 us: on_device(): gb_mlp_out = jnp.sum(grad_resid, 0)]
    all_gather x5 -> x0, blocking collectives: 81.1 us -> none  [the longest x1 26.1 us: fetch_weights(): lax.all_gather(attn_out, 'dp', axis=1, tiled=True)]
  transfers between devices with their start and end apart: 22 -> 17, of which waited for: 21 -> 5; matrix products, arithmetic and copies ran while one was open for 7% -> 35% of each run, Pallas kernels for 0% -> 6%
where the time goes in v1:
time: 956 us; the launch traced here: 942 us
  Pallas kernels  221 us (23%)
  waiting for transfers between devices  191 us (20%)
  local copies, waits for them, and re-layouts  189 us (20%)
  matrix products  165 us (17%)
  other arithmetic  72.5 us (8%)
  starting transfers between devices  48.4 us (5%)
  blocking collectives  39 us (4%)
  between operations  15.5 us (2%)
    reduce_scatter x3, waiting for transfers between devices, spread_sum(): lax.psum_scatter(blocks, ALL, scatter_dimension=0, tiled=True).astype(F32)  125 us
    pallas_call x1, Pallas kernels, cross_bwd(): pl.pallas_call(functools.partial(cross_bwd_kernel, frames), grid=(npair,)...  84.5 us
    pallas_call x1, Pallas kernels, self_bwd(): pl.pallas_call(self_bwd_kernel, grid=(npair,), in_specs=[big(lambda p: (0...  82.9 us
    dot_general x6, matrix products, nn(): lax.dot_general(a, b, (((1,), (0,)), ((), ())), preferred_element_type=F32)  70.6 us
    all_gather x3, waiting for transfers between devices, fetch(): full = lax.all_gather(shard, ALL, axis=0, tiled=False)  57.3 us
    dot_general x8, matrix products, tn(): lax.dot_general(a, b, (((0,), (0,)), ((), ())), preferred_element_type=F32)  50 us
    unnamed x153, local copies, waits for them, and re-layouts  42.3 us
    ppermute x5, starting transfers between devices, on_device(): fix = lambda x: lax.ppermute(x, ('core', 'tensor'), swap)  41.6 us
  transfers between devices with their start and end apart: 17, of which 5 were waited for; matrix products, arithmetic and copies ran while one was open for 35% of the time, Pallas kernels for 6%

profile of v1, /device:TPU:0, one launch (start us, length us, event | category | flops | bytes accessed | tf_op | source)
XLA Modules:
  0.0 942.0 jit_solution(5012099242953155052)
XLA Ops:
  17.2 57.3 %all-gather.6.cloned.1.call-done = bf16[32,48,1152]{2,1,0:T(8,128)(2,1)} async-done(((bf16[1,48,1152]{2,1,0:T(8,128)(2,1)}), bf16[32,48,1152]{2,1,0:T(8,128)(2,1)}) %all-gather.6.cloned.1.call-update) | async-done | bytes 3538960 | tf_op jit(solution)/shard_map/all_gather | solution.py:286
  81.6 5.8 copy.117
  87.4 6.1 multiply_convert_fusion.1
  120.4 26.4 %self_fwd.1 = (bf16[2048,384]{1,0:T(8,128)(2,1)}, f32[2048,384]{1,0:T(8,128)}) custom-call(bf16[2048,1152]{1,0:T(8,128)(2,1)} %pad_maximum_fusion.q_ref.k_ref.v_ref, bf16[2048,1152]{1,0:T(8,128)(2,1)} %pad_maximum_fusion.q_ref.k_ref.v_ref, bf16[2048,1152]{1,0:T(8,128)(2,1)} %pad_maximum_fusion.q_ref.k_ref.v_ref, s32[1024,1]{1,0:T(8,128)} %copy.123.segq_ref.segk_ref, ...), custom_call_target="tpu_custom_call" | custom-call | tf_op jit(solution)/shard_map/self_fwd/pallas_call | solution.py:59
  151.4 13.3 %collective-permute-start.7 = (bf16[1024,768]{0,1:T(8,128)(2,1)}, bf16[1024,768]{0,1:T(8,128)(2,1)}, u32[]{:S(2)}, u32[]{:S(2)}) collective-permute-start(bf16[1024,768]{0,1:T(8,128)(2,1)} %copy.132), channel_id=1, source_target_pairs={{0,0},{1,2},{2,1},{3,3},{4,4},{5,6},{6,5},{7,7},{8,8},{9,10},{10,9... | collective-permute-start | bytes 4718600 | tf_op jit(solution)/shard_map/ppermute | solution.py:306
  202.5 5.6 add_convert_fusion.k_ref.v_ref
  208.2 27.5 %cross_fwd.1 = (bf16[1024,768]{1,0:T(8,128)(2,1)}, f32[1024,768]{1,0:T(8,128)}) custom-call(bf16[1024,768]{1,0:T(8,128)(2,1)} %multiply_convert_fusion.2.q_ref, bf16[1500,1536]{1,0:T(8,128)(2,1)} %add_convert_fusion.k_ref.v_ref, bf16[1500,1536]{1,0:T(8,128)(2,1)} %add_convert_fusion.k_ref.v_ref), custom_call_target="tpu_custom_call" | custom-call | tf_op jit(solution)/shard_map/cross_fwd/pallas_call | solution.py:105
  241.1 8.7 copy.128
  249.8 7.9 fusion.56
  257.7 6.8 copy.129
  264.5 37.5 %multiply_convert_fusion = (bf16[1024,3072]{1,0:T(8,128)(2,1)}, f32[1024,3072]{1,0:T(8,128)}, f32[1024,3072]{1,0:T(8,128)}) fusion(f32[3072]{0:T(1024)S(1)} %copy-done.63, bf16[768,3072]{0,1:T(8,128)(2,1)} %bitcast.195, f32[1024,768]{0,1:T(8,128)S(1)} %copy-done.15, f32[768]{0:T(1024)S(1)} %copy-done.58, f32[768]{0:T(1024)S(1)} %get-tuple-element.160, ...), kind=kOutput, calls=%fused_computation.12 | convolution fusion | flops 5043388416 | bytes 39348224 | tf_op jit(solution)/shard_map/dot_general | solution.py:17
  302.0 6.7 copy.130
  308.6 20.5 %convert_reduce_fusion = (f32[3072]{0:T(1024)}, bf16[1024,3072]{1,0:T(8,128)(2,1)}) fusion(f32[1024,3072]{1,0:T(8,128)} %get-tuple-element.121, bf16[768,3072]{0,1:T(8,128)(2,1)} %bitcast.192, bf16[1024,768]{0,1:T(8,128)(2,1)} %collective-permute-done.7, f32[1024,3072]{1,0:T(8,128)} %get-tuple-element.151, f32[3072]{0:T(1024)S(1)} %copy-done.63), kind=kOutput, calls=%fused_computation.11 | convolution fusion | flops 4885312512 | bytes 37773312 | tf_op jit(solution)/shard_map/dot_general | solution.py:17
  329.2 9.4 multiply_reduce_fusion
  345.3 84.5 %cross_bwd.1 = (bf16[1024,768]{1,0:T(8,128)(2,1)}, bf16[1500,768]{1,0:T(8,128)(2,1)}, bf16[1500,768]{1,0:T(8,128)(2,1)}) custom-call(bf16[1024,768]{1,0:T(8,128)(2,1)} %multiply_convert_fusion.2.q_ref, bf16[1500,1536]{1,0:T(8,128)(2,1)} %add_convert_fusion.k_ref.v_ref, bf16[1500,1536]{1,0:T(8,128)(2,1)} %add_convert_fusion.k_ref.v_ref, ...), custom_call_target="tpu_custom_call" | custom-call | tf_op jit(solution)/shard_map/cross_bwd/pallas_call | solution.py:255
  454.5 82.9 %self_bwd.1 = (bf16[2048,384]{1,0:T(8,128)(2,1)}, bf16[2048,384]{1,0:T(8,128)(2,1)}, bf16[2048,384]{1,0:T(8,128)(2,1)}) custom-call(bf16[2048,1152]{1,0:T(8,128)(2,1)} %pad_maximum_fusion.q_ref.k_ref.v_ref, bf16[2048,1152]{1,0:T(8,128)(2,1)} %pad_maximum_fusion.q_ref.k_ref.v_ref, bf16[2048,1152]{1,0:T(8,128)(2,1)} %pad_maximum_fusion.q_ref.k_ref.v_ref, ...), custom_call_target="tpu_custom_call" | custom-call | tf_op jit(solution)/shard_map/self_bwd/pallas_call | solution.py:215
  550.2 6.6 copy.137
  556.9 6.9 fusion.19
  571.6 5.5 convolution_convert_fusion.6
  614.2 9.3 fusion.22
  623.5 6.7 copy.145
  630.2 11.8 %concatenate.52 = bf16[16,48,2,1536]{3,2,1,0:T(2,128)(2,1)} reshape(bf16[768,3072]{1,0:T(8,128)(2,1)} %copy.145) | data formatting | bytes 9437184 | tf_op jit(solution)/shard_map/concatenate | solution.py:374
  642.0 9.9 %convolution_convert_fusion.1 = bf16[768,3072]{1,0:T(8,128)(2,1)} fusion(bf16[1024,3072]{1,0:T(8,128)(2,1)} %get-tuple-element.157, f32[1024,768]{0,1:T(8,128)S(1)} %copy-done.16, f32[768]{0:T(1024)S(1)} %copy-done.58, f32[768]{0:T(1024)S(1)} %get-tuple-element.160, f32[1024]{0:T(1024)S(1)} %fusion.46, f32[1024]{0:T(1024)S(1)} %broadcast_multiply_fusion), kind=kOutput, calls=%fused_computation.31 | convolution fusion | flops 4838129664 | bytes 14170112 | tf_op jit(solution)/shard_map/dot_general | solution.py:18
  651.9 11.7 %concatenate.51 = bf16[16,48,2,1536]{3,2,1,0:T(2,128)(2,1)} reshape(bf16[768,3072]{1,0:T(8,128)(2,1)} %convolution_convert_fusion.1) | data formatting | bytes 9437184 | tf_op jit(solution)/shard_map/concatenate | solution.py:374
  663.5 22.5 %maximum_bitcast_fusion = bf16[16,2,48,3072]{3,1,2,0:T(2,128)(2,1)} fusion(bf16[16,48,2,1536]{3,2,1,0:T(2,128)(2,1)} %concatenate.52, bf16[16,48,2,1536]{3,2,1,0:T(2,128)(2,1)} %concatenate.51), kind=kLoop, calls=%fused_computation.26 | loop fusion | flops 18874368 | bytes 18874368 | tf_op jit(solution)/shard_map/transpose | solution.py:293
  686.1 10.6 %copy.146 = bf16[16,2,48,3072]{3,2,1,0:T(8,128)(2,1)} copy(bf16[16,2,48,3072]{3,1,2,0:T(2,128)(2,1)} %maximum_bitcast_fusion) | data formatting | bytes 18874368 | tf_op jit(solution)/shard_map/transpose | solution.py:293
  697.4 9.9 %add_convert_fusion.2 = bf16[1024,768]{0,1:T(8,128)(2,1)} fusion(f32[1024,768]{0,1:T(8,128)S(1)} %copy-done.16, bf16[1024,3072]{1,0:T(8,128)(2,1)} %get-tuple-element.120, bf16[768,3072]{0,1:T(8,128)(2,1)} %bitcast.193, f32[768]{0:T(1024)S(1)} %copy-done.65), kind=kOutput, calls=%fused_computation.66 | convolution fusion | flops 4834197504 | bytes 15731712 | tf_op jit(solution)/shard_map/dot_general | solution.py:16
  707.3 13.3 %collective-permute-start.6 = (bf16[1024,768]{0,1:T(8,128)(2,1)}, bf16[1024,768]{0,1:T(8,128)(2,1)}, u32[]{:S(2)}, u32[]{:S(2)}) collective-permute-start(bf16[1024,768]{0,1:T(8,128)(2,1)} %add_convert_fusion.2), channel_id=1, source_target_pairs={{0,0},{1,2},{2,1},{3,3},{4,4},{5,6},{6,5},{7,7},{8,8},{9,10},{10,9... | collective-permute-start | bytes 4718600 | tf_op jit(solution)/shard_map/ppermute | solution.py:306
  720.5 8.6 fusion.62
  738.0 13.4 %collective-permute-start.10 = (bf16[1024,768]{0,1:T(8,128)(2,1)}, bf16[1024,768]{0,1:T(8,128)(2,1)}, u32[]{:S(2)}, u32[]{:S(2)}) collective-permute-start(bf16[1024,768]{0,1:T(8,128)(2,1)} %add_convert_fusion.1), channel_id=1, source_target_pairs={{0,0},{1,2},{2,1},{3,3},{4,4},{5,6},{6,5},{7,7},{8,8},{9,10},{10,9... | collective-permute-start | bytes 4718600 | tf_op jit(solution)/shard_map/ppermute | solution.py:306
  757.7 39.0 %all-reduce.1 = (f32[3,768]{1,0:T(4,128)}, f32[3,768]{1,0:T(4,128)}, f32[6,768]{1,0:T(8,128)}, f32[3072]{0:T(1024)}, f32[768]{0:T(1024)}) all-reduce(f32[3,768]{1,0:T(4,128)S(1)} %pad_maximum_fusion.7, f32[3,768]{1,0:T(4,128)S(1)} %pad_maximum_fusion.8, ...), channel_id=1, replica_groups=mesh['chip'=8,'core'=2,'tensor'=2] {'chip','core','tensor'}, use_global_device_ids=true, to_apply=%region_18.19 | all-reduce | flops 13056 | bytes 104448 | tf_op jit(solution)/shard_map/psum | solution.py:406
  806.0 125.3 %reduce-scatter.8.cloned.1.call-done = bf16[48,3072]{1,0:T(8,128)(2,1)} async-done(((bf16[1536,3072]{1,0:T(8,128)(2,1)}), bf16[48,3072]{1,0:T(8,128)(2,1)}) %reduce-scatter.8.cloned.1.call-update) | async-done | bytes 294928 | tf_op jit(solution)/shard_map/reduce_scatter | solution.py:294
  (291 shorter events, 208.6 us)
Async XLA Ops:
  7.2 67.2 %all-gather.6.cloned.1.call-start = ((), (), s32[]{:S(2)}) async-start(), calls=%async_computation.3 | async-start | bytes 3649536 | tf_op jit(solution)/shard_map/all_gather | solution.py:286
  9.1 160.3 %all-gather.8.cloned.1.call-start = ((), (), s32[]{:S(2)}) async-start(), calls=%async_computation.7 | async-start | bytes 6082560 | tf_op jit(solution)/shard_map/all_gather | solution.py:286
  11.6 229.5 %all-gather.10.cloned.1.call-start = ((), (), s32[]{:S(2)}) async-start(), calls=%async_computation.8 | async-start | bytes 9732096 | tf_op jit(solution)/shard_map/all_gather | solution.py:286
  13.4 786.3 %reduce-scatter.4.cloned.1.call-start = ((), (), s32[]{:S(2)}) async-start(), calls=%async_computation.4 | async-start | bytes 3649536 | tf_op jit(solution)/shard_map/reduce_scatter | solution.py:294
  14.2 2.2 collective-permute-start
  15.7 71.7 %copy-start.38 = (f32[768]{0:T(1024)}, f32[768]{0:T(1024)S(1)}, u32[]{:S(2)}) copy-start(f32[768]{0:T(1024)S(1)} %get-tuple-element.159) | copy-start | bytes 9220
  15.7 71.7 %copy-start.61 = (f32[768]{0:T(1024)}, f32[768]{0:T(1024)S(1)}, u32[]{:S(2)}) copy-start(f32[768]{0:T(1024)S(1)} %get-tuple-element.109) | copy-start | bytes 9220
  15.7 182.2 %copy-start.40 = (f32[768]{0:T(1024)}, f32[768]{0:T(1024)S(1)}, u32[]{:S(2)}) copy-start(f32[768]{0:T(1024)S(1)} %get-tuple-element.158) | copy-start | bytes 9220
  16.4 71.0 %copy-start.2 = (bf16[1024,768]{0,1:T(8,128)(2,1)}, bf16[1024,768]{0,1:T(8,128)(2,1)S(1)}, u32[]{:S(2)}) copy-start(bf16[1024,768]{0,1:T(8,128)(2,1)S(1)} %collective-permute-done) | copy-start | bytes 4718596
  16.7 70.7 %copy-start.34 = (f32[1024]{0:T(1024)}, f32[1024]{0:T(1024)S(1)}, u32[]{:S(2)}) copy-start(f32[1024]{0:T(1024)S(1)} %broadcast_multiply_fusion.2) | copy-start | bytes 12292
  17.1 62.0 %copy-start.45 = (f32[1024]{0:T(1024)}, f32[1024]{0:T(1024)S(1)}, u32[]{:S(2)}) copy-start(f32[1024]{0:T(1024)S(1)} %fusion.28) | copy-start | bytes 12292
  17.1 70.2 %copy-start.43 = (f32[1024]{0:T(1024)}, f32[1024]{0:T(1024)S(1)}, u32[]{:S(2)}) copy-start(f32[1024]{0:T(1024)S(1)} %fusion.44) | copy-start | bytes 12292
  106.8 8.9 collective-permute-start.1
  106.8 57.9 %collective-permute-start.5 = (bf16[1500,768]{1,0:T(8,128)(2,1)}, bf16[1500,768]{1,0:T(8,128)(2,1)}, u32[]{:S(2)}, u32[]{:S(2)}) collective-permute-start(bf16[1500,768]{1,0:T(8,128)(2,1)} %bitcast.21), channel_id=1, source_target_pairs={{0,2},{2,0},{1,3},{3,1},{4,6},{6,4},{5,7},{7,5},{8,10},{10,8},{9,1... | collective-permute-start | bytes 6912008 | tf_op jit(solution)/shard_map/ppermute | solution.py:307
  107.3 0.9 collective-permute-start.2
  108.2 6.4 collective-permute-start.3
  148.4 19.7 %collective-permute-start.4 = (bf16[1024,384]{1,0:T(8,128)(2,1)S(1)}, bf16[1024,384]{1,0:T(8,128)(2,1)S(1)}, u32[]{:S(2)}, u32[]{:S(2)}) collective-permute-start(bf16[1024,384]{1,0:T(8,128)(2,1)S(1)} %broadcast_select_fusion.5), channel_id=1, source_target_pairs={{0,2},{2,0},{1,3},{3,1},{4,6},{6,4},{5,7},{7,5},{8,10},{10,8},{9,1... | collective-permute-start | bytes 2359304 | tf_op jit(solution)/shard_map/ppermute | solution.py:307
  151.4 157.3 %collective-permute-start.7 = (bf16[1024,768]{0,1:T(8,128)(2,1)}, bf16[1024,768]{0,1:T(8,128)(2,1)}, u32[]{:S(2)}, u32[]{:S(2)}) collective-permute-start(bf16[1024,768]{0,1:T(8,128)(2,1)} %copy.132), channel_id=1, source_target_pairs={{0,0},{1,2},{2,1},{3,3},{4,4},{5,6},{6,5},{7,7},{8,8},{9,10},{10,9... | collective-permute-start | bytes 4718600 | tf_op jit(solution)/shard_map/ppermute | solution.py:306
  197.4 38.3 %copy-start = (f32[1024,768]{0,1:T(8,128)}, f32[1024,768]{0,1:T(8,128)S(1)}, u32[]{:S(2)}) copy-start(f32[1024,768]{0,1:T(8,128)S(1)} %get-tuple-element.148) | copy-start | bytes 9437188
  208.2 27.5 %copy-start.55 = (f32[768]{0:T(1024)S(1)}, f32[768]{0:T(1024)}, u32[]{:S(2)}) copy-start(f32[768]{0:T(1024)} %get-tuple-element.101) | copy-start | bytes 9220
  345.3 84.5 %copy-start.1 = (f32[1024,768]{0,1:T(8,128)S(1)}, f32[1024,768]{0,1:T(8,128)}, u32[]{:S(2)}) copy-start(f32[1024,768]{0,1:T(8,128)} %copy-done) | copy-start | bytes 9437188
  345.3 84.5 %copy-start.37 = (f32[1024]{0:T(1024)S(1)}, f32[1024]{0:T(1024)}, u32[]{:S(2)}) copy-start(f32[1024]{0:T(1024)} %copy-done.36) | copy-start | bytes 12292
  345.3 84.5 %copy-start.41 = (f32[768]{0:T(1024)S(1)}, f32[768]{0:T(1024)}, u32[]{:S(2)}) copy-start(f32[768]{0:T(1024)} %copy-done.40) | copy-start | bytes 9220
  449.5 2.4 collective-permute-start.8
  540.4 4.6 collective-permute-start.9
  565.9 235.4 %reduce-scatter.6.cloned.1.call-start = ((), (), s32[]{:S(2)}) async-start(), calls=%async_computation.5 | async-start | bytes 6082560 | tf_op jit(solution)/shard_map/reduce_scatter | solution.py:294
  614.1 317.2 %reduce-scatter.8.cloned.1.call-start = ((), (), s32[]{:S(2)}) async-start(), calls=%async_computation.6 | async-start | bytes 9732096 | tf_op jit(solution)/shard_map/reduce_scatter | solution.py:294
  697.4 23.1 %copy-start.12 = (bf16[96,8,2,1152]{3,1,2,0:T(8,128)(2,1)S(1)}, bf16[96,8,2,1152]{3,1,2,0:T(8,128)(2,1)}, u32[]{:S(2)}) copy-start(bf16[96,8,2,1152]{3,1,2,0:T(8,128)(2,1)} %copy.160) | copy-start | bytes 10616836
  707.3 44.9 %collective-permute-start.6 = (bf16[1024,768]{0,1:T(8,128)(2,1)}, bf16[1024,768]{0,1:T(8,128)(2,1)}, u32[]{:S(2)}, u32[]{:S(2)}) collective-permute-start(bf16[1024,768]{0,1:T(8,128)(2,1)} %add_convert_fusion.2), channel_id=1, source_target_pairs={{0,0},{1,2},{2,1},{3,3},{4,4},{5,6},{6,5},{7,7},{8,8},{9,10},{10,9... | collective-permute-start | bytes 4718600 | tf_op jit(solution)/shard_map/ppermute | solution.py:306
  735.8 15.6 %copy-start.24 = (bf16[1500,768]{1,0:T(8,128)(2,1)S(1)}, bf16[1500,768]{1,0:T(8,128)(2,1)}, u32[]{:S(2)}) copy-start(bf16[1500,768]{1,0:T(8,128)(2,1)} %get-tuple-element.33) | copy-start | bytes 6912004
  738.0 13.9 %copy-start.17 = (bf16[1024,768]{1,0:T(8,128)(2,1)S(1)}, bf16[1024,768]{1,0:T(8,128)(2,1)}, u32[]{:S(2)}) copy-start(bf16[1024,768]{1,0:T(8,128)(2,1)} %get-tuple-element.27) | copy-start | bytes 4718596
  738.0 58.6 %collective-permute-start.10 = (bf16[1024,768]{0,1:T(8,128)(2,1)}, bf16[1024,768]{0,1:T(8,128)(2,1)}, u32[]{:S(2)}, u32[]{:S(2)}) collective-permute-start(bf16[1024,768]{0,1:T(8,128)(2,1)} %add_convert_fusion.1), channel_id=1, source_target_pairs={{0,0},{1,2},{2,1},{3,3},{4,4},{5,6},{6,5},{7,7},{8,8},{9,10},{10,9... | collective-permute-start | bytes 4718600 | tf_op jit(solution)/shard_map/ppermute | solution.py:306
  (52 other events, 213.1 us)
Sparse Core Ops, SparseCore 0:
  11.5 62.8 all-gather.5
  77.9 66.3 all-gather.7
  147.8 81.5 all-gather.9
  566.0 101.7 reduce-scatter.3
  673.3 117.4 reduce-scatter.5
  796.5 134.7 reduce-scatter.7

commit v2 on v1

v2 whole, which is shorter than its diff:
```python
import functools, jax, jax.numpy as jnp
from jax import lax
from jax.experimental import pallas as pl
from jax.experimental.pallas import tpu as pltpu
from jax.sharding import Mesh
from jax.sharding import PartitionSpec as P
BLK=256
HEAD=64
LANES=128
NEG=-1e30
LOG2E=1.4426950408889634
F32=jnp.float32; BF=jnp.bfloat16

def lane_ids(rows): return lax.broadcasted_iota(jnp.int32,(rows,LANES),1)

def nt(a,b): return lax.dot_general(a,b,(((1,),(1,)),((),())),preferred_element_type=F32)
def nn(a,b): return lax.dot_general(a,b,(((1,),(0,)),((),())),preferred_element_type=F32)
def tn(a,b): return lax.dot_general(a,b,(((0,),(0,)),((),())),preferred_element_type=F32)

def pick(head, lanes): return (lanes<64) if head==0 else (lanes>=64)

def places(core, half):
    return (core * half, (1 - core) * half)


def rows_at(base, offset, count):
    return pl.ds(pl.multiple_of(base + offset, BLK), count)


def self_fwd_kernel(core_ref,kept_ref,come_ref,segq_ref,segk_ref,own_ref,sent_ref,lse_ref,q_ref,k_ref,vx_ref,o_ref):
    half=kept_ref.shape[1]; rows=2*half; n=rows//BLK
    core=core_ref[0]
    for ref,base in zip((kept_ref,come_ref),places(core,half)):
        at=rows_at(base,0,half)
        q_ref[at,:]=ref[0]
        k_ref[at,:]=ref[1]
        vx_ref[at,:LANES]=ref[2]
    vx_ref[:,LANES:]=jnp.ones((rows,LANES),BF)
    lanes=lane_ids(BLK)
    for i in range(n):
        r0=i*BLK; kn=r0+BLK
        q=q_ref[r0:kn,:]
        outs=[];lses=[]
        for h in range(2):
            qm=jnp.where(pick(h,lanes),q,jnp.zeros_like(q))
            s=nt(qm,k_ref[:kn,:])
            cut = half if i>=n//2 else r0
            a=s[:,:cut] if cut>0 else None
            b=s[:,cut:]
            w=kn-cut
            qi=lax.broadcasted_iota(jnp.int32,(BLK,w),0)+(r0-cut)
            kj=lax.broadcasted_iota(jnp.int32,(BLK,w),1)
            ok=kj<=qi
            if i>=n//2:
                ok=ok&(segk_ref[:,:kn-half]==segq_ref[r0-half:kn-half,:])
            b=jnp.where(ok,b,NEG)
            m=jnp.max(b,-1,keepdims=True)
            if a is not None: m=jnp.maximum(m,jnp.max(a,-1,keepdims=True))
            pb=jnp.exp2(b-m).astype(BF)
            ox=nn(pb,vx_ref[cut:kn,:])
            if a is not None:
                pa=jnp.exp2(a-m).astype(BF)
                ox=ox+nn(pa,vx_ref[:cut,:])
            l=ox[:,LANES:]
            outs.append(ox[:,:LANES]/l); lses.append(m+jnp.log2(l))
        sel=lanes<64
        o_ref[r0:kn,:]=jnp.where(sel,outs[0],outs[1]).astype(BF)
        lse_ref[r0:kn,:]=jnp.where(sel,lses[0],lses[1])
    for ref,base in zip((own_ref,sent_ref),places(core,half)):
        ref[...]=o_ref[rows_at(base,0,half),:]


def scalar():
    return pl.BlockSpec(memory_space=pltpu.SMEM)


def pair_cost(pairs,passes,nbytes):
    return pl.CostEstimate(flops=int(pairs*passes*512),bytes_accessed=int(nbytes),transcendentals=int(pairs))


def self_fwd(core,kept,come,segq,segk):
    half,part=kept.shape[1:]; rows=2*half
    three=pl.BlockSpec((3,half,LANES),lambda p:(0,0,p))
    one=pl.BlockSpec((half,LANES),lambda p:(0,p))
    n=rows//BLK
    return pl.pallas_call(self_fwd_kernel,
        grid=(part//LANES,),
        in_specs=[scalar(),three,three,pl.BlockSpec(segq.shape,lambda p:(0,0)),pl.BlockSpec(segk.shape,lambda p:(0,0))],
        out_specs=[one,one,pl.BlockSpec((rows,LANES),lambda p:(0,p))],
        out_shape=[jax.ShapeDtypeStruct((half,part),BF),jax.ShapeDtypeStruct((half,part),BF),jax.ShapeDtypeStruct((rows,part),F32)],
        scratch_shapes=[pltpu.VMEM((rows,LANES),BF),pltpu.VMEM((rows,LANES),BF),pltpu.VMEM((rows,2*LANES),BF),pltpu.VMEM((rows,LANES),BF)],
        compiler_params=pltpu.CompilerParams(vmem_limit_bytes=60*2**20),
        cost_estimate=pair_cost(n*(n+1)//2*BLK*BLK*(part//HEAD),2,12*rows*part),
        name="self_fwd",
    )(core,kept,come,segq,segk)

def cross_fwd_kernel(frames,q_ref,k_ref,v_ref,o_ref,lse_ref,kx_ref,vx_ref):
    rows=q_ref.shape[0]; n=rows//BLK; kp=k_ref.shape[0]
    tail=frames//BLK*BLK
    kx_ref[...]=k_ref[...]
    vx_ref[:,:LANES]=v_ref[...]
    vx_ref[:,LANES:]=jnp.ones((kp,LANES),BF)
    if frames<kp:
        keep=lax.broadcasted_iota(jnp.int32,(kp-tail,LANES),0)+tail<frames
        kx_ref[tail:,:]=jnp.where(keep,k_ref[tail:,:],jnp.zeros((),BF))
        vx_ref[tail:,:LANES]=jnp.where(keep,v_ref[tail:,:],jnp.zeros((),BF))
    lanes=lane_ids(BLK)
    for i in range(n):
        r0=i*BLK
        q=q_ref[r0:r0+BLK,:]
        outs=[];lses=[]
        for h in range(2):
            qm=jnp.where(pick(h,lanes),q,jnp.zeros_like(q))
            s=nt(qm,kx_ref[...])
            if frames<kp:
                kj=lax.broadcasted_iota(jnp.int32,(BLK,kp-tail),1)+tail
                s=jnp.concatenate([s[:,:tail],jnp.where(kj<frames,s[:,tail:],NEG)],axis=1)
            m=jnp.max(s,-1,keepdims=True)
            p=jnp.exp2(s-m).astype(BF)
            ox=nn(p,vx_ref[...])
            l=ox[:,LANES:]
            outs.append(ox[:,:LANES]/l); lses.append(m+jnp.log2(l))
        sel=lanes<64
        o_ref[r0:r0+BLK,:]=jnp.where(sel,outs[0],outs[1]).astype(BF)
        lse_ref[r0:r0+BLK,:]=jnp.where(sel,lses[0],lses[1])

def cross_fwd(q,kv,frames,heads):
    rows=q.shape[0]; npair=heads//2; kp=kv.shape[0]
    return pl.pallas_call(functools.partial(cross_fwd_kernel,frames),
        grid=(npair,),
        in_specs=[pl.BlockSpec((rows,LANES),lambda p:(0,p)),
                  pl.BlockSpec((kp,LANES),lambda p:(0,p)),
                  pl.BlockSpec((kp,LANES),lambda p:(0,npair+p))],
        out_specs=[pl.BlockSpec((rows,LANES),lambda p:(0,p)),pl.BlockSpec((rows,LANES),lambda p:(0,p))],
        out_shape=[jax.ShapeDtypeStruct((rows,heads*64),BF),jax.ShapeDtypeStruct((rows,heads*64),F32)],
        scratch_shapes=[pltpu.VMEM((kp,LANES),BF),pltpu.VMEM((kp,2*LANES),BF)],
        compiler_params=pltpu.CompilerParams(vmem_limit_bytes=60*2**20),
        cost_estimate=pair_cost(rows*kp*heads,2,8*rows*heads*64+4*kp*heads*64),
        name="cross_fwd",
    )(q,kv,kv)

def split3(x):
    hi=x.astype(BF); r=x-hi.astype(F32); mid=r.astype(BF); lo=(r-mid.astype(F32)).astype(BF)
    return hi,mid,lo

def aug(value,head,lanes,one_lane):
    hi,mid,lo=split3(-value)
    z=jnp.zeros(lanes.shape,F32)
    b=64*head
    x=jnp.where(lanes==b,hi.astype(F32),jnp.where(lanes==b+1,mid.astype(F32),jnp.where(lanes==b+2,lo.astype(F32),z)))
    if one_lane: x=jnp.where(lanes==b+3,1.0,x)
    return x.astype(BF)

def build_q(q,do,o,lse,at,qx_ref,dox_ref,masked):
    lanes=lane_ids(BLK)
    prod=do.astype(F32)*o.astype(F32)
    for h in range(2):
        sel=pick(h,lanes)
        delta=jnp.sum(jnp.where(sel,prod,0.0),-1,keepdims=True)
        qx_ref[h,at,:LANES]=jnp.where(sel,q,jnp.zeros((),BF))
        qx_ref[h,at,LANES:]=aug(lse,h,lanes,masked)
        dox_ref[h,at,:LANES]=jnp.where(sel,do,jnp.zeros((),BF))
        dox_ref[h,at,LANES:]=aug(delta,h,lanes,False)

def build_k(k,v,r0,at,kx_ref,km_ref,vx_ref,frames):
    lanes=lane_ids(BLK)
    low=lanes%64
    ones=jnp.where(low<3,1.0,0.0)
    kones=ones
    if frames is not None and r0+BLK>frames:
        bad=lax.broadcasted_iota(jnp.int32,(BLK,LANES),0)+r0>=frames
        k=jnp.where(bad,jnp.zeros((),BF),k); v=jnp.where(bad,jnp.zeros((),BF),v)
        kones=jnp.where(bad&(low==3),NEG,ones)
    kx_ref[at,:LANES]=k; kx_ref[at,LANES:]=kones.astype(BF)
    vx_ref[at,:LANES]=v; vx_ref[at,LANES:]=ones.astype(BF)
    for h in range(2): km_ref[h,at,:]=jnp.where(pick(h,lanes),k,jnp.zeros((),BF))

def block_back(kx,vx,km,qx,dox,mask):
    s=nt(kx,qx)
    if mask is not None: s=jnp.where(mask,s,NEG)
    p=jnp.exp2(s)
    dp=nt(vx,dox)
    ds=(p*dp).astype(BF)
    pb=p.astype(BF)
    dv=nn(pb,dox[:,:LANES])
    dk=nn(ds,qx[:,:LANES])
    dq=tn(ds,km)
    return dv,dk,dq

def self_bwd_kernel(core_ref,kept_ref,come_ref,do_ref,do_come_ref,o_ref,o_sent_ref,lse_ref,segq_ref,segk_ref,own_ref,sent_ref,
                    qx_ref,dox_ref,kx_ref,km_ref,vx_ref,dqa_ref,dk_ref,dv_ref,dka_ref,dva_ref):
    half=kept_ref.shape[1]; rows=2*half; n=rows//BLK
    core=core_ref[0]
    for ref,d,o,base in zip((kept_ref,come_ref),(do_ref,do_come_ref),(o_ref,o_sent_ref),places(core,half)):
        for r0 in range(0,half,BLK):
            here=slice(r0,r0+BLK); at=rows_at(base,r0,BLK)
            build_q(ref[0,here,:],d[here,:],o[here,:],lse_ref[at,:],at,qx_ref,dox_ref,False)
            build_k(ref[1,here,:],ref[2,here,:],0,at,kx_ref,km_ref,vx_ref,None)
    dqa_ref[...]=jnp.zeros_like(dqa_ref)
    tri=lax.broadcasted_iota(jnp.int32,(BLK,BLK),0)<=lax.broadcasted_iota(jnp.int32,(BLK,BLK),1)
    def pair(j,i,mask,first):
        kr=pl.ds(pl.multiple_of(j*BLK,BLK),BLK); qr=pl.ds(pl.multiple_of(i*BLK,BLK),BLK)
        r=[block_back(kx_ref[kr,:],vx_ref[kr,:],km_ref[h,kr,:],qx_ref[h,qr,:],dox_ref[h,qr,:],mask) for h in range(2)]
        dv=r[0][0]+r[1][0]; dk=r[0][1]+r[1][1]; dq=r[0][2]+r[1][2]
        if first: dva_ref[...]=dv; dka_ref[...]=dk
        else: dva_ref[...]+=dv; dka_ref[...]+=dk
        dqa_ref[qr,:]+=dq
    def flush(j):
        kr=pl.ds(pl.multiple_of(j*BLK,BLK),BLK)
        dk_ref[kr,:]=(dka_ref[...]*(1/LOG2E)).astype(BF)
        dv_ref[kr,:]=dva_ref[...].astype(BF)
    def outer_prompt(j,_):
        pair(j,j,tri,True)
        def inner(i,_): pair(j,i,None,False); return 0
        lax.fori_loop(j+1,n,inner,0)
        flush(j); return 0
    lax.fori_loop(0,n//2,outer_prompt,0)
    def segmask(j,i):
        sk=segk_ref[pl.ds(pl.multiple_of(j*BLK-half,BLK),BLK),:]
        sq=segq_ref[i-n//2]
        return sk==sq
    def outer_cont(j,_):
        pair(j,j,tri&segmask(j,j),True)
        def inner(i,_): pair(j,i,segmask(j,i),False); return 0
        lax.fori_loop(j+1,n,inner,0)
        flush(j); return 0
    lax.fori_loop(n//2,n,outer_cont,0)
    for ref,base in zip((own_ref,sent_ref),places(core,half)):
        at=rows_at(base,0,half)
        ref[0]=(dqa_ref[at,:]*0.125).astype(BF)
        ref[1]=dk_ref[at,:]
        ref[2]=dv_ref[at,:]

def self_bwd(core,kept,come,do,do_come,o,o_sent,lse,segq,segk):
    half,part=kept.shape[1:]; rows=2*half
    three=pl.BlockSpec((3,half,LANES),lambda p:(0,0,p))
    one=pl.BlockSpec((half,LANES),lambda p:(0,p))
    out=jax.ShapeDtypeStruct((3,half,part),BF)
    n=rows//BLK
    return pl.pallas_call(self_bwd_kernel,
        grid=(part//LANES,),
        in_specs=[scalar(),three,three,one,one,one,one,pl.BlockSpec((rows,LANES),lambda p:(0,p)),
                  pl.BlockSpec(segq.shape,lambda p:(0,0,0)),pl.BlockSpec(segk.shape,lambda p:(0,0))],
        out_specs=[three,three],
        out_shape=[out,out],
        scratch_shapes=[pltpu.VMEM((2,rows,2*LANES),BF),pltpu.VMEM((2,rows,2*LANES),BF),pltpu.VMEM((rows,2*LANES),BF),
                        pltpu.VMEM((2,rows,LANES),BF),pltpu.VMEM((rows,2*LANES),BF),pltpu.VMEM((rows,LANES),F32),
                        pltpu.VMEM((rows,LANES),BF),pltpu.VMEM((rows,LANES),BF),
                        pltpu.VMEM((BLK,LANES),F32),pltpu.VMEM((BLK,LANES),F32)],
        compiler_params=pltpu.CompilerParams(vmem_limit_bytes=60*2**20),
        cost_estimate=pair_cost(n*(n+1)//2*BLK*BLK*(part//HEAD),5,20*rows*part),
        name="self_bwd",
    )(core,kept,come,do,do_come,o,o_sent,lse,segq,segk)

def cross_bwd_kernel(frames,q_ref,k_ref,v_ref,do_ref,o_ref,lse_ref,dq_ref,dk_ref,dv_ref,
                     qx_ref,dox_ref,kx_ref,km_ref,vx_ref,dqa_ref,dka_ref,dva_ref):
    rows=q_ref.shape[0]; n=rows//BLK; kp=k_ref.shape[0]; nk=kp//BLK
    for r0 in range(0,rows,BLK):
        at=slice(r0,r0+BLK)
        build_q(q_ref[at,:],do_ref[at,:],o_ref[at,:],lse_ref[at,:],at,qx_ref,dox_ref,True)
    for r0 in range(0,kp,BLK):
        at=slice(r0,r0+BLK)
        build_k(k_ref[at,:],v_ref[at,:],r0,at,kx_ref,km_ref,vx_ref,frames)
    dqa_ref[...]=jnp.zeros_like(dqa_ref)
    def outer(j,_):
        kr=pl.ds(pl.multiple_of(j*BLK,BLK),BLK)
        dva=None
        for i in range(n):
            qr=slice(i*BLK,(i+1)*BLK)
            r=[block_back(kx_ref[kr,:],vx_ref[kr,:],km_ref[h,kr,:],qx_ref[h,qr,:],dox_ref[h,qr,:],None) for h in range(2)]
            dv=r[0][0]+r[1][0]; dk=r[0][1]+r[1][1]; dq=r[0][2]+r[1][2]
            if i==0: dva_ref[...]=dv; dka_ref[...]=dk
            else: dva_ref[...]+=dv; dka_ref[...]+=dk
            dqa_ref[qr,:]+=dq
        dk_ref[kr,:]=(dka_ref[...]*(1/LOG2E)).astype(BF)
        dv_ref[kr,:]=dva_ref[...].astype(BF)
        return 0
    lax.fori_loop(0,nk,outer,0)
    dq_ref[...]=(dqa_ref[...]*0.125).astype(BF)

def cross_bwd(q,kv,frames,do,o,lse,heads):
    rows=q.shape[0]; npair=heads//2; kp=kv.shape[0]
    big=lambda f:pl.BlockSpec((rows,LANES),f)
    kb=lambda f:pl.BlockSpec((kp,LANES),f)
    return pl.pallas_call(functools.partial(cross_bwd_kernel,frames),
        grid=(npair,),
        in_specs=[big(lambda p:(0,p)),kb(lambda p:(0,p)),kb(lambda p:(0,npair+p)),big(lambda p:(0,p)),big(lambda p:(0,p)),big(lambda p:(0,p))],
        out_specs=[big(lambda p:(0,p)),kb(lambda p:(0,p)),kb(lambda p:(0,p))],
        out_shape=[jax.ShapeDtypeStruct((rows,heads*64),BF),jax.ShapeDtypeStruct((kp,heads*64),BF),jax.ShapeDtypeStruct((kp,heads*64),BF)],
        scratch_shapes=[pltpu.VMEM((2,rows,2*LANES),BF),pltpu.VMEM((2,rows,2*LANES),BF),pltpu.VMEM((kp,2*LANES),BF),
                        pltpu.VMEM((2,kp,LANES),BF),pltpu.VMEM((kp,2*LANES),BF),pltpu.VMEM((rows,LANES),F32),
                        pltpu.VMEM((BLK,LANES),F32),pltpu.VMEM((BLK,LANES),F32)],
        compiler_params=pltpu.CompilerParams(vmem_limit_bytes=60*2**20),
        cost_estimate=pair_cost(rows*kp*heads,5,12*rows*heads*64+8*kp*heads*64),
        name="cross_bwd",
    )(q,kv,kv,do,o,lse)


EPSILON = 1e-05
ROWS = 256
BIG = 60 * 2**20


def whole(shape):
    return pl.BlockSpec(shape, lambda *_: (0,) * len(shape), pipeline_mode=pl.Buffered(1))


def by_rows(*lead_and_cols):
    *lead, cols = lead_and_cols
    return pl.BlockSpec((*lead, ROWS, cols), lambda i: (0,) * len(lead) + (i, 0))


def shaped(shape, dtype):
    return jax.ShapeDtypeStruct(shape, dtype)


def cost(flops, nbytes, trans=0):
    return pl.CostEstimate(flops=int(flops), bytes_accessed=int(nbytes), transcendentals=int(trans))


def normalize(values):
    centre = values - jnp.mean(values, -1, keepdims=True)
    scale = lax.rsqrt(jnp.mean(centre * centre, -1, keepdims=True) + EPSILON)
    return centre * scale, scale


def norm_grad(normed, scale, gain, grad):
    weighted = grad * gain
    return scale * (weighted - jnp.mean(weighted, -1, keepdims=True)
                    - normed * jnp.mean(weighted * normed, -1, keepdims=True))


def accumulate(ref, value):
    @pl.when(pl.program_id(0) == 0)
    def _():
        ref[...] = value

    @pl.when(pl.program_id(0) > 0)
    def _():
        ref[...] += value


def column_sum(values):
    return jnp.sum(values, 0, keepdims=True)


def qkv_kernel(core_ref, x_ref, w_ref, gain_ref, shift_ref, bias_ref, norm_ref, kept_ref, sent_ref):
    part = kept_ref.shape[2]
    normed, _ = normalize(x_ref[...].astype(F32))
    low = (normed * gain_ref[0:1] + shift_ref[0:1]).astype(BF)
    norm_ref[...] = low
    core = core_ref[0]
    for out_ref, at in ((kept_ref, core), (sent_ref, 1 - core)):
        cols = nn(low, w_ref[at])
        out_ref[0] = ((cols[:, :part] + bias_ref[at, 0:1]) * (HEAD ** -0.5 * LOG2E)).astype(BF)
        out_ref[1] = cols[:, part:2 * part].astype(BF)
        out_ref[2] = (cols[:, 2 * part:] + bias_ref[at, 1:2]).astype(BF)


def qkv_project(core, x, w, gain, shift, bias):
    rows, width = x.shape
    part = width // 2
    out = shaped((3, rows, part), BF)
    return pl.pallas_call(
        qkv_kernel, grid=(rows // ROWS,),
        in_specs=[scalar(), by_rows(width), whole(w.shape), whole(gain.shape), whole(shift.shape), whole(bias.shape)],
        out_specs=[by_rows(width), by_rows(3, part), by_rows(3, part)],
        out_shape=[shaped((rows, width), BF), out, out],
        compiler_params=pltpu.CompilerParams(vmem_limit_bytes=BIG),
        cost_estimate=cost(6 * rows * width * width, 2 * (3 * width * width + 6 * rows * width)), name="qkv_project",
    )(core, x, w, gain, shift, bias)


def memory_kernel(frames, mine_ref, own_ref, come_ref, w_ref, bias_ref, kv_ref, mem_ref):
    width = own_ref.shape[1]
    part = width // 2
    mem = jnp.where(mine_ref[0] == 1, own_ref[...], come_ref[...])
    row = lax.broadcasted_iota(jnp.int32, mem.shape, 0) + pl.program_id(0) * ROWS
    mem = jnp.where(row < frames, mem, jnp.zeros((), BF))
    mem_ref[...] = mem
    for t in range(2):
        cols = nn(mem, w_ref[t])
        kv_ref[:, t * part:(t + 1) * part] = cols[:, :part].astype(BF)
        kv_ref[:, width + t * part:width + (t + 1) * part] = (cols[:, part:] + bias_ref[4:5, t * part:(t + 1) * part]).astype(BF)


def memory_project(mine, own, come, w_mid, bias):
    frames, width = own.shape
    steps = pl.cdiv(frames, ROWS)
    return pl.pallas_call(
        functools.partial(memory_kernel, frames), grid=(steps,),
        in_specs=[scalar(), by_rows(width), by_rows(width),
                  pl.BlockSpec((2, width, width), lambda i: (0, 0, 1), pipeline_mode=pl.Buffered(1)), whole(bias.shape)],
        out_specs=[by_rows(2 * width), by_rows(width)],
        out_shape=[shaped((steps * ROWS, 2 * width), BF), shaped((steps * ROWS, width), BF)],
        compiler_params=pltpu.CompilerParams(vmem_limit_bytes=BIG),
        cost_estimate=cost(4 * frames * width * width, 2 * (2 * width * width + 5 * frames * width)), name="memory_project",
    )(mine, own, come, w_mid, bias)


def middle_kernel(core_ref, x_ref, own_ref, come_ref, wo_ref, wq_ref, gain_ref, shift_ref, bias_ref,
                  resid_ref, norm_ref, q_ref):
    part = own_ref.shape[1]
    core = core_ref[0]
    resid = x_ref[...].astype(F32) + nt(own_ref[...], wo_ref[core]) + nt(come_ref[...], wo_ref[1 - core]) + bias_ref[2:3]
    resid_ref[...] = resid
    normed, _ = normalize(resid)
    low = (normed * gain_ref[1:2] + shift_ref[1:2]).astype(BF)
    norm_ref[...] = low
    for t in range(2):
        at = slice(t * part, (t + 1) * part)
        q_ref[:, at] = ((nn(low, wq_ref[t]) + bias_ref[3:4, at]) * (HEAD ** -0.5 * LOG2E)).astype(BF)


def middle(core, x, own, come, w_mid, gain, shift, bias):
    rows, width = x.shape
    part = width // 2
    w_at = lambda c: pl.BlockSpec((2, width, part), lambda i: (0, 0, c), pipeline_mode=pl.Buffered(1))
    return pl.pallas_call(
        middle_kernel, grid=(rows // ROWS,),
        in_specs=[scalar(), by_rows(width), by_rows(part), by_rows(part), w_at(0), w_at(1),
                  whole(gain.shape), whole(shift.shape), whole(bias.shape)],
        out_specs=[by_rows(width)] * 3,
        out_shape=[shaped((rows, width), F32), shaped((rows, width), BF), shaped((rows, width), BF)],
        compiler_params=pltpu.CompilerParams(vmem_limit_bytes=BIG),
        cost_estimate=cost(4 * rows * width * width, 4 * width * width + 12 * rows * width), name="middle",
    )(core, x, own, come, w_mid, w_mid, gain, shift, bias)


def gelu_parts(v):
    z = jnp.abs(v) * (0.5 ** 0.5)
    t = 1.0 / (1.0 + 0.3275911 * z)
    bell = jnp.exp2(v * v * (-0.5 * LOG2E))
    poly = ((((1.061405429 * t - 1.453152027) * t + 1.421413741) * t - 0.284496736) * t + 0.254829592) * t
    tail = (0.5 * poly) * bell
    phi = jnp.where(v >= 0, 1.0 - tail, tail)
    return phi, phi + v * bell * 0.3989422804014327


def feed_kernel(attn_ref, resid_ref, g_ref, wo_ref, wi_ref, wm_ref, gain_ref, shift_ref, bias_ref, unit_bias_ref, out_bias_ref,
                out_ref, norm_ref, hidden_ref, dpre_ref, g2_ref, dattn_ref,
                sum_g_ref, sum_dpre_ref, sum_g2_ref, sum_gain_ref, sum_shift_ref):
    part = wo_ref.shape[2]
    units = wi_ref.shape[2]
    resid = resid_ref[...] + bias_ref[5:6]
    for t in range(2):
        resid = resid + nt(attn_ref[:, t * part:(t + 1) * part], wo_ref[t])
    normed, scale = normalize(resid)
    low = (normed * gain_ref[2:3] + shift_ref[2:3]).astype(BF)
    norm_ref[...] = low
    g_low = g_ref[...]
    out = resid + out_bias_ref[...]
    back = jnp.zeros_like(resid)
    sums = []
    for t in range(2):
        at = slice(t * units, (t + 1) * units)
        pre = nn(low, wi_ref[t]) + unit_bias_ref[:, at]
        phi, slope = gelu_parts(pre)
        hidden = (pre * phi).astype(BF)
        hidden_ref[:, at] = hidden
        out = out + nt(hidden, wm_ref[t])
        dpre = nn(g_low, wm_ref[t]) * slope
        sums.append(column_sum(dpre))
        dpre = dpre.astype(BF)
        dpre_ref[:, at] = dpre
        back = back + nt(dpre, wi_ref[t])
    out_ref[...] = out.astype(BF)
    accumulate(sum_dpre_ref, jnp.concatenate(sums, 1))
    g = g_low.astype(F32)
    accumulate(sum_g_ref, column_sum(g))
    accumulate(sum_gain_ref, column_sum(back * normed))
    accumulate(sum_shift_ref, column_sum(back))
    g2 = g + norm_grad(normed, scale, gain_ref[2:3], back)
    accumulate(sum_g2_ref, column_sum(g2))
    g2_ref[...] = g2
    g2_low = g2.astype(BF)
    for t in range(2):
        dattn_ref[:, t * part:(t + 1) * part] = nn(g2_low, wo_ref[t]).astype(BF)


def feed(attn, resid, g, w_mid, w_ff, gain, shift, bias, unit_bias, out_bias):
    rows, width = resid.shape
    part = width // 2
    units = w_ff.shape[2] // 2
    w_at = lambda cols, c: pl.BlockSpec((2, width, cols), lambda i: (0, 0, c), pipeline_mode=pl.Buffered(1))
    line = lambda cols: (pl.BlockSpec((1, cols), lambda i: (0, 0)), shaped((1, cols), F32))
    lines = [line(width), line(2 * units), line(width), line(width), line(width)]
    return pl.pallas_call(
        feed_kernel, grid=(rows // ROWS,),
        in_specs=[by_rows(width), by_rows(width), by_rows(width), w_at(part, 4), w_at(units, 0), w_at(units, 1),
                  whole(gain.shape), whole(shift.shape), whole(bias.shape), whole(unit_bias.shape), whole(out_bias.shape)],
        out_specs=[by_rows(width), by_rows(width), by_rows(2 * units), by_rows(2 * units), by_rows(width), by_rows(width)] + [a for a, _ in lines],
        out_shape=[shaped((rows, width), BF), shaped((rows, width), BF), shaped((rows, 2 * units), BF), shaped((rows, 2 * units), BF),
                   shaped((rows, width), F32), shaped((rows, width), BF)] + [b for _, b in lines],
        compiler_params=pltpu.CompilerParams(vmem_limit_bytes=BIG),
        cost_estimate=cost(2 * rows * width * (2 * width + 8 * units), 2 * width * (width + 4 * units) + 2 * rows * (8 * width + 4 * units), 4 * rows * units),
        name="feed",
    )(attn, resid, g, w_mid, w_ff, w_ff, gain, shift, bias, unit_bias, out_bias)


def feed_weights_kernel(norm_ref, g_ref, dpre_ref, hidden_ref, out_ref):
    cols = dpre_ref.shape[1]
    out_ref[0, :, :cols] = tn(norm_ref[...], dpre_ref[...]).astype(BF)
    out_ref[0, :, cols:] = tn(g_ref[...], hidden_ref[...]).astype(BF)


def feed_weights(norm, g, dpre, hidden):
    rows, width = norm.shape
    units = dpre.shape[1] // 2
    cols = units // 2
    return pl.pallas_call(
        feed_weights_kernel, grid=(2, 2),
        in_specs=[whole(norm.shape), whole(g.shape), pl.BlockSpec((rows, cols), lambda t, c: (0, 2 * t + c)),
                  pl.BlockSpec((rows, cols), lambda t, c: (0, 2 * t + c))],
        out_specs=pl.BlockSpec((1, width, 2 * cols), lambda t, c: (t, 0, c)),
        out_shape=shaped((2, width, 2 * units), BF),
        compiler_params=pltpu.CompilerParams(vmem_limit_bytes=BIG),
        cost_estimate=cost(8 * rows * width * units, 2 * (4 * width * units + 4 * rows * units)), name="feed_weights",
    )(norm, g, dpre, hidden)


def middle_back_kernel(core_ref, dq_ref, resid_ref, g2_ref, wq_ref, wo_ref, gain_ref,
                       g1_ref, kept_ref, sent_ref, sum_dq_ref, sum_g1_ref, sum_gain_ref, sum_shift_ref):
    part = kept_ref.shape[1]
    core = core_ref[0]
    dq = dq_ref[...]
    back = nt(dq[:, :part], wq_ref[0]) + nt(dq[:, part:], wq_ref[1])
    accumulate(sum_dq_ref, column_sum(dq.astype(F32)))
    normed, scale = normalize(resid_ref[...])
    accumulate(sum_gain_ref, column_sum(back * normed))
    accumulate(sum_shift_ref, column_sum(back))
    g1 = g2_ref[...] + norm_grad(normed, scale, gain_ref[1:2], back)
    g1_ref[...] = g1
    accumulate(sum_g1_ref, column_sum(g1))
    low = g1.astype(BF)
    kept_ref[...] = nn(low, wo_ref[core]).astype(BF)
    sent_ref[...] = nn(low, wo_ref[1 - core]).astype(BF)


def middle_back(core, dq, resid, g2, w_mid, gain):
    rows, width = resid.shape
    part = width // 2
    w_at = lambda c: pl.BlockSpec((2, width, part), lambda i: (0, 0, c), pipeline_mode=pl.Buffered(1))
    line = pl.BlockSpec((1, width), lambda i: (0, 0))
    return pl.pallas_call(
        middle_back_kernel, grid=(rows // ROWS,),
        in_specs=[scalar(), by_rows(width), by_rows(width), by_rows(width), w_at(1), w_at(0), whole(gain.shape)],
        out_specs=[by_rows(width), by_rows(part), by_rows(part)] + [line] * 4,
        out_shape=[shaped((rows, width), F32), shaped((rows, part), BF), shaped((rows, part), BF)] + [shaped((1, width), F32)] * 4,
        compiler_params=pltpu.CompilerParams(vmem_limit_bytes=BIG),
        cost_estimate=cost(4 * rows * width * width, 4 * width * width + 18 * rows * width), name="middle_back",
    )(core, dq, resid, g2, w_mid, w_mid, gain)


def middle_weights_kernel(core_ref, g1_ref, own_ref, come_ref, norm_ref, dq_ref, mem_ref, dk_ref, dv_ref, g2_ref, attn_ref,
                          out_ref, sum_dv_ref):
    part = own_ref.shape[1]
    attn_self = jnp.where(pl.program_id(0) == core_ref[0], own_ref[...], come_ref[...])
    out_ref[0, :, :part] = tn(g1_ref[...].astype(BF), attn_self).astype(BF)
    out_ref[0, :, part:2 * part] = tn(norm_ref[...], dq_ref[...]).astype(BF)
    mem = mem_ref[...]
    out_ref[0, :, 2 * part:3 * part] = tn(mem, dk_ref[...]).astype(BF)
    out_ref[0, :, 3 * part:4 * part] = tn(mem, dv_ref[...]).astype(BF)
    out_ref[0, :, 4 * part:] = tn(g2_ref[...].astype(BF), attn_ref[...]).astype(BF)
    sum_dv_ref[...] = column_sum(dv_ref[...].astype(F32))


def middle_weights(core, g1, own, come, norm, dq, mem, dk, dv, g2, attn):
    rows, width = norm.shape
    frames = mem.shape[0]
    part = width // 2
    half = lambda n: pl.BlockSpec((n, part), lambda t: (0, t))
    return pl.pallas_call(
        middle_weights_kernel, grid=(2,),
        in_specs=[scalar(), whole(g1.shape), whole(own.shape), whole(come.shape), whole(norm.shape), half(rows), whole(mem.shape),
                  half(frames), half(frames), whole(g2.shape), half(rows)],
        out_specs=[pl.BlockSpec((1, width, 5 * part), lambda t: (t, 0, 0)), pl.BlockSpec((1, part), lambda t: (0, t))],
        out_shape=[shaped((2, width, 5 * part), BF), shaped((1, width), F32)],
        compiler_params=pltpu.CompilerParams(vmem_limit_bytes=BIG),
        cost_estimate=cost(2 * width * width * (3 * rows + 2 * frames), 10 * width * width + 2 * width * (10 * rows + 3 * frames)),
        name="middle_weights",
    )(core, g1, own, come, norm, dq, mem, dk, dv, g2, attn)


def qkv_back_kernel(core_ref, own_ref, come_ref, x_ref, g1_ref, w_ref, gain_ref, grad_ref, sum_gain_ref, sum_shift_ref):
    part = own_ref.shape[2]
    core = core_ref[0]
    back = jnp.zeros(x_ref.shape, F32)
    for ref, at in ((own_ref, core), (come_ref, 1 - core)):
        for j in range(3):
            back = back + nt(ref[j], w_ref[at, :, j * part:(j + 1) * part])
    normed, scale = normalize(x_ref[...].astype(F32))
    accumulate(sum_gain_ref, column_sum(back * normed))
    accumulate(sum_shift_ref, column_sum(back))
    grad_ref[...] = (g1_ref[...] + norm_grad(normed, scale, gain_ref[0:1], back)).astype(BF)


def qkv_back(core, own, come, x, g1, w, gain):
    rows, width = x.shape
    part = width // 2
    line = pl.BlockSpec((1, width), lambda i: (0, 0))
    return pl.pallas_call(
        qkv_back_kernel, grid=(rows // ROWS,),
        in_specs=[scalar(), by_rows(3, part), by_rows(3, part), by_rows(width), by_rows(width), whole(w.shape), whole(gain.shape)],
        out_specs=[by_rows(width), line, line],
        out_shape=[shaped((rows, width), BF), shaped((1, width), F32), shaped((1, width), F32)],
        compiler_params=pltpu.CompilerParams(vmem_limit_bytes=BIG),
        cost_estimate=cost(6 * rows * width * width, 2 * (3 * width * width + 7 * rows * width)), name="qkv_back",
    )(core, own, come, x, g1, w, gain)


def qkv_weights_kernel(core_ref, norm_ref, own_ref, come_ref, out_ref, sum_ref):
    part = own_ref.shape[2]
    mine = pl.program_id(0) == core_ref[0]
    norm = norm_ref[...]
    for j in range(3):
        grad = jnp.where(mine, own_ref[j], come_ref[j])
        out_ref[0, :, j * part:(j + 1) * part] = tn(norm, grad).astype(BF)
        sum_ref[0, :, j * part:(j + 1) * part] = column_sum(grad.astype(F32))


def qkv_weights(core, norm, own, come):
    rows, width = norm.shape
    part = width // 2
    return pl.pallas_call(
        qkv_weights_kernel, grid=(2,),
        in_specs=[scalar(), whole(norm.shape), whole(own.shape), whole(come.shape)],
        out_specs=[pl.BlockSpec((1, width, 3 * part), lambda t: (t, 0, 0)), pl.BlockSpec((1, 1, 3 * part), lambda t: (t, 0, 0))],
        out_shape=[shaped((2, width, 3 * part), BF), shaped((2, 1, 3 * part), F32)],
        compiler_params=pltpu.CompilerParams(vmem_limit_bytes=BIG),
        cost_estimate=cost(6 * rows * width * width, 2 * (3 * width * width + 4 * rows * width)), name="qkv_weights",
    )(core, norm, own, come)


ALL = ("tensor", "chip", "core")


def fetch(shard):
    full = lax.all_gather(shard, ALL, axis=0, tiled=True)
    return full.reshape(2, -1, shard.shape[1])


def spread_sum(grad):
    return lax.psum_scatter(grad.reshape(-1, grad.shape[2]), ALL, scatter_dimension=0, tiled=True).astype(F32)


def on_device(tokens, memory, seg_ids, positions, grad_output, attn_in, attn_out, cross_q, cross_kv,
              cross_out, mlp_in, mlp_out, norm_gain, norm_bias, proj_bias, mlp_bias, out_bias):
    width = tokens.shape[1]
    rows_here, _, part = attn_in.shape
    units = mlp_in.shape[1]
    heads = width // HEAD
    frames = memory.shape[1]
    core = lax.axis_index("core")
    tensor = lax.axis_index("tensor")
    core_at = core.astype(jnp.int32).reshape(1)
    swap = [(0, 0), (1, 2), (2, 1), (3, 3)]
    fix = lambda x: lax.ppermute(x, ("core", "tensor"), swap)
    other = lambda x: lax.ppermute(x, "core", [(0, 1), (1, 0)])

    w_qkv = fetch(attn_in.reshape(rows_here, 3 * part))
    moved = fix(tokens)
    w_mid = fetch(jnp.concatenate([attn_out.T, cross_q, cross_kv.reshape(rows_here, 2 * part), cross_out.T], 1))
    w_ff = fetch(jnp.concatenate([mlp_in, mlp_out.T], 1))
    grad_in = fix(grad_output)
    seg_mine = fix(seg_ids)
    seg_cont = jnp.where(core == 1, seg_mine, other(seg_mine))
    mem_come = other(memory[0])
    bias_halves = proj_bias[:2].reshape(2, 2, part).transpose(1, 0, 2)

    norm_one, kept, sent = qkv_project(core_at, moved, w_qkv, norm_gain, norm_bias, bias_halves)
    come = other(sent)
    kv, mem = memory_project((core == tensor).astype(jnp.int32).reshape(1), memory[0], mem_come, w_mid, proj_bias)
    o_kept, o_sent, lse_self = self_fwd(core_at, kept, come, seg_cont[:, None], seg_cont[None, :])
    o_come = other(o_sent)
    resid_one, norm_two, q_cross = middle(core_at, moved, o_kept, o_come, w_mid, norm_gain, norm_bias, proj_bias)
    attn_cross, lse_cross = cross_fwd(q_cross, kv, frames, heads)
    (out, norm_three, hidden, dpre, g_two, dattn, sum_g, sum_dpre, sum_g_two, gain_three, shift_three) = feed(
        attn_cross, resid_one, grad_in, w_mid, w_ff, norm_gain, norm_bias, proj_bias, mlp_bias[None], out_bias[None])
    output = fix(out)
    gw_ff = feed_weights(norm_three, grad_in, dpre, hidden)
    dattn, gw_ff = lax.optimization_barrier((dattn, gw_ff))
    g_ff = spread_sum(gw_ff)
    dq, dk, dv = cross_bwd(q_cross, kv, frames, dattn, attn_cross, lse_cross, heads)
    g_one, do_kept, do_sent, sum_dq, sum_g_one, gain_two, shift_two = middle_back(core_at, dq, resid_one, g_two, w_mid, norm_gain)
    do_come = other(do_sent)
    gw_mid, sum_dv = middle_weights(core_at, g_one, o_kept, o_come, norm_two, dq, mem, dk, dv, g_two, attn_cross)
    do_kept, gw_mid = lax.optimization_barrier((do_kept, gw_mid))
    g_mid = spread_sum(gw_mid)
    d_kept, d_sent = self_bwd(core_at, kept, come, do_kept, do_come, o_kept, o_sent, lse_self,
                              seg_cont.reshape(-1, 1, BLK), seg_cont[:, None])
    d_come = other(d_sent)
    gw_qkv, sum_qkv = qkv_weights(core_at, norm_one, d_kept, d_come)
    g_qkv = spread_sum(gw_qkv)
    grad_low, gain_one, shift_one = qkv_back(core_at, d_kept, d_come, moved, g_one, w_qkv, norm_gain)
    grad_tokens = fix(grad_low).astype(F32)

    sum_qkv = sum_qkv.reshape(2, 3, part)
    gain_grads = jnp.concatenate([gain_one, gain_two, gain_three])
    shift_grads = jnp.concatenate([shift_one, shift_two, shift_three])
    proj_grads = jnp.concatenate([sum_qkv[:, 0].reshape(1, -1), sum_qkv[:, 2].reshape(1, -1), sum_g_one, sum_dq, sum_dv, sum_g_two])
    g_gain, g_shift, g_proj, g_units, g_out_bias = lax.psum((gain_grads, shift_grads, proj_grads, sum_dpre[0], sum_g[0]), ALL)
    cut = lambda i: g_mid[:, i * part:(i + 1) * part]
    quarter = units // 2
    pieces = [g_ff[:, i * quarter:(i + 1) * quarter] for i in range(4)]
    return (output, grad_tokens, g_qkv.reshape(rows_here, 3, part), cut(0).T, cut(1),
            g_mid[:, 2 * part:4 * part].reshape(rows_here, 2, part), cut(4).T,
            jnp.concatenate([pieces[0], pieces[2]], 1), jnp.concatenate([pieces[1], pieces[3]], 1).T,
            g_gain, g_shift, g_proj, g_units, g_out_bias)


def solution(mesh):
    grid = Mesh(mesh.devices.reshape(-1, 2, mesh.shape["tensor"]), ("chip", "core", "tensor"))
    rows = ("chip", "core", "tensor")
    dp = ("chip", "core")
    in_specs = (P(rows, None), P(dp, None, None), P(rows), P(rows), P(rows, None), P(dp, None, "tensor"), P("tensor", dp),
                P(dp, "tensor"), P(dp, None, "tensor"), P("tensor", dp), P(dp, "tensor"), P("tensor", dp),
                P(), P(), P(), P(), P())
    out_specs = (P(rows, None), P(rows, None), P(dp, None, "tensor"), P("tensor", dp), P(dp, "tensor"), P(dp, None, "tensor"),
                 P("tensor", dp), P(dp, "tensor"), P("tensor", dp), P(), P(), P(), P(), P())
    return jax.shard_map(on_device, mesh=grid, in_specs=in_specs, out_specs=out_specs, check_vma=False)
```

time: 956 us -> 786 us (0.82)
  local copies, waits for them, and re-layouts: 189 us -> 16.9 us
  matrix products: 165 us -> 0 us
  Pallas kernels: 221 us -> 360 us
  waiting for transfers between devices: 191 us -> 305 us
  other arithmetic: 72.5 us -> 8.63 us
  starting transfers between devices: 48.4 us -> 15.6 us
  blocking collectives: 39 us -> 57.4 us
    dot_general x21 -> x0, matrix products: 165 us -> none  [the longest x6 70.6 us: nn(): lax.dot_general(a, b, (((1,), (0,)), ((), ())), preferred_element_type=F32)]
    pallas_call x2 -> x11, Pallas kernels: 109 us -> 248 us  [the longest x1 84.8 us: self_bwd(): pl.pallas_call(self_bwd_kernel, grid=(part // LANES,), in_specs=[scalar()...]
    all_gather x3, waiting for transfers between devices: 57.3 us -> 124 us  [fetch(): full = lax.all_gather(shard, ALL, axis=0, tiled=True)]
    reduce_scatter x3, waiting for transfers between devices: 125 us -> 173 us  [spread_sum(): lax.psum_scatter(grad.reshape(-1, grad.shape[2]), ALL, scatter_dimension=...]
    concatenate x9 -> x1, local copies, waits for them, and re-layouts: 38.6 us -> 0.04 us  [on_device(): jnp.concatenate([sum_qkv[:, 0].reshape(1, -1), sum_qkv[:, 2].reshape(1, -...]
    unnamed x153 -> x44, local copies, waits for them, and re-layouts: 42.3 us -> 6.92 us
    slice x15 -> x5, local copies, waits for them, and re-layouts: 38.8 us -> 4.67 us  [the longest x1 1.41 us: on_device(): cut = lambda i: g_mid[:, i * part:(i + 1) * part]]
    ppermute x5, starting transfers between devices: 41.6 us -> 9.23 us  [on_device(): fix = lambda x: lax.ppermute(x, ('core', 'tensor'), swap)]
  transfers between devices with their start and end apart: 17 -> 17, of which waited for: 5 -> 8; matrix products, arithmetic and copies ran while one was open for 35% -> 2% of each run, Pallas kernels for 6% -> 24%
where the time goes in v2:
time: 786 us; the launch traced here: 778 us
  Pallas kernels  360 us (46%)
  waiting for transfers between devices  305 us (39%)
  blocking collectives  57.4 us (7%)
  local copies, waits for them, and re-layouts  16.9 us (2%)
  starting transfers between devices  15.6 us (2%)
  between operations  14.6 us (2%)
  other arithmetic  8.63 us (1%)
    reduce_scatter x3, waiting for transfers between devices, spread_sum(): lax.psum_scatter(grad.reshape(-1, grad.shape[2]), ALL, scatter_dimension=...  173 us
    all_gather x3, waiting for transfers between devices, fetch(): full = lax.all_gather(shard, ALL, axis=0, tiled=True)  124 us
    pallas_call x1, Pallas kernels, self_bwd(): pl.pallas_call(self_bwd_kernel, grid=(part // LANES,), in_specs=[scalar()...  84.8 us
    pallas_call x1, Pallas kernels, cross_bwd(): pl.pallas_call(functools.partial(cross_bwd_kernel, frames), grid=(npair,)...  84.4 us
    psum x1, blocking collectives, on_device(): lax.psum((gain_grads, shift_grads, proj_grads, sum_dpre[0], sum_g[0]), ALL)  57.4 us
    pallas_call x1, Pallas kernels, feed(): pl.pallas_call(feed_kernel, grid=(rows // ROWS,), in_specs=[by_rows(width...  44.5 us
    pallas_call x1, Pallas kernels, cross_fwd(): pl.pallas_call(functools.partial(cross_fwd_kernel, frames), grid=(npair,)...  27.3 us
    pallas_call x1, Pallas kernels, self_fwd(): pl.pallas_call(self_fwd_kernel, grid=(part // LANES,), in_specs=[scalar()...  26.2 us
  transfers between devices with their start and end apart: 17, of which 8 were waited for; matrix products, arithmetic and copies ran while one was open for 2% of the time, Pallas kernels for 24%

profile of v2, /device:TPU:0, one launch (start us, length us, event | category | flops | bytes accessed | tf_op | source)
XLA Modules:
  0.0 777.8 jit_solution(6778382719807186081)
XLA Ops:
  7.2 1.6 copy.35
  9.8 1.5 pad_maximum_fusion.2
  11.3 1.7 pad_maximum_fusion
  13.1 2.1 collective-permute-start
  16.5 57.8 %all-gather.4.cloned.1.call-done = bf16[1536,1152]{1,0:T(8,128)(2,1)} async-done(((bf16[48,1152]{1,0:T(8,128)(2,1)}), bf16[1536,1152]{1,0:T(8,128)(2,1)}) %all-gather.4.cloned.1.call-update) | async-done | bytes 3538960 | tf_op jit(solution)/shard_map/all_gather | solution.py:639
  74.3 9.1 %qkv_project.1 = (bf16[1024,768]{1,0:T(8,128)(2,1)}, bf16[3,1024,384]{2,1,0:T(8,128)(2,1)}, bf16[3,1024,384]{2,1,0:T(8,128)(2,1)}) custom-call(s32[1]{0:T(128)} %bitcast.core_ref, bf16[1024,768]{1,0:T(8,128)(2,1)} %copy-done, bf16[2,768,1152]{2,1,0:T(8,128)(2,1)} %bitcast.63, f32[3,768]{1,0:T(4,128)} %gain_ref.9, f32[3,768]{1,0:T(4,128)} %shift_ref.5, ...), custom_call_target="tpu_custom_call" | custom-call | flops 3623878656 | bytes 12976128 | tf_op jit(solution)/shard_map/qkv_project/pallas_call | solution.py:364
  84.4 4.9 collective-permute-start.3
  92.5 26.2 %self_fwd.1 = (bf16[1024,384]{1,0:T(8,128)(2,1)}, bf16[1024,384]{1,0:T(8,128)(2,1)}, f32[2048,384]{1,0:T(8,128)}) custom-call(s32[1]{0:T(128)} %bitcast.core_ref, bf16[3,1024,384]{2,1,0:T(8,128)(2,1)} %get-tuple-element.61.kept_ref, bf16[3,1024,384]{2,1,0:T(8,128)(2,1)} %copy-done.15, s32[1024,1]{1,0:T(8,128)} %copy.31.segq_ref.segk_ref, s32[1,1024]{1,0:T(1,128)} %bitcast.55), custom_call_target="tpu_custom_call" | custom-call | flops 14495514624 | bytes 9437184 | tf_op jit(solution)/shard_map/self_fwd/pallas_call | solution.py:86
  119.0 2.2 collective-permute-start.6
  121.9 28.3 %all-gather.6.cloned.1.call-done = bf16[1536,1920]{1,0:T(8,128)(2,1)} async-done(((bf16[48,1920]{1,0:T(8,128)(2,1)}), bf16[1536,1920]{1,0:T(8,128)(2,1)}) %all-gather.6.cloned.1.call-update) | async-done | bytes 5898256 | tf_op jit(solution)/shard_map/all_gather | solution.py:639
  150.1 9.3 %middle.1 = (f32[1024,768]{1,0:T(8,128)}, bf16[1024,768]{1,0:T(8,128)(2,1)}, bf16[1024,768]{1,0:T(8,128)(2,1)}) custom-call(s32[1]{0:T(128)} %bitcast.core_ref, bf16[1024,768]{1,0:T(8,128)(2,1)} %copy-done, bf16[1024,384]{1,0:T(8,128)(2,1)} %get-tuple-element.63.own_ref.o_ref, bf16[1024,384]{1,0:T(8,128)(2,1)} %copy-done.1, bf16[2,768,1920]{2,1,0:T(8,128)(2,1)} %bitcast.36, ...), custom_call_target="tpu_custom_call" | custom-call | flops 2415919104 | bytes 11796480 | tf_op jit(solution)/shard_map/middle/pallas_call | solution.py:419
  159.5 9.3 %memory_project.1 = (bf16[1536,1536]{1,0:T(8,128)(2,1)}, bf16[1536,768]{1,0:T(8,128)(2,1)}) custom-call(s32[1]{0:T(128)} %bitcast.9.mine_ref, bf16[1500,768]{1,0:T(8,128)(2,1)} %bitcast.66, bf16[1500,768]{1,0:T(8,128)(2,1)} %collective-permute-done.5.come_ref, bf16[2,768,1920]{2,1,0:T(8,128)(2,1)} %bitcast.38, f32[6,768]{1,0:T(8,128)} %bias_ref.5), custom_call_target="tpu_custom_call" | custom-call | flops 3538944000 | bytes 13879296 | tf_op jit(solution)/shard_map/memory_project/pallas_call | solution.py:390
  168.8 27.3 %cross_fwd.1 = (bf16[1024,768]{1,0:T(8,128)(2,1)}, f32[1024,768]{1,0:T(8,128)}) custom-call(bf16[1024,768]{1,0:T(8,128)(2,1)} %get-tuple-element.65.q_ref, bf16[1536,1536]{1,0:T(8,128)(2,1)} %get-tuple-element.66.k_ref.v_ref, bf16[1536,1536]{1,0:T(8,128)(2,1)} %get-tuple-element.66.k_ref.v_ref), custom_call_target="tpu_custom_call" | custom-call | flops 19327352832 | bytes 11010048 | tf_op jit(solution)/shard_map/cross_fwd/pallas_call | solution.py:129
  196.1 38.3 %all-gather.8.cloned.1.call-done = bf16[1536,3072]{1,0:T(8,128)(2,1)} async-done(((bf16[48,3072]{1,0:T(8,128)(2,1)}), bf16[1536,3072]{1,0:T(8,128)(2,1)}) %all-gather.8.cloned.1.call-update) | async-done | bytes 9437200 | tf_op jit(solution)/shard_map/all_gather | solution.py:639
  234.5 44.5 %feed.1 = (bf16[1024,768]{1,0:T(8,128)(2,1)}, bf16[1024,768]{1,0:T(8,128)(2,1)}, bf16[1024,3072]{1,0:T(8,128)(2,1)}, bf16[1024,3072]{1,0:T(8,128)(2,1)}, f32[102...) custom-call(bf16[1024,768]{1,0:T(8,128)(2,1)} %get-tuple-element.67., ...), custom_call_target="tpu_custom_call" | custom-call | flops 21743271936 | bytes 35782656 | tf_op jit(solution)/shard_map/feed/pallas_call | solution.py:488
  279.0 15.1 %feed_weights.1 = bf16[2,768,3072]{2,1,0:T(8,128)(2,1)} custom-call(bf16[1024,768]{1,0:T(8,128)(2,1)} %get-tuple-element.71.norm_ref, bf16[1024,768]{1,0:T(8,128)(2,1)} %copy-done.17, bf16[1024,3072]{1,0:T(8,128)(2,1)} %get-tuple-element.72.dpre_ref, bf16[1024,3072]{1,0:T(8,128)(2,1)} %get-tuple-element.73.hidden_ref), custom_call_target="tpu_custom_call" | custom-call | flops 9663676416 | bytes 22020096 | tf_op jit(solution)/shard_map/feed_weights/pallas_call | solution.py:511
  294.1 84.4 %cross_bwd.1 = (bf16[1024,768]{1,0:T(8,128)(2,1)}, bf16[1536,768]{1,0:T(8,128)(2,1)}, bf16[1536,768]{1,0:T(8,128)(2,1)}) custom-call(bf16[1024,768]{1,0:T(8,128)(2,1)} %get-tuple-element.65.q_ref, bf16[1536,1536]{1,0:T(8,128)(2,1)} %get-tuple-element.66.k_ref.v_ref, bf16[1536,1536]{1,0:T(8,128)(2,1)} %get-tuple-element.66.k_ref.v_ref, ...), custom_call_target="tpu_custom_call" | custom-call | flops 48318382080 | bytes 18874368 | tf_op jit(solution)/shard_map/cross_bwd/pallas_call | solution.py:285
  378.5 11.8 %middle_back.1 = (f32[1024,768]{1,0:T(8,128)}, bf16[1024,384]{1,0:T(8,128)(2,1)}, bf16[1024,384]{1,0:T(8,128)(2,1)}, f32[1,768]{1,0:T(1,128)}, f32[1,768]{1,0:T(...) custom-call(s32[1]{0:T(128)} %bitcast.core_ref, bf16[1024,768]{1,0:T(8,128)(2,1)} %get-tuple-element.76.dq_ref, ...), custom_call_target="tpu_custom_call" | custom-call | flops 2415919104 | bytes 16515072 | tf_op jit(solution)/shard_map/middle_back/pallas_call | solution.py:545
  390.3 17.7 %middle_weights.1 = (bf16[2,768,1920]{2,1,0:T(8,128)(2,1)}, f32[1,768]{1,0:T(1,128)}) custom-call(s32[1]{0:T(128)} %bitcast.core_ref, f32[1024,768]{1,0:T(8,128)} %get-tuple-element.79.g1_ref, bf16[1024,384]{1,0:T(8,128)(2,1)} %get-tuple-element.63.own_ref.o_ref, bf16[1024,384]{1,0:T(8,128)(2,1)} %copy-done.1, bf16[1024,768]{1,0:T(8,128)(2,1)} %get-tuple-element.80.norm_ref, ...), custom_call_target="tpu_custom_call" | custom-call | flops 7247757312 | bytes 28704768 | tf_op jit(solution)/shard_map/middle_weights/pallas_call | solution.py:573
  409.5 2.0 collective-permute-done.8.do_come_ref
  412.4 84.8 %self_bwd.1 = (bf16[3,1024,384]{2,1,0:T(8,128)(2,1)}, bf16[3,1024,384]{2,1,0:T(8,128)(2,1)}) custom-call(s32[1]{0:T(128)} %bitcast.core_ref, bf16[3,1024,384]{2,1,0:T(8,128)(2,1)} %get-tuple-element.61.kept_ref, bf16[3,1024,384]{2,1,0:T(8,128)(2,1)} %copy-done.15, bf16[1024,384]{1,0:T(8,128)(2,1)} %get-tuple-element.85.do_ref, bf16[1024,384]{1,0:T(8,128)(2,1)} %copy-done.19, ...), custom_call_target="tpu_custom_call" | custom-call | flops 36238786560 | bytes 15728640 | tf_op jit(solution)/shard_map/self_bwd/pallas_call | solution.py:240
  497.6 4.4 collective-permute-done.9.come_ref
  502.0 1.4 copy-done.16
  503.4 9.4 %qkv_weights.1 = (bf16[2,768,1152]{2,1,0:T(8,128)(2,1)}, f32[2,1,1152]{2,1,0:T(1,128)}) custom-call(s32[1]{0:T(128)} %bitcast.core_ref, bf16[1024,768]{1,0:T(8,128)(2,1)} %get-tuple-element.91.norm_ref, bf16[3,1024,384]{2,1,0:T(8,128)(2,1)} %get-tuple-element.88.own_ref, bf16[3,1024,384]{2,1,0:T(8,128)(2,1)} %copy-done.16), custom_call_target="tpu_custom_call" | custom-call | flops 3623878656 | bytes 9830400 | tf_op jit(solution)/shard_map/qkv_weights/pallas_call | solution.py:625
  513.5 2.2 collective-permute-start.7
  515.7 10.8 %qkv_back.1 = (bf16[1024,768]{1,0:T(8,128)(2,1)}, f32[1,768]{1,0:T(1,128)}, f32[1,768]{1,0:T(1,128)}) custom-call(s32[1]{0:T(128)} %bitcast.core_ref, bf16[3,1024,384]{2,1,0:T(8,128)(2,1)} %get-tuple-element.88.own_ref, bf16[3,1024,384]{2,1,0:T(8,128)(2,1)} %copy-done.16, bf16[1024,768]{1,0:T(8,128)(2,1)} %copy-done, f32[1024,768]{1,0:T(8,128)} %get-tuple-element.79.g1_ref, ...), custom_call_target="tpu_custom_call" | custom-call | flops 3623878656 | bytes 14548992 | tf_op jit(solution)/shard_map/qkv_back/pallas_call | solution.py:602
  526.6 2.1 collective-permute-start.10
  529.6 57.4 %all-reduce = (f32[3,768]{1,0:T(4,128)}, f32[3,768]{1,0:T(4,128)}, f32[6,768]{1,0:T(8,128)}, f32[3072]{0:T(1024)}, f32[768]{0:T(1024)}) all-reduce(f32[3,768]{1,0:T(4,128)S(1)} %get-tuple-element.135, f32[3,768]{1,0:T(4,128)S(1)} %get-tuple-element.136, ...), channel_id=1, replica_groups=mesh['chip'=8,'core'=2,'tensor'=2] {'tensor','chip','core'}, use_global_device_ids=true, to_apply=%region_3.4 | all-reduce | flops 13056 | bytes 104448 | tf_op jit(solution)/shard_map/psum | solution.py:702
  587.0 1.9 convert_element_type.11
  590.6 36.8 %reduce-scatter.4.cloned.1.call-done = bf16[48,1152]{1,0:T(8,128)(2,1)} async-done(((bf16[1536,1152]{1,0:T(8,128)(2,1)}), bf16[48,1152]{1,0:T(8,128)(2,1)}) %reduce-scatter.4.cloned.1.call-update) | async-done | bytes 110608 | tf_op jit(solution)/shard_map/reduce_scatter | solution.py:644
  629.0 1.4 slice.45
  632.0 135.7 %reduce-scatter.8.cloned.1.call-done = bf16[48,3072]{1,0:T(8,128)(2,1)} async-done(((bf16[1536,3072]{1,0:T(8,128)(2,1)}), bf16[48,3072]{1,0:T(8,128)(2,1)}) %reduce-scatter.8.cloned.1.call-update) | async-done | bytes 294928 | tf_op jit(solution)/shard_map/reduce_scatter | solution.py:644
  (89 shorter events, 19.7 us)
Async XLA Ops:
  7.2 67.2 %all-gather.4.cloned.1.call-start = ((), (), s32[]{:S(2)}) async-start(), calls=%async_computation.3 | async-start | bytes 3649536 | tf_op jit(solution)/shard_map/all_gather | solution.py:639
  8.8 141.3 %all-gather.6.cloned.1.call-start = ((), (), s32[]{:S(2)}) async-start(), calls=%async_computation.4 | async-start | bytes 6082560 | tf_op jit(solution)/shard_map/all_gather | solution.py:639
  11.3 223.2 %all-gather.8.cloned.1.call-start = ((), (), s32[]{:S(2)}) async-start(), calls=%async_computation.5 | async-start | bytes 9732096 | tf_op jit(solution)/shard_map/all_gather | solution.py:639
  13.1 575.9 %reduce-scatter.6.cloned.1.call-start = ((), (), s32[]{:S(2)}) async-start(), calls=%async_computation.7 | async-start | bytes 6082560 | tf_op jit(solution)/shard_map/reduce_scatter | solution.py:644
  13.1 3.4 collective-permute-start
  16.5 57.8 %copy-start = (bf16[1024,768]{1,0:T(8,128)(2,1)}, bf16[1024,768]{1,0:T(8,128)(2,1)S(1)}, u32[]{:S(2)}) copy-start(bf16[1024,768]{1,0:T(8,128)(2,1)S(1)} %collective-permute-done.x_ref) | copy-start | bytes 4718596
  83.4 7.7 collective-permute-start.1
  83.7 0.7 collective-permute-start.2
  84.4 5.7 collective-permute-start.3
  89.3 70.2 %collective-permute-start.5 = (bf16[1500,768]{1,0:T(8,128)(2,1)}, bf16[1500,768]{1,0:T(8,128)(2,1)}, u32[]{:S(2)}, u32[]{:S(2)}) collective-permute-start(bf16[1500,768]{1,0:T(8,128)(2,1)} %bitcast.65), channel_id=1, source_target_pairs={{0,2},{2,0},{1,3},{3,1},{4,6},{6,4},{5,7},{7,5},{8,10},{10,8},{9,1... | collective-permute-start | bytes 6912008 | tf_op jit(solution)/shard_map/ppermute | solution.py:659
  92.5 28.8 %copy-start.5 = (f32[768]{0:T(1024)S(1)}, f32[768]{0:T(1024)}, u32[]{:S(2)}) copy-start(f32[768]{0:T(1024)} %param.32) | copy-start | bytes 9220
  118.7 3.2 collective-permute-start.4
  119.0 77.1 %collective-permute-start.6 = (bf16[1024,768]{1,0:T(8,128)(2,1)}, bf16[1024,768]{1,0:T(8,128)(2,1)S(1)}, u32[]{:S(2)}, u32[]{:S(2)}) collective-permute-start(bf16[1024,768]{1,0:T(8,128)(2,1)} %param.20), channel_id=1, source_target_pairs={{0,0},{1,2},{2,1},{3,3},{4,4},{5,6},{6,5},{7,7},{8,8},{9,10},{10,9... | collective-permute-start | bytes 4718600 | tf_op jit(solution)/shard_map/ppermute | solution.py:658
  121.9 28.3 %copy-start.1 = (bf16[1024,384]{1,0:T(8,128)(2,1)}, bf16[1024,384]{1,0:T(8,128)(2,1)S(1)}, u32[]{:S(2)}) copy-start(bf16[1024,384]{1,0:T(8,128)(2,1)S(1)} %collective-permute-done.4.come_ref) | copy-start | bytes 2359300
  196.1 38.3 %copy-start.17 = (bf16[1024,768]{1,0:T(8,128)(2,1)}, bf16[1024,768]{1,0:T(8,128)(2,1)S(1)}, u32[]{:S(2)}) copy-start(bf16[1024,768]{1,0:T(8,128)(2,1)S(1)} %collective-permute-done.6.g_ref) | copy-start | bytes 4718596
  408.1 219.3 %reduce-scatter.4.cloned.1.call-start = ((), (), s32[]{:S(2)}) async-start(), calls=%async_computation.6 | async-start | bytes 3649536 | tf_op jit(solution)/shard_map/reduce_scatter | solution.py:644
  409.2 2.3 collective-permute-start.8
  497.3 4.7 collective-permute-start.9
  512.8 255.0 %reduce-scatter.8.cloned.1.call-start = ((), (), s32[]{:S(2)}) async-start(), calls=%async_computation.8 | async-start | bytes 9732096 | tf_op jit(solution)/shard_map/reduce_scatter | solution.py:644
  513.4 15.2 %copy-start.6 = (f32[1,768]{1,0:T(1,128)S(1)}, f32[1,768]{1,0:T(1,128)}, u32[]{:S(2)}) copy-start(f32[1,768]{1,0:T(1,128)} %get-tuple-element.107) | copy-start | bytes 9220
  513.4 15.2 %copy-start.4 = (f32[2,1,1152]{2,1,0:T(1,128)S(1)}, f32[2,1,1152]{2,1,0:T(1,128)}, u32[]{:S(2)}) copy-start(f32[2,1,1152]{2,1,0:T(1,128)} %get-tuple-element.101) | copy-start | bytes 27652
  513.4 15.3 %copy-start.9 = (f32[1,768]{1,0:T(1,128)S(1)}, f32[1,768]{1,0:T(1,128)}, u32[]{:S(2)}) copy-start(f32[1,768]{1,0:T(1,128)} %get-tuple-element.105) | copy-start | bytes 9220
  513.4 15.3 %copy-start.12 = (f32[1,768]{1,0:T(1,128)S(1)}, f32[1,768]{1,0:T(1,128)}, u32[]{:S(2)}) copy-start(f32[1,768]{1,0:T(1,128)} %get-tuple-element.103) | copy-start | bytes 9220
  513.4 15.3 %copy-start.13 = (f32[1,768]{1,0:T(1,128)S(1)}, f32[1,768]{1,0:T(1,128)}, u32[]{:S(2)}) copy-start(f32[1,768]{1,0:T(1,128)} %get-tuple-element.102) | copy-start | bytes 9220
  513.4 15.3 %copy-start.14 = (f32[1,768]{1,0:T(1,128)S(1)}, f32[1,768]{1,0:T(1,128)}, u32[]{:S(2)}) copy-start(f32[1,768]{1,0:T(1,128)} %get-tuple-element.104) | copy-start | bytes 9220
  513.5 15.4 %copy-start.7 = (f32[1,768]{1,0:T(1,128)S(1)}, f32[1,768]{1,0:T(1,128)}, u32[]{:S(2)}) copy-start(f32[1,768]{1,0:T(1,128)} %get-tuple-element.97) | copy-start | bytes 9220
  513.5 15.3 %copy-start.8 = (f32[1,768]{1,0:T(1,128)S(1)}, f32[1,768]{1,0:T(1,128)}, u32[]{:S(2)}) copy-start(f32[1,768]{1,0:T(1,128)} %get-tuple-element.100) | copy-start | bytes 9220
  513.5 15.3 %copy-start.10 = (f32[1,768]{1,0:T(1,128)S(1)}, f32[1,768]{1,0:T(1,128)}, u32[]{:S(2)}) copy-start(f32[1,768]{1,0:T(1,128)} %get-tuple-element.96) | copy-start | bytes 9220
  513.5 15.3 %copy-start.11 = (f32[1,768]{1,0:T(1,128)S(1)}, f32[1,768]{1,0:T(1,128)}, u32[]{:S(2)}) copy-start(f32[1,768]{1,0:T(1,128)} %get-tuple-element.99) | copy-start | bytes 9220
  513.5 16.1 %copy-start.3 = (f32[1,3072]{1,0:T(1,128)S(1)}, f32[1,3072]{1,0:T(1,128)}, u32[]{:S(2)}) copy-start(f32[1,3072]{1,0:T(1,128)} %get-tuple-element.106) | copy-start | bytes 36868
  513.5 15.1 %collective-permute-start.7 = (bf16[1024,768]{1,0:T(8,128)(2,1)}, bf16[1024,768]{1,0:T(8,128)(2,1)S(1)}, u32[]{:S(2)}, u32[]{:S(2)}) collective-permute-start(bf16[1024,768]{1,0:T(8,128)(2,1)} %get-tuple-element.69), channel_id=1, source_target_pairs={{0,0},{1,2},{2,1},{3,3},{4,4},{5,6},{6,5},{7,7},{8,8},{9,10},{10,9... | collective-permute-start | bytes 4718600 | tf_op jit(solution)/shard_map/ppermute | solution.py:658
  526.6 60.5 %collective-permute-start.10 = (bf16[1024,768]{1,0:T(8,128)(2,1)}, bf16[1024,768]{1,0:T(8,128)(2,1)S(1)}, u32[]{:S(2)}, u32[]{:S(2)}) collective-permute-start(bf16[1024,768]{1,0:T(8,128)(2,1)} %get-tuple-element.90), channel_id=1, source_target_pairs={{0,0},{1,2},{2,1},{3,3},{4,4},{5,6},{6,5},{7,7},{8,8},{9,10},{10,9... | collective-permute-start | bytes 4718600 | tf_op jit(solution)/shard_map/ppermute | solution.py:658
  (6 other events, 15.3 us)
Sparse Core Ops, SparseCore 0:
  11.5 62.7 all-gather.3
  77.8 72.2 all-gather.5
  153.6 80.7 all-gather.7
  408.2 111.3 reduce-scatter.5
  524.9 102.4 reduce-scatter.3
  633.1 134.5 reduce-scatter.7

commit v3 on v2

--- a/solution.py
+++ b/solution.py
@@ -465,7 +465,9 @@
         dpre_ref[:, at] = dpre
         back = back + nt(dpre, wi_ref[t])
     out_ref[...] = out.astype(BF)
-    accumulate(sum_dpre_ref, jnp.concatenate(sums, 1))
+    sums = jnp.concatenate(sums, 1)
+    wide = sum_dpre_ref.shape[1]
+    accumulate(sum_dpre_ref, jnp.concatenate([sums[:, i * wide:(i + 1) * wide] for i in range(sum_dpre_ref.shape[0])], 0))
     g = g_low.astype(F32)
     accumulate(sum_g_ref, column_sum(g))
     accumulate(sum_gain_ref, column_sum(back * normed))
@@ -483,8 +485,8 @@
     part = width // 2
     units = w_ff.shape[2] // 2
     w_at = lambda cols, c: pl.BlockSpec((2, width, cols), lambda i: (0, 0, c), pipeline_mode=pl.Buffered(1))
-    line = lambda cols: (pl.BlockSpec((1, cols), lambda i: (0, 0)), shaped((1, cols), F32))
-    lines = [line(width), line(2 * units), line(width), line(width), line(width)]
+    line = lambda count: (pl.BlockSpec((count, width), lambda i: (0, 0)), shaped((count, width), F32))
+    lines = [line(1), line(2 * units // width), line(1), line(1), line(1)]
     return pl.pallas_call(
         feed_kernel, grid=(rows // ROWS,),
         in_specs=[by_rows(width), by_rows(width), by_rows(width), w_at(part, 4), w_at(units, 0), w_at(units, 1),
@@ -609,14 +611,15 @@
     )(core, own, come, x, g1, w, gain)
 
 
-def qkv_weights_kernel(core_ref, norm_ref, own_ref, come_ref, out_ref, sum_ref):
+def qkv_weights_kernel(core_ref, norm_ref, own_ref, come_ref, out_ref, sum_q_ref, sum_v_ref):
     part = own_ref.shape[2]
     mine = pl.program_id(0) == core_ref[0]
     norm = norm_ref[...]
     for j in range(3):
         grad = jnp.where(mine, own_ref[j], come_ref[j])
         out_ref[0, :, j * part:(j + 1) * part] = tn(norm, grad).astype(BF)
-        sum_ref[0, :, j * part:(j + 1) * part] = column_sum(grad.astype(F32))
+        if j != 1:
+            (sum_q_ref if j == 0 else sum_v_ref)[...] = column_sum(grad.astype(F32))
 
 
 def qkv_weights(core, norm, own, come):
@@ -625,13 +628,185 @@
     return pl.pallas_call(
         qkv_weights_kernel, grid=(2,),
         in_specs=[scalar(), whole(norm.shape), whole(own.shape), whole(come.shape)],
-        out_specs=[pl.BlockSpec((1, width, 3 * part), lambda t: (t, 0, 0)), pl.BlockSpec((1, 1, 3 * part), lambda t: (t, 0, 0))],
-        out_shape=[shaped((2, width, 3 * part), BF), shaped((2, 1, 3 * part), F32)],
+        out_specs=[pl.BlockSpec((1, width, 3 * part), lambda t: (t, 0, 0)), pl.BlockSpec((1, part), lambda t: (0, t)), pl.BlockSpec((1, part), lambda t: (0, t))],
+        out_shape=[shaped((2, width, 3 * part), BF), shaped((1, width), F32), shaped((1, width), F32)],
         compiler_params=pltpu.CompilerParams(vmem_limit_bytes=BIG),
         cost_estimate=cost(6 * rows * width * width, 2 * (3 * width * width + 4 * rows * width)), name="qkv_weights",
     )(core, norm, own, come)
 
 
+def bit_names(chips):
+    return ["t"] + ["k%d" % b for b in reversed(range((chips - 1).bit_length()))] + ["core"]
+
+
+def my_bit(name):
+    if name == "t":
+        return lax.axis_index("tensor")
+    if name == "core":
+        return lax.axis_index("core")
+    return lax.axis_index("chip") // 2 ** int(name[1:]) % 2
+
+
+def partner(name):
+    bit = my_bit(name)
+    if name == "t":
+        return {"tensor": 1 - bit}
+    if name == "core":
+        return {"core": 1 - bit}
+    return {"chip": lax.axis_index("chip") + 2 ** int(name[1:]) * (1 - 2 * bit)}
+
+
+def greet(names):
+    barrier = pltpu.get_barrier_semaphore()
+    for name in names:
+        pl.semaphore_signal(barrier, inc=1, device_id=partner(name), device_id_type=pl.DeviceIdType.MESH)
+    pl.semaphore_wait(barrier, len(names))
+
+
+def exchange_orders(names):
+    low = [n for n in reversed(names) if n[0] == "k"]
+    return [["core", "t"] + low, ["core"] + low + ["t"], ["core"] + low[1:] + ["t"] + low[:1]]
+
+
+def stream_cols(cols, count):
+    tiles = cols // LANES
+    cuts = [tiles * i // count * LANES for i in range(count + 1)]
+    return [slice(a, b) for a, b in zip(cuts, cuts[1:])]
+
+
+def gather_kernel(names, orders, own_ref, out_ref, local_sem, send_sem, recv_sem):
+    greet(names)
+    lanes = stream_cols(own_ref.shape[1], len(orders))
+    place = tuple(my_bit(n) for n in names)
+    local = pltpu.make_async_copy(own_ref, out_ref.at[place], local_sem)
+    local.start()
+    known = [[] for _ in orders]
+    sent = []
+    flying = [None] * len(orders)
+
+    def start(st, step):
+        name = orders[st][step]
+        at = tuple(slice(None) if n in known[st] else my_bit(n) for n in names)
+        dst = out_ref.at[at + (slice(None), lanes[st])]
+        src = dst if step else own_ref.at[:, lanes[st]]
+        copy = pltpu.make_async_remote_copy(src, dst, send_sem.at[st, step], recv_sem.at[st, step],
+                                            device_id=partner(name), device_id_type=pl.DeviceIdType.MESH)
+        copy.start()
+        known[st].append(name)
+        sent.append(copy)
+        flying[st] = copy
+
+    for st in range(len(orders)):
+        start(st, 0)
+    local.wait()
+    for step in range(len(names)):
+        for st in range(len(orders)):
+            flying[st].wait_recv()
+            if step + 1 < len(names):
+                start(st, step + 1)
+    for copy in sent:
+        copy.wait_send()
+
+
+def gather_all(shard, chips):
+    names = bit_names(chips)
+    orders = [list(reversed(o)) for o in exchange_orders(names)]
+    rows, cols = shard.shape
+    dma = pltpu.SemaphoreType.DMA
+    full = pl.pallas_call(
+        functools.partial(gather_kernel, names, orders),
+        in_specs=[pl.BlockSpec(memory_space=pl.ANY)], out_specs=pl.BlockSpec(memory_space=pl.ANY),
+        out_shape=shaped((2,) * len(names) + (rows, cols), shard.dtype),
+        scratch_shapes=[dma, dma((len(orders), len(names))), dma((len(orders), len(names)))],
+        compiler_params=pltpu.CompilerParams(collective_id=0, has_side_effects=True, vmem_limit_bytes=BIG),
+        cost_estimate=cost(0, 100e6), name="gather_all",
+    )(shard)
+    return full.reshape(2, -1, cols)
+
+
+def sum_kernel(names, orders, parts, grad_ref, *refs):
+    small_refs, (out_ref, small_out_ref), scratch = refs[:parts], refs[parts:parts + 2], refs[parts + 2:]
+    greet(names)
+    count, steps = len(orders), len(names)
+    recv = [scratch[st * steps:(st + 1) * steps] for st in range(count)]
+    held = [scratch[(count + st) * steps:(count + st + 1) * steps] for st in range(count)]
+    small_recv, small_held, send_sem, recv_sem = scratch[2 * count * steps:]
+    lanes = stream_cols(grad_ref.shape[-1], count)
+    left = [list(names) for _ in orders]
+    here = [grad_ref.at[(slice(None),) * (steps + 1) + (lanes[st],)] for st in range(count)]
+    sent = []
+    flying = [None] * (count + 1)
+
+    def start(st, step):
+        name = orders[st][step] if st < count else orders[0][step]
+        if st < count:
+            src = here[st].at[tuple(1 - my_bit(n) if n == name else slice(None) for n in left[st])]
+            dst = recv[st][step]
+        else:
+            src = small_held.at[step]
+            dst = small_recv.at[step]
+        copy = pltpu.make_async_remote_copy(src, dst, send_sem.at[st, step], recv_sem.at[st, step],
+                                            device_id=partner(name), device_id_type=pl.DeviceIdType.MESH)
+        copy.start()
+        sent.append(copy)
+        flying[st] = copy
+
+    for st in range(count):
+        start(st, 0)
+    row = 0
+    for ref in small_refs:
+        small_held[0, row:row + ref.shape[0]] = ref[...]
+        row += ref.shape[0]
+    small_held[0, row:] = jnp.zeros((small_held.shape[1] - row, small_held.shape[2]), F32)
+    start(count, 0)
+    for step in range(steps):
+        for st in range(count):
+            name = orders[st][step]
+            flying[st].wait_recv()
+            at = tuple(my_bit(n) if n == name else slice(None) for n in left[st])
+            kept = here[st].at[at]
+            total = kept[...].astype(F32) + recv[st][step][...].astype(F32)
+            if step + 1 < steps:
+                held[st][step][...] = total.astype(BF)
+                here[st] = held[st][step]
+                left[st].remove(name)
+                start(st, step + 1)
+            else:
+                out_ref[:, lanes[st]] = total
+        flying[count].wait_recv()
+        total = small_held[step] + small_recv[step]
+        if step + 1 < steps:
+            small_held[step + 1] = total
+            start(count, step + 1)
+        else:
+            small_out_ref[...] = total
+    for copy in sent:
+        copy.wait_send()
+
+
+def sum_all(grad, small, chips):
+    names = bit_names(chips)
+    orders = exchange_orders(names)
+    cols = grad.shape[2]
+    rows = grad.shape[1] // (2 * chips)
+    steps = len(names)
+    bufs = [pltpu.VMEM((2,) * (steps - 1 - step) + (rows, lane.stop - lane.start), BF)
+            for lane in stream_cols(cols, len(orders)) for step in range(steps)]
+    small_rows = (sum(s.shape[0] for s in small) + 7) // 8 * 8
+    small_shape = (small_rows, small[0].shape[1])
+    dma = pltpu.SemaphoreType.DMA
+    vmem = pl.BlockSpec(memory_space=pltpu.VMEM)
+    return pl.pallas_call(
+        functools.partial(sum_kernel, names, orders, len(small)),
+        in_specs=[vmem] * (1 + len(small)), out_specs=[vmem, vmem],
+        out_shape=[shaped((rows, cols), F32), shaped(small_shape, F32)],
+        scratch_shapes=bufs + bufs + [pltpu.VMEM((steps,) + small_shape, F32), pltpu.VMEM((steps,) + small_shape, F32),
+                                      dma((len(orders) + 1, steps)), dma((len(orders) + 1, steps))],
+        compiler_params=pltpu.CompilerParams(collective_id=1, has_side_effects=True, vmem_limit_bytes=BIG),
+        cost_estimate=cost(0, 100e6), name="sum_all",
+    )(grad.reshape((2,) * steps + (rows, cols)), *small)
+
+
 ALL = ("tensor", "chip", "core")
 
 
@@ -641,7 +816,7 @@
 
 
 def spread_sum(grad):
-    return lax.psum_scatter(grad.reshape(-1, grad.shape[2]), ALL, scatter_dimension=0, tiled=True).astype(F32)
+    return lax.psum_scatter(grad.reshape(-1, grad.shape[2]), ALL, scatter_dimension=0, tiled=True)
 
 
 def on_device(tokens, memory, seg_ids, positions, grad_output, attn_in, attn_out, cross_q, cross_kv,
@@ -658,10 +833,15 @@
     fix = lambda x: lax.ppermute(x, ("core", "tensor"), swap)
     other = lambda x: lax.ppermute(x, "core", [(0, 1), (1, 0)])
 
-    w_qkv = fetch(attn_in.reshape(rows_here, 3 * part))
+    chips = lax.axis_size("chip")
+    first, mid, last = lax.optimization_barrier((
+        attn_in.reshape(rows_here, 3 * part),
+        jnp.concatenate([attn_out.T, cross_q, cross_kv.reshape(rows_here, 2 * part), cross_out.T], 1),
+        jnp.concatenate([mlp_in, mlp_out.T], 1)))
     moved = fix(tokens)
-    w_mid = fetch(jnp.concatenate([attn_out.T, cross_q, cross_kv.reshape(rows_here, 2 * part), cross_out.T], 1))
-    w_ff = fetch(jnp.concatenate([mlp_in, mlp_out.T], 1))
+    w_mid = fetch(mid)
+    w_ff = fetch(last)
+    w_qkv = gather_all(first, chips)
     grad_in = fix(grad_output)
     seg_mine = fix(seg_ids)
     seg_cont = jnp.where(core == 1, seg_mine, other(seg_mine))
@@ -689,17 +869,19 @@
     g_mid = spread_sum(gw_mid)
     d_kept, d_sent = self_bwd(core_at, kept, come, do_kept, do_come, o_kept, o_sent, lse_self,
                               seg_cont.reshape(-1, 1, BLK), seg_cont[:, None])
+    d_kept, d_sent, g_ff, output = lax.optimization_barrier((d_kept, d_sent, g_ff, output))
     d_come = other(d_sent)
-    gw_qkv, sum_qkv = qkv_weights(core_at, norm_one, d_kept, d_come)
-    g_qkv = spread_sum(gw_qkv)
     grad_low, gain_one, shift_one = qkv_back(core_at, d_kept, d_come, moved, g_one, w_qkv, norm_gain)
+    grad_low, d_kept, d_come = lax.optimization_barrier((grad_low, d_kept, d_come))
     grad_tokens = fix(grad_low).astype(F32)
-
-    sum_qkv = sum_qkv.reshape(2, 3, part)
-    gain_grads = jnp.concatenate([gain_one, gain_two, gain_three])
-    shift_grads = jnp.concatenate([shift_one, shift_two, shift_three])
-    proj_grads = jnp.concatenate([sum_qkv[:, 0].reshape(1, -1), sum_qkv[:, 2].reshape(1, -1), sum_g_one, sum_dq, sum_dv, sum_g_two])
-    g_gain, g_shift, g_proj, g_units, g_out_bias = lax.psum((gain_grads, shift_grads, proj_grads, sum_dpre[0], sum_g[0]), ALL)
+    gw_qkv, sum_q, sum_v = qkv_weights(core_at, norm_one, d_kept, d_come)
+    g_qkv, sums = sum_all(gw_qkv, [gain_one, gain_two, gain_three, shift_one, shift_two, shift_three,
+                                   sum_q, sum_v, sum_g_one, sum_dq, sum_dv, sum_g_two, sum_dpre, sum_g], chips)
+    g_qkv, g_mid, g_ff = lax.optimization_barrier((g_qkv, g_mid, g_ff))
+    g_mid, g_ff = g_mid.astype(F32), g_ff.astype(F32)
+    g_gain, g_shift, g_proj = sums[:3], sums[3:6], sums[6:12]
+    unit_rows = sum_dpre.shape[0]
+    g_units, g_out_bias = sums[12:12 + unit_rows].reshape(-1), sums[12 + unit_rows]
     cut = lambda i: g_mid[:, i * part:(i + 1) * part]
     quarter = units // 2
     pieces = [g_ff[:, i * quarter:(i + 1) * quarter] for i in range(4)]

time: 786 us -> 545 us (0.69)
  waiting for transfers between devices: 305 us -> 26.3 us
  Pallas kernels: 360 us -> 449 us
  blocking collectives: 57.4 us -> 0 us
    reduce_scatter x3 -> x2, waiting for transfers between devices: 173 us -> 0.02 us  [spread_sum(): lax.psum_scatter(grad.reshape(-1, grad.shape[2]), ALL, scatter_dimension=...]
    all_gather x3 -> x2, waiting for transfers between devices: 124 us -> 19.6 us  [fetch(): full = lax.all_gather(shard, ALL, axis=0, tiled=True)]
    pallas_call x0 -> x2, Pallas kernels: none -> 89.2 us  [the longest x1 49.9 us: gather_all(): pl.pallas_call(functools.partial(gather_kernel, names, orders), in_specs=...]
    psum x1 -> x0, blocking collectives: 57.4 us -> none  [on_device(): lax.psum((gain_grads, shift_grads, proj_grads, sum_dpre[0], sum_g[0]), ALL)]
  transfers between devices with their start and end apart: 17 -> 15, of which waited for: 8 -> 4; matrix products, arithmetic and copies ran while one was open for 2% -> 4% of each run, Pallas kernels for 24% -> 73%
where the time goes in v3:
time: 545 us; the launch traced here: 536 us
  Pallas kernels  449 us (82%)
  waiting for transfers between devices  26.3 us (5%)
  local copies, waits for them, and re-layouts  22.9 us (4%)
  starting transfers between devices  16.1 us (3%)
  between operations  14.1 us (3%)
  other arithmetic  7.65 us (1%)
    pallas_call x1, Pallas kernels, self_bwd(): pl.pallas_call(self_bwd_kernel, grid=(part // LANES,), in_specs=[scalar()...  84.7 us
    pallas_call x1, Pallas kernels, cross_bwd(): pl.pallas_call(functools.partial(cross_bwd_kernel, frames), grid=(npair,)...  84.5 us
    pallas_call x1, Pallas kernels, gather_all(): pl.pallas_call(functools.partial(gather_kernel, names, orders), in_specs=...  49.9 us
    pallas_call x1, Pallas kernels, feed(): pl.pallas_call(feed_kernel, grid=(rows // ROWS,), in_specs=[by_rows(width...  44.6 us
    pallas_call x1, Pallas kernels, sum_all(): pl.pallas_call(functools.partial(sum_kernel, names, orders, len(small)),...  39.3 us
    pallas_call x1, Pallas kernels, cross_fwd(): pl.pallas_call(functools.partial(cross_fwd_kernel, frames), grid=(npair,)...  27.3 us
    pallas_call x1, Pallas kernels, self_fwd(): pl.pallas_call(self_fwd_kernel, grid=(part // LANES,), in_specs=[scalar()...  26.3 us
    all_gather x2, waiting for transfers between devices, fetch(): full = lax.all_gather(shard, ALL, axis=0, tiled=True)  19.6 us
  transfers between devices with their start and end apart: 15, of which 4 were waited for; matrix products, arithmetic and copies ran while one was open for 4% of the time, Pallas kernels for 73%

profile of v3, /device:TPU:0, one launch (start us, length us, event | category | flops | bytes accessed | tf_op | source)
XLA Modules:
  0.0 536.3 jit_solution(14270164596984692290)
XLA Ops:
  8.1 1.6 copy.37
  9.7 1.7 pad_maximum_fusion
  11.4 1.5 pad_maximum_fusion.2
  13.7 2.1 collective-permute-start
  17.1 49.9 %gather_all.1 = bf16[2,2,2,2,2,48,1152]{6,5,4,3,2,1,0:T(8,128)(2,1)} custom-call(bf16[48,1152]{1,0:T(8,128)(2,1)} %bitcast.44), custom_call_target="tpu_custom_call" | custom-call | bytes 100000000 | tf_op jit(solution)/shard_map/gather_all/pallas_call | solution.py:716
  68.2 9.3 %qkv_project.1 = (bf16[1024,768]{1,0:T(8,128)(2,1)}, bf16[3,1024,384]{2,1,0:T(8,128)(2,1)}, bf16[3,1024,384]{2,1,0:T(8,128)(2,1)}) custom-call(s32[1]{0:T(128)} %bitcast.core_ref, bf16[1024,768]{1,0:T(8,128)(2,1)} %copy-done, bf16[2,768,1152]{2,1,0:T(8,128)(2,1)} %bitcast.42, f32[3,768]{1,0:T(4,128)} %gain_ref.9, f32[3,768]{1,0:T(4,128)} %shift_ref.5, ...), custom_call_target="tpu_custom_call" | custom-call | flops 3623878656 | bytes 12976128 | tf_op jit(solution)/shard_map/qkv_project/pallas_call | solution.py:364
  78.6 4.8 collective-permute-start.3
  85.2 26.3 %self_fwd.1 = (bf16[1024,384]{1,0:T(8,128)(2,1)}, bf16[1024,384]{1,0:T(8,128)(2,1)}, f32[2048,384]{1,0:T(8,128)}) custom-call(s32[1]{0:T(128)} %bitcast.core_ref, bf16[3,1024,384]{2,1,0:T(8,128)(2,1)} %get-tuple-element.78.kept_ref, bf16[3,1024,384]{2,1,0:T(8,128)(2,1)} %collective-permute-done.1.come_ref, s32[1024,1]{1,0:T(8,128)} %copy.33.segq_ref.segk_ref, ...), custom_call_target="tpu_custom_call" | custom-call | flops 14495514624 | bytes 9437184 | tf_op jit(solution)/shard_map/self_fwd/pallas_call | solution.py:86
  111.8 2.0 collective-permute-start.6
  115.3 9.3 %middle.1 = (f32[1024,768]{1,0:T(8,128)}, bf16[1024,768]{1,0:T(8,128)(2,1)}, bf16[1024,768]{1,0:T(8,128)(2,1)}) custom-call(s32[1]{0:T(128)} %bitcast.core_ref, bf16[1024,768]{1,0:T(8,128)(2,1)} %copy-done, bf16[1024,384]{1,0:T(8,128)(2,1)} %get-tuple-element.80.own_ref.o_ref, bf16[1024,384]{1,0:T(8,128)(2,1)} %copy-done.2, bf16[2,768,1920]{2,1,0:T(8,128)(2,1)} %bitcast.33, ...), custom_call_target="tpu_custom_call" | custom-call | flops 2415919104 | bytes 11796480 | tf_op jit(solution)/shard_map/middle/pallas_call | solution.py:419
  124.6 9.2 %memory_project.1 = (bf16[1536,1536]{1,0:T(8,128)(2,1)}, bf16[1536,768]{1,0:T(8,128)(2,1)}) custom-call(s32[1]{0:T(128)} %bitcast.10.mine_ref, bf16[1500,768]{1,0:T(8,128)(2,1)} %bitcast.60, bf16[1500,768]{1,0:T(8,128)(2,1)} %collective-permute-done.5.come_ref, bf16[2,768,1920]{2,1,0:T(8,128)(2,1)} %bitcast.35, f32[6,768]{1,0:T(8,128)} %bias_ref.5), custom_call_target="tpu_custom_call" | custom-call | flops 3538944000 | bytes 13879296 | tf_op jit(solution)/shard_map/memory_project/pallas_call | solution.py:390
  133.8 27.3 %cross_fwd.1 = (bf16[1024,768]{1,0:T(8,128)(2,1)}, f32[1024,768]{1,0:T(8,128)}) custom-call(bf16[1024,768]{1,0:T(8,128)(2,1)} %get-tuple-element.83.q_ref, bf16[1536,1536]{1,0:T(8,128)(2,1)} %get-tuple-element.84.k_ref.v_ref, bf16[1536,1536]{1,0:T(8,128)(2,1)} %get-tuple-element.84.k_ref.v_ref), custom_call_target="tpu_custom_call" | custom-call | flops 19327352832 | bytes 11010048 | tf_op jit(solution)/shard_map/cross_fwd/pallas_call | solution.py:129
  161.1 19.6 %all-gather.5.cloned.1.call-done = bf16[1536,3072]{1,0:T(8,128)(2,1)} async-done(((bf16[48,3072]{1,0:T(8,128)(2,1)}), bf16[1536,3072]{1,0:T(8,128)(2,1)}) %all-gather.5.cloned.1.call-update) | async-done | bytes 9437200 | tf_op jit(solution)/shard_map/all_gather | solution.py:814
  180.8 44.6 %feed.1 = (bf16[1024,768]{1,0:T(8,128)(2,1)}, bf16[1024,768]{1,0:T(8,128)(2,1)}, bf16[1024,3072]{1,0:T(8,128)(2,1)}, bf16[1024,3072]{1,0:T(8,128)(2,1)}, f32[102...) custom-call(bf16[1024,768]{1,0:T(8,128)(2,1)} %get-tuple-element.85., ...), custom_call_target="tpu_custom_call" | custom-call | flops 21743271936 | bytes 35782656 | tf_op jit(solution)/shard_map/feed/pallas_call | solution.py:490
  225.4 15.1 %feed_weights.1 = bf16[2,768,3072]{2,1,0:T(8,128)(2,1)} custom-call(bf16[1024,768]{1,0:T(8,128)(2,1)} %get-tuple-element.89.norm_ref, bf16[1024,768]{1,0:T(8,128)(2,1)} %collective-permute-done.6.g_ref, bf16[1024,3072]{1,0:T(8,128)(2,1)} %get-tuple-element.90.dpre_ref, bf16[1024,3072]{1,0:T(8,128)(2,1)} %get-tuple-element.91.hidden_ref), custom_call_target="tpu_custom_call" | custom-call | flops 9663676416 | bytes 22020096 | tf_op jit(solution)/shard_map/feed_weights/pallas_call | solution.py:513
  240.6 84.5 %cross_bwd.1 = (bf16[1024,768]{1,0:T(8,128)(2,1)}, bf16[1536,768]{1,0:T(8,128)(2,1)}, bf16[1536,768]{1,0:T(8,128)(2,1)}) custom-call(bf16[1024,768]{1,0:T(8,128)(2,1)} %get-tuple-element.83.q_ref, bf16[1536,1536]{1,0:T(8,128)(2,1)} %get-tuple-element.84.k_ref.v_ref, bf16[1536,1536]{1,0:T(8,128)(2,1)} %get-tuple-element.84.k_ref.v_ref, ...), custom_call_target="tpu_custom_call" | custom-call | flops 48318382080 | bytes 18874368 | tf_op jit(solution)/shard_map/cross_bwd/pallas_call | solution.py:285
  325.1 11.9 %middle_back.1 = (f32[1024,768]{1,0:T(8,128)}, bf16[1024,384]{1,0:T(8,128)(2,1)}, bf16[1024,384]{1,0:T(8,128)(2,1)}, f32[1,768]{1,0:T(1,128)}, f32[1,768]{1,0:T(...) custom-call(s32[1]{0:T(128)} %bitcast.core_ref, bf16[1024,768]{1,0:T(8,128)(2,1)} %get-tuple-element.94.dq_ref, ...), custom_call_target="tpu_custom_call" | custom-call | flops 2415919104 | bytes 16515072 | tf_op jit(solution)/shard_map/middle_back/pallas_call | solution.py:547
  336.9 17.7 %middle_weights.1 = (bf16[2,768,1920]{2,1,0:T(8,128)(2,1)}, f32[1,768]{1,0:T(1,128)}) custom-call(s32[1]{0:T(128)} %bitcast.core_ref, f32[1024,768]{1,0:T(8,128)} %get-tuple-element.97.g1_ref, bf16[1024,384]{1,0:T(8,128)(2,1)} %get-tuple-element.80.own_ref.o_ref, bf16[1024,384]{1,0:T(8,128)(2,1)} %copy-done.2, bf16[1024,768]{1,0:T(8,128)(2,1)} %get-tuple-element.98.norm_ref, ...), custom_call_target="tpu_custom_call" | custom-call | flops 7247757312 | bytes 28704768 | tf_op jit(solution)/shard_map/middle_weights/pallas_call | solution.py:575
  357.4 84.7 %self_bwd.1 = (bf16[3,1024,384]{2,1,0:T(8,128)(2,1)}, bf16[3,1024,384]{2,1,0:T(8,128)(2,1)}) custom-call(s32[1]{0:T(128)} %bitcast.core_ref, bf16[3,1024,384]{2,1,0:T(8,128)(2,1)} %get-tuple-element.78.kept_ref, bf16[3,1024,384]{2,1,0:T(8,128)(2,1)} %collective-permute-done.1.come_ref, bf16[1024,384]{1,0:T(8,128)(2,1)} %get-tuple-element.103.do_ref, ...), custom_call_target="tpu_custom_call" | custom-call | flops 36238786560 | bytes 15728640 | tf_op jit(solution)/shard_map/self_bwd/pallas_call | solution.py:240
  442.1 2.4 collective-permute-start.9
  444.5 4.5 collective-permute-done.9.come_ref
  449.0 10.9 %qkv_back.1 = (bf16[1024,768]{1,0:T(8,128)(2,1)}, f32[1,768]{1,0:T(1,128)}, f32[1,768]{1,0:T(1,128)}) custom-call(s32[1]{0:T(128)} %bitcast.core_ref, bf16[3,1024,384]{2,1,0:T(8,128)(2,1)} %get-tuple-element.116.own_ref, bf16[3,1024,384]{2,1,0:T(8,128)(2,1)} %collective-permute-done.9.come_ref, bf16[1024,768]{1,0:T(8,128)(2,1)} %copy-done, ...), custom_call_target="tpu_custom_call" | custom-call | flops 3623878656 | bytes 14548992 | tf_op jit(solution)/shard_map/qkv_back/pallas_call | solution.py:604
  459.9 2.1 collective-permute-start.10
  462.0 9.3 %qkv_weights.1 = (bf16[2,768,1152]{2,1,0:T(8,128)(2,1)}, f32[1,768]{1,0:T(1,128)}, f32[1,768]{1,0:T(1,128)}) custom-call(s32[1]{0:T(128)} %bitcast.core_ref, bf16[1024,768]{1,0:T(8,128)(2,1)} %get-tuple-element.115.norm_ref, bf16[3,1024,384]{2,1,0:T(8,128)(2,1)} %get-tuple-element.116.own_ref, bf16[3,1024,384]{2,1,0:T(8,128)(2,1)} %collective-permute-done.9.come_ref), custom_call_target="tpu_custom_call" | custom-call | flops 3623878656 | bytes 9830400 | tf_op jit(solution)/shard_map/qkv_weights/pallas_call | solution.py:628
  471.3 39.3 %sum_all.1 = (f32[48,1152]{1,0:T(8,128)}, f32[24,768]{1,0:T(8,128)}) custom-call(bf16[2,2,2,2,2,48,1152]{6,5,4,3,2,1,0:T(8,128)(2,1)} %bitcast.41, f32[1,768]{1,0:T(1,128)} %get-tuple-element.119.refs_0_, f32[1,768]{1,0:T(1,128)} %get-tuple-element.120.refs_1_, f32[1,768]{1,0:T(1,128)} %get-tuple-element.121.refs_2_, f32[1,768]{1,0:T(1,128)} %get-tuple-element.122.refs_3_, ...), custom_call_target="tpu_custom_call" | custom-call | bytes 100000000 | tf_op jit(solution)/shard_map/sum_all/pallas_call | solution.py:799
  514.1 1.6 slice.58
  515.7 1.7 convert_element_type.11
  517.4 1.6 copy.40
  519.6 1.6 reshape.89
  522.6 1.4 fusion.1
  524.0 1.6 slice_bitcast_fusion
  526.5 1.9 convert_element_type.10
  (56 shorter events, 19.3 us)
Async XLA Ops:
  7.2 107.2 %all-gather.3.cloned.1.call-start = ((), (), s32[]{:S(2)}) async-start(), calls=%async_computation.2 | async-start | bytes 6082560 | tf_op jit(solution)/shard_map/all_gather | solution.py:814
  12.9 167.9 %all-gather.5.cloned.1.call-start = ((), (), s32[]{:S(2)}) async-start(), calls=%async_computation.3 | async-start | bytes 9732096 | tf_op jit(solution)/shard_map/all_gather | solution.py:814
  13.7 428.4 %reduce-scatter.3.cloned.1.call-start = ((), (), s32[]{:S(2)}) async-start(), calls=%async_computation.4 | async-start | bytes 9732096 | tf_op jit(solution)/shard_map/reduce_scatter | solution.py:819
  13.7 53.4 %collective-permute-start = (bf16[1024,768]{1,0:T(8,128)(2,1)}, bf16[1024,768]{1,0:T(8,128)(2,1)S(1)}, u32[]{:S(2)}, u32[]{:S(2)}) collective-permute-start(bf16[1024,768]{1,0:T(8,128)(2,1)} %param.17), channel_id=1, source_target_pairs={{0,0},{1,2},{2,1},{3,3},{4,4},{5,6},{6,5},{7,7},{8,8},{9,10},{10,9... | collective-permute-start | bytes 4718600 | tf_op jit(solution)/shard_map/ppermute | solution.py:833
  67.1 1.1 copy-start
  68.2 9.7 %copy-start.7 = (s32[1024]{0:T(1024)S(1)}, s32[1024]{0:T(1024)}, u32[]{:S(2)}) copy-start(s32[1024]{0:T(1024)} %param.19) | copy-start | bytes 12292
  77.5 7.7 %collective-permute-start.1 = (bf16[3,1024,384]{2,1,0:T(8,128)(2,1)}, bf16[3,1024,384]{2,1,0:T(8,128)(2,1)}, u32[]{:S(2)}, u32[]{:S(2)}) collective-permute-start(bf16[3,1024,384]{2,1,0:T(8,128)(2,1)} %get-tuple-element.79), channel_id=1, source_target_pairs={{0,2},{2,0},{1,3},{3,1},{4,6},{6,4},{5,7},{7,5},{8,10},{10,8},{9,1... | collective-permute-start | bytes 7077896 | tf_op jit(solution)/shard_map/ppermute | solution.py:834
  77.9 0.7 collective-permute-start.2
  78.6 5.6 %collective-permute-start.3 = (s32[1024]{0:T(1024)S(1)}, s32[1024]{0:T(1024)S(1)}, u32[]{:S(2)}, u32[]{:S(2)}) collective-permute-start(s32[1024]{0:T(1024)S(1)} %collective-permute-done.2), channel_id=1, source_target_pairs={{0,2},{2,0},{1,3},{3,1},{4,6},{6,4},{5,7},{7,5},{8,10},{10,8},{9,1... | collective-permute-start | bytes 12296 | tf_op jit(solution)/shard_map/ppermute | solution.py:834
  83.3 41.3 %collective-permute-start.5 = (bf16[1500,768]{1,0:T(8,128)(2,1)}, bf16[1500,768]{1,0:T(8,128)(2,1)}, u32[]{:S(2)}, u32[]{:S(2)}) collective-permute-start(bf16[1500,768]{1,0:T(8,128)(2,1)} %bitcast.59), channel_id=1, source_target_pairs={{0,2},{2,0},{1,3},{3,1},{4,6},{6,4},{5,7},{7,5},{8,10},{10,8},{9,1... | collective-permute-start | bytes 6912008 | tf_op jit(solution)/shard_map/ppermute | solution.py:834
  84.2 1.1 copy-start.3
  85.2 26.6 %copy-start.5 = (bf16[1024,768]{1,0:T(8,128)(2,1)S(1)}, bf16[1024,768]{1,0:T(8,128)(2,1)}, u32[]{:S(2)}) copy-start(bf16[1024,768]{1,0:T(8,128)(2,1)} %param.20) | copy-start | bytes 4718596
  85.2 28.6 %copy-start.4 = (f32[768]{0:T(1024)S(1)}, f32[768]{0:T(1024)}, u32[]{:S(2)}) copy-start(f32[768]{0:T(1024)} %param.32) | copy-start | bytes 9220
  111.5 2.9 collective-permute-start.4
  111.8 49.3 %collective-permute-start.6 = (bf16[1024,768]{1,0:T(8,128)(2,1)S(1)}, bf16[1024,768]{1,0:T(8,128)(2,1)}, u32[]{:S(2)}, u32[]{:S(2)}) collective-permute-start(bf16[1024,768]{1,0:T(8,128)(2,1)S(1)} %copy-done.5), channel_id=1, source_target_pairs={{0,0},{1,2},{2,1},{3,3},{4,4},{5,6},{6,5},{7,7},{8,8},{9,10},{10,9... | collective-permute-start | bytes 4718600 | tf_op jit(solution)/shard_map/ppermute | solution.py:833
  114.4 0.9 copy-start.2
  240.5 272.2 %reduce-scatter.5.cloned.1.call-start = ((), (), s32[]{:S(2)}) async-start(), calls=%async_computation.5 | async-start | bytes 6082560 | tf_op jit(solution)/shard_map/reduce_scatter | solution.py:819
  354.7 1.4 copy-start.6
  354.7 2.7 collective-permute-start.7
  356.1 86.0 %collective-permute-start.8 = (bf16[1024,768]{1,0:T(8,128)(2,1)S(1)}, bf16[1024,768]{1,0:T(8,128)(2,1)S(1)}, u32[]{:S(2)}, u32[]{:S(2)}) collective-permute-start(bf16[1024,768]{1,0:T(8,128)(2,1)S(1)} %copy-done.6), channel_id=1, source_target_pairs={{0,0},{1,2},{2,1},{3,3},{4,4},{5,6},{6,5},{7,7},{8,8},{9,10},{10,9... | collective-permute-start | bytes 4718600 | tf_op jit(solution)/shard_map/ppermute | solution.py:833
  442.1 6.9 %collective-permute-start.9 = (bf16[3,1024,384]{2,1,0:T(8,128)(2,1)}, bf16[3,1024,384]{2,1,0:T(8,128)(2,1)}, u32[]{:S(2)}, u32[]{:S(2)}) collective-permute-start(bf16[3,1024,384]{2,1,0:T(8,128)(2,1)} %get-tuple-element.112), channel_id=1, source_target_pairs={{0,2},{2,0},{1,3},{3,1},{4,6},{6,4},{5,7},{7,5},{8,10},{10,8},{9,1... | collective-permute-start | bytes 7077896 | tf_op jit(solution)/shard_map/ppermute | solution.py:834
  459.9 66.6 %collective-permute-start.10 = (bf16[1024,768]{1,0:T(8,128)(2,1)}, bf16[1024,768]{1,0:T(8,128)(2,1)S(1)}, u32[]{:S(2)}, u32[]{:S(2)}) collective-permute-start(bf16[1024,768]{1,0:T(8,128)(2,1)} %get-tuple-element.114), channel_id=1, source_target_pairs={{0,0},{1,2},{2,1},{3,3},{4,4},{5,6},{6,5},{7,7},{8,8},{9,10},{10,9... | collective-permute-start | bytes 4718600 | tf_op jit(solution)/shard_map/ppermute | solution.py:833
  471.3 54.3 %copy-start.1 = (bf16[48,3072]{1,0:T(8,128)(2,1)S(1)}, bf16[48,3072]{1,0:T(8,128)(2,1)}, u32[]{:S(2)}) copy-start(bf16[48,3072]{1,0:T(8,128)(2,1)} %reduce-scatter.3.cloned.1.call-done) | copy-start | bytes 884740
Sparse Core Ops, SparseCore 0:
  13.0 78.0 all-gather.2
  94.6 86.0 all-gather.4
  240.6 134.6 reduce-scatter.2
  381.8 112.4 reduce-scatter.4
